TPU v7x, 512 devices: a whole 4x4x16 slice. The times are simulated.
512 devices in a mesh: ctx: 64 (over x, z_lo, y), dp: 8 (over z_hi, core).
Axes of the slice: x: 4, y: 4, z: 16 (z_hi: 4, z_lo: 4; z = z_hi * 4 + z_lo), core: 2. Of those that a mesh axis runs over, the one named last changes fastest.
Arguments:
- layer_input: bfloat16 [16, 4096, 4096], P('dp', 'ctx'), may hold values from -1 to 1
- queries: bfloat16 [16, 4096, 1024], P('dp', 'ctx'), may hold values from -8 to 8
- key_states: bfloat16 [16, 4096, 128], P('dp', 'ctx'), may hold values from -8 to 8
- value_states: bfloat16 [16, 4096, 128], P('dp', 'ctx'), may hold values from -6 to 6
- attn_output: bfloat16 [16, 4096, 1024], P('dp', 'ctx'), may hold values from -6 to 6
- out_grad: bfloat16 [16, 4096, 1024], P('dp', 'ctx'), may hold values from -6 to 6
- doc_ids: int32 [16, 4096], P('dp'), may hold values from 0 to 15, never falling along the last dimension, each value on 1 to 1024 neighbouring positions
- positions: int32 [16, 4096], P('dp'), may hold values from 0 to 4095, as said below
Outputs:
- query_grad: bfloat16 [16, 4096, 1024], P('dp', 'ctx')
- kv_weight_grad: float32 [4096, 256], P('ctx')
Inputs may be any that keep to these rules, and one draw needn't show every extreme that they name: `positions`: stored row c * 64 + r of a sequence (c below 64, r below 64) holds a position from r * (64) to (r + 1) * 64 - 1; every position of a sequence is held by exactly one row.
All inputs are finite; a program needn't handle non-finite values.
Results may differ from a plain program's by a relative error of at most 0.005.
Values may be sent and summed in bfloat16 or wider, within the bound.
No kernel may reach another device: no remote copies, remote signals or barrier semaphores. Data moves between devices by JAX's collectives and lax.ppermute only.
A program may use at most 64 MiB of HBM per device.

v0:
```python
import math

import jax
import jax.numpy as jnp
from jax import lax
from jax.sharding import PartitionSpec as P

NEG_FILL = -1e30


def passed_along(x, axis, by):
    length = lax.axis_size(axis)
    return lax.ppermute(x, axis, [(i, (i + by) % length) for i in range(length)])


def heads_first(tensor, head_count):
    seq_count, row_count, width_all = tensor.shape
    head_size = width_all // head_count
    split_up = tensor.reshape(seq_count, row_count, head_count, head_size)
    return split_up.transpose(0, 2, 1, 3).reshape(seq_count, head_count * row_count, head_size)


def local(
    layer_input, queries, key_states, value_states, attn_output, out_grad, doc_ids, positions
):
    seq_count, row_count, model_width = layer_input.shape
    head_size = key_states.shape[2]
    head_count = queries.shape[2] // head_size
    ctx_count = lax.axis_size("ctx")
    ctx_index = lax.axis_index("ctx")
    score_scale = 1.0 / math.sqrt(head_size)
    query_n = heads_first(queries, head_count)
    grad_n = heads_first(out_grad, head_count)
    row_product = (out_grad.astype(jnp.float32) * attn_output.astype(jnp.float32)).reshape(
        seq_count, row_count, head_count, head_size
    )
    delta_n = (
        jnp.sum(row_product, axis=3).transpose(0, 2, 1).reshape(seq_count, head_count * row_count)
    )
    doc_full = jnp.take_along_axis(doc_ids, positions, axis=1)
    own_pos = lax.dynamic_slice_in_dim(positions, ctx_index * row_count, row_count, 1)
    own_doc = lax.dynamic_slice_in_dim(doc_full, ctx_index * row_count, row_count, 1)
    query_pos = jnp.tile(own_pos, (1, head_count))
    query_doc = jnp.tile(own_doc, (1, head_count))
    key_all, value_all = (
        lax.all_gather(key_states, "ctx", axis=1, tiled=True),
        lax.all_gather(value_states, "ctx", axis=1, tiled=True),
    )
    group_rows = 4 * row_count
    query_total = head_count * row_count

    def live_mask(key_doc, key_pos):
        return (key_doc[:, :, None] == query_doc[:, None, :]) & (
            key_pos[:, :, None] <= query_pos[:, None, :]
        )

    def scores_of(key_block):
        return (
            jnp.einsum("skd,snd->skn", key_block, query_n, preferred_element_type=jnp.float32)
            * score_scale
        )

    def stats_step(group_index, loop_state):
        run_max, run_sum = loop_state
        row_start = group_index * group_rows
        key_block = lax.dynamic_slice_in_dim(key_all, row_start, group_rows, 1)
        key_doc = lax.dynamic_slice_in_dim(doc_full, row_start, group_rows, 1)
        key_pos = lax.dynamic_slice_in_dim(positions, row_start, group_rows, 1)
        live_pairs = live_mask(key_doc, key_pos)
        scores = scores_of(key_block)
        block_max = jnp.max(jnp.where(live_pairs, scores, NEG_FILL), axis=1)
        new_max = jnp.maximum(run_max, block_max)
        exp_terms = jnp.where(live_pairs, jnp.exp(scores - new_max[:, None, :]), 0.0)
        run_sum = run_sum * jnp.exp(run_max - new_max) + jnp.sum(exp_terms, axis=1)
        return (new_max, run_sum)

    start_max = jnp.full((seq_count, query_total), NEG_FILL, jnp.float32)
    start_sum = jnp.zeros((seq_count, query_total), jnp.float32)
    run_max, run_sum = lax.fori_loop(0, ctx_count // 4, stats_step, (start_max, start_sum))
    log_total = run_max + jnp.log(run_sum)

    def block_terms(row_start, block_rows):
        key_block = lax.dynamic_slice_in_dim(key_all, row_start, block_rows, 1)
        value_block = lax.dynamic_slice_in_dim(value_all, row_start, block_rows, 1)
        key_doc = lax.dynamic_slice_in_dim(doc_full, row_start, block_rows, 1)
        key_pos = lax.dynamic_slice_in_dim(positions, row_start, block_rows, 1)
        live_pairs = live_mask(key_doc, key_pos)
        scores = scores_of(key_block)
        probs = jnp.where(live_pairs, jnp.exp(scores - log_total[:, None, :]), 0.0)
        probs_half = probs.astype(jnp.bfloat16)
        value_grad = jnp.einsum(
            "skn,snd->skd", probs_half, grad_n, preferred_element_type=jnp.float32
        )
        prob_grad = jnp.einsum(
            "skd,snd->skn", value_block, grad_n, preferred_element_type=jnp.float32
        )
        score_grad = (probs * (prob_grad - delta_n[:, None, :])).astype(jnp.bfloat16)
        query_part = jnp.einsum(
            "skn,skd->snd", score_grad, key_block, preferred_element_type=jnp.float32
        )
        key_grad = (
            jnp.einsum("skn,snd->skd", score_grad, query_n, preferred_element_type=jnp.float32)
            * score_scale
        )
        return (jnp.concatenate([key_grad, value_grad], axis=2), query_part)

    start_query = jnp.zeros((seq_count, query_total, head_size), jnp.float32)

    def pass_on(accumulated):
        return passed_along(accumulated, "ctx", 1)

    def one_block(accumulated, query_sum, step_index):
        block_index = (ctx_index - step_index - 1) % ctx_count
        partial_value, query_part = block_terms(block_index * row_count, row_count)
        return (accumulated + partial_value, query_sum + query_part)

    def four_steps(turn_index, loop_state):
        accumulated, query_sum = loop_state
        for inner_step in range(4):
            accumulated, query_sum = one_block(accumulated, query_sum, 4 * turn_index + inner_step)
            accumulated = pass_on(accumulated)
        return (accumulated, query_sum)

    start_accum = jnp.zeros((seq_count, row_count, 2 * head_size), jnp.float32)
    accumulated, query_sum = lax.fori_loop(
        0, ctx_count // 4 - 1, four_steps, (start_accum, start_query)
    )
    for inner_step in range(3):
        accumulated, query_sum = one_block(accumulated, query_sum, ctx_count - 4 + inner_step)
        accumulated = pass_on(accumulated)
    accumulated, query_sum = one_block(accumulated, query_sum, ctx_count - 1)
    query_grad = (query_sum * score_scale).reshape(seq_count, head_count, row_count, head_size)
    query_grad = (
        query_grad.transpose(0, 2, 1, 3)
        .reshape(seq_count, row_count, head_count * head_size)
        .astype(jnp.bfloat16)
    )
    kv_half = accumulated.astype(jnp.bfloat16)
    flat_input = layer_input.reshape(seq_count * row_count, model_width)
    flat_grad = kv_half.reshape(seq_count * row_count, 2 * head_size)
    row_share = lax.psum_scatter(
        lax.dot_general(
            flat_input, flat_grad, (((0,), (0,)), ((), ())), preferred_element_type=jnp.float32
        ),
        "ctx",
        scatter_dimension=0,
        tiled=True,
    )
    weight_grad = lax.psum(row_share, "dp")
    return (query_grad, weight_grad)


def solution(mesh):
    in_specs = (
        P("dp", "ctx", None),
        P("dp", "ctx", None),
        P("dp", "ctx", None),
        P("dp", "ctx", None),
        P("dp", "ctx", None),
        P("dp", "ctx", None),
        P("dp", None),
        P("dp", None),
    )
    out_specs = (P("dp", "ctx", None), P("ctx", None))
    return jax.shard_map(local, mesh=mesh, in_specs=in_specs, out_specs=out_specs, check_vma=False)
```

profile of v0, /device:TPU:1, one launch (start us, length us, event | category | flops | bytes accessed | tf_op | source)
XLA Modules:
  0.0 2075.9 jit_solution(13382836654781288007)
XLA Ops:
  11.6 69.1 %gather_fusion = s32[8192]{0:T(1024)S(1)} fusion(s32[2,4096]{1,0:T(2,128)S(1)} %copy-done.1, s32[8192]{0:T(1024)S(1)} %bitcast.181), kind=kCustom, calls=%fused_computation | custom fusion | bytes 131072 | tf_op jit(solution)/shard_map/jit(take_along_axis)/gather | solution.py:40
  81.1 244.9 %all-gather.3.cloned.1.call-done = bf16[2,4096,128]{2,1,0:T(8,128)(2,1)} async-done(((bf16[2,64,128]{2,1,0:T(8,128)(2,1)}), bf16[2,4096,128]{2,1,0:T(8,128)(2,1)}) %all-gather.3.cloned.1.call-update) | async-done | bytes 2097168 | tf_op jit(solution)/shard_map/all_gather | solution.py:46
  326.0 30.1 %while.36 = (s32[]{:T(128)}, f32[2,512]{1,0:T(2,128)S(1)}, f32[2,512]{1,0:T(2,128)S(1)}, s32[2,4096]{1,0:T(2,128)S(1)}, s32[2,4096]{1,0:T(2,128)S(1)}, /*index=5...) while((s32[]{:T(128)}, f32[2,512]{1,0:T(2,128)S(1)}, ...), condition=%wide.region_3.4_spmd.clone, body=%wide.region_0.3_spmd.clone.sunk | while | flops 70259720 | bytes 2602182 | solution.py:79
  364.2 316.7 %all-gather.5.cloned.1.call-done = bf16[2,4096,128]{2,1,0:T(8,128)(2,1)} async-done(((bf16[2,64,128]{2,1,0:T(8,128)(2,1)}), bf16[2,4096,128]{2,1,0:T(8,128)(2,1)}) %all-gather.5.cloned.1.call-update) | async-done | bytes 2097168 | tf_op jit(solution)/shard_map/all_gather | solution.py:47
  682.7 754.8 %while.37 = (s32[]{:T(128)}, f32[2,64,256]{2,1,0:T(8,128)S(1)}, f32[2,512,128]{2,1,0:T(8,128)S(1)}, s32[]{:T(128)}, s32[2,4096]{1,0:T(2,128)S(1)}, /*index=5*/s3...) while((s32[]{:T(128)}, f32[2,64,256]{2,1,0:T(8,128)S(1)}, ...), condition=%wide.wide.region_6.7_spmd.clone, body=%wide.wide.region_5.6_spmd.clone.sunk | while | flops 339148864 | bytes 17799364 | solution.py:125
  699.5 9.6 collective-permute-done.1
  711.2 9.7 collective-permute-done.2
  749.3 9.6 collective-permute-done.1
  761.0 9.6 collective-permute-done.2
  773.7 8.8 collective-permute-done.3
  800.3 10.5 collective-permute-done.1
  812.9 9.6 collective-permute-done.2
  825.5 8.7 collective-permute-done.3
  850.9 9.6 collective-permute-done.1
  862.6 9.6 collective-permute-done.2
  875.3 8.7 collective-permute-done.3
  900.6 9.6 collective-permute-done.1
  912.4 9.6 collective-permute-done.2
  925.0 9.0 collective-permute-done.3
  950.6 10.3 collective-permute-done.1
  963.0 9.6 collective-permute-done.2
  1001.0 9.6 collective-permute-done.1
  1012.7 9.6 collective-permute-done.2
  1050.7 9.6 collective-permute-done.1
  1062.4 9.6 collective-permute-done.2
  1075.1 9.3 collective-permute-done.3
  1100.9 9.7 collective-permute-done.1
  1112.8 9.6 collective-permute-done.2
  1150.8 9.6 collective-permute-done.1
  1162.5 9.6 collective-permute-done.2
  1175.2 8.7 collective-permute-done.3
  1200.5 9.6 collective-permute-done.1
  1212.2 9.6 collective-permute-done.2
  1224.9 9.8 collective-permute-done.3
  1251.3 10.3 collective-permute-done.1
  1263.7 10.9 collective-permute-done.2
  1303.0 9.6 collective-permute-done.1
  1314.7 9.6 collective-permute-done.2
  1327.4 8.7 collective-permute-done.3
  1352.7 9.6 collective-permute-done.1
  1364.4 9.6 collective-permute-done.2
  1402.4 10.5 collective-permute-done.1
  1415.1 10.6 collective-permute-done.2
  1428.7 8.7 collective-permute-done.3
  1452.4 9.6 collective-permute-done.5
  1464.2 9.6 collective-permute-done.6
  1485.4 438.7 %reduce-scatter.4.cloned.1.call-done = f32[64,256]{1,0:T(8,128)} async-done(((f32[4096,256]{1,0:T(8,128)}), f32[64,256]{1,0:T(8,128)}) %reduce-scatter.4.cloned.1.call-update) | async-done | bytes 65552
  1927.5 140.3 %all-reduce.2.cloned.1.call-done = f32[64,256]{0,1:T(8,128)} async-done(((f32[64,256]{0,1:T(8,128)}), f32[64,256]{0,1:T(8,128)}) %all-reduce.2.cloned.1.call-update) | async-done | bytes 65552 | tf_op jit(solution)/shard_map/psum | solution.py:149
  (758 shorter events, 453.5 us)
Async XLA Ops:
  7.2 318.8 %all-gather.3.cloned.1.call-start = ((), (), s32[]{:S(2)}) async-start(), calls=%async_computation.1 | async-start | bytes 2129920 | tf_op jit(solution)/shard_map/all_gather | solution.py:46
  7.9 672.9 %all-gather.5.cloned.1.call-start = ((), (), s32[]{:S(2)}) async-start(), calls=%async_computation.2 | async-start | bytes 2129920 | tf_op jit(solution)/shard_map/all_gather | solution.py:47
  8.7 1915.4 %reduce-scatter.4.cloned.1.call-start = ((), (), s32[]{:S(2)}) async-start(), calls=%async_computation.4 | async-start | bytes 4259840
  685.4 11.8 collective-permute-start
  697.3 11.8 collective-permute-start.1
  709.1 11.8 collective-permute-start.2
  735.3 11.8 collective-permute-start
  747.2 11.7 collective-permute-start.1
  758.9 11.7 collective-permute-start.2
  770.7 11.8 collective-permute-start.3
  785.1 13.0 collective-permute-start
  798.2 12.6 collective-permute-start.1
  836.9 11.8 collective-permute-start
  848.8 11.7 collective-permute-start.1
  860.5 11.7 collective-permute-start.2
  886.6 11.8 collective-permute-start
  898.5 11.7 collective-permute-start.1
  910.2 11.7 collective-permute-start.2
  922.0 12.0 collective-permute-start.3
  936.6 11.8 collective-permute-start
  948.5 12.4 collective-permute-start.1
  987.0 11.8 collective-permute-start
  998.9 11.7 collective-permute-start.1
  1022.4 11.7 collective-permute-start.3
  1036.7 11.8 collective-permute-start
  1048.6 11.7 collective-permute-start.1
  1060.3 11.7 collective-permute-start.2
  1072.1 12.3 collective-permute-start.3
  1087.0 11.8 collective-permute-start
  1098.8 11.9 collective-permute-start.1
  1110.7 11.7 collective-permute-start.2
  1136.8 11.8 collective-permute-start
  1148.7 11.7 collective-permute-start.1
  1160.4 11.7 collective-permute-start.2
  1186.5 11.8 collective-permute-start
  1221.9 12.8 collective-permute-start.3
  1237.3 11.8 collective-permute-start
  1249.2 12.4 collective-permute-start.1
  1261.6 13.0 collective-permute-start.2
  1289.0 11.8 collective-permute-start
  1324.4 11.7 collective-permute-start.3
  1338.7 11.8 collective-permute-start
  1350.6 11.7 collective-permute-start.1
  1388.4 11.8 collective-permute-start
  1400.3 12.6 collective-permute-start.1
  1413.0 12.8 collective-permute-start.2
  1438.4 11.9 collective-permute-start.4
  1482.1 585.6 %all-reduce.2.cloned.1.call-start = ((), (), s32[]{:S(2)}) async-start(), calls=%async_computation.3 | async-start | bytes 262144 | tf_op jit(solution)/shard_map/psum | solution.py:149
  (29 other events, 1919.0 us)
Sparse Core Ops, SparseCore 0:
  10.1 315.8 all-gather.2
  328.1 352.7 all-gather.4
  1482.3 441.7 reduce-scatter.3
  1927.1 140.6 all-reduce.1
where the time goes:
time: 2090 us; the launch traced here: 2080 us
  waiting for transfers between devices  1600 us (77%)
  matrix products  243 us (12%)
  starting transfers between devices  121 us (6%)
  local copies, waits for them, and re-layouts  86.8 us (4%)
    ppermute x63, waiting for transfers between devices, passed_along(): lax.ppermute(x, axis, [(i, (i + by) % length) for i in range(length)])  454 us
    unnamed x5, waiting for transfers between devices  440 us
    all_gather x1, waiting for transfers between devices, local(): lax.all_gather(value_states, 'ctx', axis=1, tiled=True)  317 us
    all_gather x1, waiting for transfers between devices, local(): lax.all_gather(key_states, 'ctx', axis=1, tiled=True)  245 us
    psum x1, waiting for transfers between devices, local(): weight_grad = lax.psum(row_share, 'dp')  140 us
    ppermute x63, starting transfers between devices, passed_along(): lax.ppermute(x, axis, [(i, (i + by) % length) for i in range(length)])  121 us
    dot_general x80, matrix products, scores_of(): jnp.einsum('skd,snd->skn', key_block, query_n, preferred_element_type=jnp...  84.8 us
    gather x2, local copies, waits for them, and re-layouts, local(): doc_full = jnp.take_along_axis(doc_ids, positions, axis=1)  69.1 us
  transfers between devices with their start and end apart: 67, of which 53 were waited for; matrix products, arithmetic and copies ran while one was open for 14% of the time, Pallas kernels for 0%

commit v1 on v0

v1 whole, which is shorter than its diff:
```python
import math

import jax
import jax.numpy as jnp
from jax import lax
from jax.experimental import pallas as pl
from jax.experimental.pallas import tpu as pltpu
from jax.sharding import Mesh
from jax.sharding import PartitionSpec as P

BF = jnp.bfloat16
F32 = jnp.float32
HEADS = 8
HD = 128
ROWS = 64
CTX = 64
PAIRS = 32
HALO = 16
SEND = 72
BACK = 56
QN = CTX * 2 * HEADS
KH = CTX * HALO
KN = KH + CTX * 2
NEG = -1e30
FAR = 1 << 20
SCALE = 1.0 / math.sqrt(HD)
LOG2E = math.log2(math.e)


def iota(shape, dim):
    return lax.broadcasted_iota(jnp.int32, shape, dim)


def one_hot(condition):
    return jnp.where(condition, 1.0, 0.0).astype(BF)


def dot(a, b):
    return lax.dot_general(a, b, (((1,), (0,)), ((), ())), preferred_element_type=F32)


def dot_t(a, b):
    return lax.dot_general(a, b, (((1,), (1,)), ((), ())), preferred_element_type=F32)


def pack_kernel(q_ref, g_ref, o_ref, k_ref, v_ref, out_ref, split):
    def heads_to_rows(ref, at):
        wide = ref[0].astype(F32)
        for h in range(HEADS):
            split[pl.ds(h, ROWS, stride=HEADS), :] = wide[:, h * HD : (h + 1) * HD]
        out_ref[:, at : at + 16, :] = split[...].reshape(PAIRS, 16, HD).astype(BF)

    heads_to_rows(q_ref, 0)
    heads_to_rows(g_ref, 16)
    product = g_ref[0].astype(F32) * o_ref[0].astype(F32)
    lane = iota((ROWS, HD), 1)
    delta = jnp.zeros((ROWS, HD), F32)
    for h in range(HEADS):
        total = jnp.sum(product[:, h * HD : (h + 1) * HD], axis=1, keepdims=True)
        delta = jnp.where(lane % HEADS == h, total, delta)
    high = delta.astype(BF).astype(F32)
    rest = delta - high
    middle = rest.astype(BF).astype(F32)
    low = rest - middle
    pieces = jnp.where(lane < 8, high, jnp.where(lane < 16, middle, low))
    pieces = jnp.where(lane < 24, -pieces, 0.0).astype(BF)
    keys, values = k_ref[0], v_ref[0]
    target, row = iota((PAIRS * HALO, ROWS), 0), iota((PAIRS * HALO, ROWS), 1)
    window = one_hot(row == 2 * (target // HALO) + target % HALO - HALO)
    out_ref[:, 32:48, :] = dot(window, keys).reshape(PAIRS, HALO, HD).astype(BF)
    out_ref[:, 48:64, :] = dot(window, values).reshape(PAIRS, HALO, HD).astype(BF)
    target, row = iota((PAIRS * 8, ROWS), 0), iota((PAIRS * 8, ROWS), 1)
    slot = target % 8
    here = row == 2 * (target // 8) + slot % 2
    own = dot(one_hot(here & (slot // 2 == 0)), keys)
    own = own + dot(one_hot(here & (slot // 2 == 1)), values)
    own = own + dot(one_hot(here & (slot // 2 == 2)), pieces)
    out_ref[:, 64:72, :] = own.reshape(PAIRS, 8, HD).astype(BF)


def attend_kernel(in_ref, kpos_ref, qpos_ref, qlow_ref, out_ref, keys, values, dkey, dvalue):
    extra = in_ref[:, 64:72, :].astype(F32).reshape(CTX * 8, HD).astype(BF)
    token, source = iota((CTX * 2, CTX * 8), 0), iota((CTX * 2, CTX * 8), 1)
    base = source == (token // 2) * 8 + token % 2

    def picked(offset):
        chosen = source == (token // 2) * 8 + token % 2 + offset
        return dot(one_hot(chosen), extra).astype(BF)

    keys[0:KH, :] = in_ref[:, 32:48, :].reshape(KH, HD)
    keys[KH:KN, :] = picked(0)
    values[0:KH, 0:HD] = in_ref[:, 48:64, :].reshape(KH, HD)
    values[KH:KN, 0:HD] = picked(2)
    values[:, HD : 2 * HD] = one_hot(iota((KN, HD), 1) < 24)
    delta = picked(4)
    kpos = jnp.broadcast_to(kpos_ref[...], (HD, KN)).T
    key_columns = keys[...].astype(F32).T.astype(BF)
    count = 256
    for c in range(QN // count):
        first = c * (count // 16)
        qc = in_ref[first : first + count // 16, 0:16, :].reshape(count, HD)
        gc = in_ref[first : first + count // 16, 16:32, :].reshape(count, HD)
        row, col = iota((count, HD), 0), iota((count, HD), 1)
        spread = dot(one_hot(col == c * (count // HEADS) + row // HEADS), delta)
        spread = jnp.where(col % HEADS == row % HEADS, spread, 0.0).astype(BF)
        scores = dot_t(keys[...], qc)
        at = slice(c * count, (c + 1) * count)
        qpos, qlow = qpos_ref[:, at], qlow_ref[:, at]
        kp = jnp.concatenate([kpos, kpos], axis=1)
        scores = jnp.where((kp <= qpos) & (kp >= qlow), scores, NEG)
        top = jnp.max(scores, axis=0, keepdims=True)
        probs = jnp.exp2((scores - top) * (SCALE * LOG2E))
        probs = probs * (1.0 / jnp.sum(probs, axis=0, keepdims=True))
        change = dot_t(values[...], jnp.concatenate([gc, spread], axis=1))
        sgrad = (probs * change).astype(BF)
        value_part = dot(probs.astype(BF), gc)
        key_part = dot(sgrad, qc)
        if c == 0:
            dvalue[...] = value_part
            dkey[...] = key_part
        else:
            dvalue[...] += value_part
            dkey[...] += key_part
        qgrad = (dot(key_columns, sgrad) * SCALE).T
        out_ref[first : first + count // 16, 0:16, :] = qgrad.reshape(count // 16, 16, HD).astype(BF)
    out_ref[:, 16:32, :] = (dkey[0:KH, :] * SCALE).reshape(CTX, HALO, HD).astype(BF)
    out_ref[:, 32:48, :] = dvalue[0:KH, :].reshape(CTX, HALO, HD).astype(BF)
    source, token = iota((CTX * 8, CTX * 2), 0), iota((CTX * 8, CTX * 2), 1)
    home = (token // 2) * 8 + token % 2
    own = dot(one_hot(source == home), (dkey[KH:KN, :] * SCALE).astype(BF))
    own = own + dot(one_hot(source == home + 2), dvalue[KH:KN, :].astype(BF))
    out_ref[:, 48:56, :] = own.reshape(CTX, 8, HD).astype(BF)


def collect_kernel(in_ref, q_ref, kv_ref, split):
    split[...] = in_ref[:, 0:16, :].astype(F32).reshape(PAIRS * 16, HD)
    for h in range(HEADS):
        q_ref[0, :, h * HD : (h + 1) * HD] = split[pl.ds(h, ROWS, stride=HEADS), :].astype(BF)
    row, source = iota((ROWS, PAIRS * HALO), 0), iota((ROWS, PAIRS * HALO), 1)
    window = one_hot(row == 2 * (source // HALO) + source % HALO - HALO)
    row, source = iota((ROWS, PAIRS * 8), 0), iota((ROWS, PAIRS * 8), 1)
    slot = source % 8
    here = row == 2 * (source // 8) + slot % 2
    extra = in_ref[:, 48:56, :].astype(F32).reshape(PAIRS * 8, HD).astype(BF)
    for part in range(2):
        halo = in_ref[:, 16 + 16 * part : 32 + 16 * part, :].reshape(PAIRS * HALO, HD)
        total = dot(window, halo) + dot(one_hot(here & (slot // 2 == part)), extra)
        kv_ref[0, :, part * HD : (part + 1) * HD] = total.astype(BF)


def whole(shape):
    return pl.BlockSpec(shape, lambda *_: (0,) * len(shape))


def local(
    layer_input, queries, key_states, value_states, attn_output, out_grad, doc_ids, positions
):
    ctx = ("x", "zl", "y")
    index = lax.axis_index(ctx)
    sequence, pair = index // PAIRS, index % PAIRS

    x_at = lax.axis_index("x")
    model = layer_input.shape[2]
    quarter = model // 4
    flat_input = layer_input.reshape(2 * ROWS, model)
    pieces = []
    for step in range(4):
        piece = lax.dynamic_slice_in_dim(flat_input, (x_at + step) % 4 * quarter, quarter, 1)
        if step:
            piece = lax.ppermute(piece, "x", [(i, (i + step) % 4) for i in range(4)])
        pieces.append(piece)

    row_spec = lambda width: pl.BlockSpec((1, ROWS, width), lambda s: (s, 0, 0))
    sent = pl.pallas_call(
        pack_kernel,
        out_shape=jax.ShapeDtypeStruct((CTX, SEND, HD), BF),
        grid=(2,),
        in_specs=[row_spec(1024), row_spec(1024), row_spec(1024), row_spec(HD), row_spec(HD)],
        out_specs=pl.BlockSpec((PAIRS, SEND, HD), lambda s: (s, 0, 0)),
        scratch_shapes=[pltpu.VMEM((ROWS * HEADS, HD), F32)],
        name="pack",
    )(queries, out_grad, attn_output, key_states, value_states)
    arrived = lax.all_to_all(sent, ctx, 0, 0, tiled=True)

    docs = lax.dynamic_index_in_dim(doc_ids, sequence, 0, keepdims=False)
    places = lax.dynamic_index_in_dim(positions, sequence, 0, keepdims=False).reshape(CTX, ROWS)
    places = jnp.pad(places, ((0, 0), (HALO, 0)), constant_values=FAR)
    places = lax.dynamic_slice_in_dim(places, 2 * pair, HALO + 2, 1)
    own = places[:, HALO:].reshape(CTX * 2)
    kpos = jnp.concatenate([places[:, :HALO].reshape(KH), own])[None, :]
    starts = jnp.sum(docs[None, :] < jnp.arange(16)[:, None], axis=1)
    low = jnp.max(jnp.where(starts[:, None] <= own[None, :], starts[:, None], 0), axis=0)
    qpos = jnp.repeat(own, HEADS)[None, :]
    qlow = jnp.repeat(low, HEADS)[None, :]

    back = pl.pallas_call(
        attend_kernel,
        out_shape=jax.ShapeDtypeStruct((CTX, BACK, HD), BF),
        grid=(1,),
        in_specs=[whole((CTX, SEND, HD)), whole((1, KN)), whole((1, QN)), whole((1, QN))],
        out_specs=whole((CTX, BACK, HD)),
        scratch_shapes=[
            pltpu.VMEM((KN, HD), BF),
            pltpu.VMEM((KN, 2 * HD), BF),
            pltpu.VMEM((KN, HD), F32),
            pltpu.VMEM((KN, HD), F32),
        ],
        compiler_params=pltpu.CompilerParams(vmem_limit_bytes=48 << 20),
        name="attend",
    )(arrived, kpos.astype(F32), qpos.astype(F32), qlow.astype(F32))
    home = lax.all_to_all(back, ctx, 0, 0, tiled=True)

    query_grad, kv_grad = pl.pallas_call(
        collect_kernel,
        out_shape=(
            jax.ShapeDtypeStruct((2, ROWS, HEADS * HD), BF),
            jax.ShapeDtypeStruct((2, ROWS, 2 * HD), BF),
        ),
        grid=(2,),
        in_specs=[pl.BlockSpec((PAIRS, BACK, HD), lambda s: (s, 0, 0))],
        out_specs=(row_spec(HEADS * HD), row_spec(2 * HD)),
        scratch_shapes=[pltpu.VMEM((PAIRS * 16, HD), F32)],
        name="collect",
    )(home)

    flat_grad = kv_grad.reshape(2 * ROWS, 2 * HD)
    grads = lax.all_to_all(
        jnp.broadcast_to(flat_grad[None], (4, 2 * ROWS, 2 * HD)), "x", 0, 0, tiled=True
    )
    part = jnp.zeros((quarter, 2 * HD), F32)
    for step in range(4):
        grad = lax.dynamic_index_in_dim(grads, (x_at - step) % 4, 0, keepdims=False)
        part = part + lax.dot_general(
            pieces[step], grad, (((0,), (0,)), ((), ())), preferred_element_type=F32
        )
    core = lax.axis_index("core")
    halves = part.reshape(16, 2, 32, 2 * HD)
    mine = lax.dynamic_index_in_dim(halves, core, 1, keepdims=False)
    other = lax.dynamic_index_in_dim(halves, 1 - core, 1, keepdims=False)
    mine = mine + lax.ppermute(other, "core", [(0, 1), (1, 0)])
    mine = jnp.sum(lax.all_to_all(mine, ("zl", "y"), 0, 0, tiled=True), axis=0)
    dp = lax.axis_size("zh") * 2
    shares = lax.all_to_all(
        jnp.broadcast_to(mine[None], (dp, 32, 2 * HD)), ("zh", "core"), 0, 0, tiled=True
    )
    weight_grad = jnp.sum(shares.reshape(dp // 2, 64, 2 * HD), axis=0)
    return (query_grad, weight_grad)


def solution(mesh):
    devices = mesh.devices.reshape(4, 4, 4, -1, 2)
    inner = Mesh(devices, ("x", "zl", "y", "zh", "core"))
    ctx, dp = ("x", "zl", "y"), ("zh", "core")
    rows = P(dp, ctx, None)
    whole_rows = P(dp, None)
    return jax.shard_map(
        local,
        mesh=inner,
        in_specs=(rows,) * 6 + (whole_rows,) * 2,
        out_specs=(rows, P(ctx, None)),
        check_vma=False,
    )
```

time: 2090 us -> 169 us (0.08)
  the two profiles are of different devices: /device:TPU:1 before, /device:TPU:34 now
where the time goes in v1:
time: 169 us
  waiting for transfers between devices  59.6 us (35%)
  blocking collectives  54.8 us (32%)
  starting transfers between devices  36.3 us (21%)
  Pallas kernels  11 us (7%)
  local copies, waits for them, and re-layouts  3.63 us (2%)
    all_to_all x1, blocking collectives, local(): lax.all_to_all(jnp.broadcast_to(mine[None], (dp, 32, 2 * HD)), ('zh', 'co...  34.2 us
    all_to_all x1, waiting for transfers between devices, local(): arrived = lax.all_to_all(sent, ctx, 0, 0, tiled=True)  27.6 us
    all_to_all x1, waiting for transfers between devices, local(): home = lax.all_to_all(back, ctx, 0, 0, tiled=True)  23.1 us
    all_to_all x1, blocking collectives, local(): mine = jnp.sum(lax.all_to_all(mine, ('zl', 'y'), 0, 0, tiled=True), axis=0)  20.7 us
    all_to_all x1, starting transfers between devices, local(): arrived = lax.all_to_all(sent, ctx, 0, 0, tiled=True)  11.8 us
    ppermute x3, starting transfers between devices, local(): piece = lax.ppermute(piece, 'x', [(i, (i + step) % 4) for i in range(4)])  9.82 us
    all_to_all x1, starting transfers between devices, local(): home = lax.all_to_all(back, ctx, 0, 0, tiled=True)  8.08 us
    ppermute x3, waiting for transfers between devices, local(): piece = lax.ppermute(piece, 'x', [(i, (i + step) % 4) for i in range(4)])  6.94 us
  transfers between devices with their start and end apart: 7, of which 5 were waited for; matrix products, arithmetic and copies ran while one was open for 1% of the time, Pallas kernels for 0%

profile of v1, /device:TPU:34, one launch (start us, length us, event | category | flops | bytes accessed | tf_op | source)
XLA Modules:
  0.0 168.6 jit_solution(15391880785665429895)
XLA Ops:
  0.6 2.7 %pack.1 = bf16[64,72,128]{2,1,0:T(8,128)(2,1)} custom-call(bf16[2,64,1024]{2,1,0:T(8,128)(2,1)} %q_ref.1, bf16[2,64,1024]{2,1,0:T(8,128)(2,1)} %g_ref.1, bf16[2,64,1024]{2,1,0:T(8,128)(2,1)} %o_ref.1, bf16[2,64,128]{2,1,0:T(8,128)(2,1)} %k_ref.1, bf16[2,64,128]{2,1,0:T(8,128)(2,1)} %v_ref.1), custom_call_target="tpu_custom_call" | custom-call | tf_op jit(solution)/shard_map/pack/pallas_call | solution.py:174
  3.3 0.0 copy-start.2
  3.3 0.0 copy-start.3
  3.3 11.8 %all-to-all-start = ((bf16[64,72,128]{2,1,0:T(8,128)(2,1)}), bf16[64,72,128]{2,1,0:T(8,128)(2,1)S(1)}, u32[]{:S(2)}, u32[]{:S(2)}) async-start(bf16[64,72,128]{2,1,0:T(8,128)(2,1)} %pack.1), calls=%async_computation | async-start | bytes 2359296 | tf_op jit(solution)/shard_map/all_to_all | solution.py:183
  15.2 0.0 copy-done.2
  15.2 0.0 copy-done.3
  15.2 0.1 dynamic-slice_reduce_fusion
  15.2 0.1 reshape.83
  15.3 0.1 pad_dynamic-slice_fusion.1
  15.4 0.1 reshape.84
  15.5 0.1 concatenate.15
  15.7 0.1 convert_reduce_fusion
  15.8 0.1 select_reduce_fusion
  15.9 0.1 broadcast_in_dim.36
  16.0 0.1 convert_element_type.21.qlow_ref
  16.1 0.1 broadcast_in_dim.20
  16.2 0.1 convert_element_type.18.qpos_ref
  16.3 0.1 pad_dynamic-slice_fusion
  16.4 0.1 concatenate.14
  16.5 27.6 %all-to-all-done.in_ref = bf16[64,72,128]{2,1,0:T(8,128)(2,1)S(1)} async-done(((bf16[64,72,128]{2,1,0:T(8,128)(2,1)}), bf16[64,72,128]{2,1,0:T(8,128)(2,1)S(1)}, u32[]{:S(2)}, u32[]{:S(2)}) %all-to-all-start) | async-done | bytes 1179680 | tf_op jit(solution)/shard_map/all_to_all | solution.py:183
  44.1 6.2 %attend.1 = bf16[64,56,128]{2,1,0:T(8,128)(2,1)} custom-call(bf16[64,72,128]{2,1,0:T(8,128)(2,1)S(1)} %all-to-all-done.in_ref, f32[1,1152]{1,0:T(1,128)S(1)} %add_convert_fusion.kpos_ref, f32[1,1024]{1,0:T(1,128)S(1)} %convert_element_type.18.qpos_ref, f32[1,1024]{1,0:T(1,128)S(1)} %convert_element_type.21.qlow_ref), custom_call_target="tpu_custom_call" | custom-call | tf_op jit(solution)/shard_map/attend/pallas_call | solution.py:196
  50.3 8.1 %all-to-all-start.1 = ((bf16[64,56,128]{2,1,0:T(8,128)(2,1)}), bf16[64,56,128]{2,1,0:T(8,128)(2,1)S(1)}, u32[]{:S(2)}, u32[]{:S(2)}) async-start(bf16[64,56,128]{2,1,0:T(8,128)(2,1)} %attend.1), calls=%async_computation.1 | async-start | bytes 1835008 | tf_op jit(solution)/shard_map/all_to_all | solution.py:211
  58.4 0.0 copy-start.1
  58.5 23.1 %all-to-all-done.1.in_ref = bf16[64,56,128]{2,1,0:T(8,128)(2,1)S(1)} async-done(((bf16[64,56,128]{2,1,0:T(8,128)(2,1)}), bf16[64,56,128]{2,1,0:T(8,128)(2,1)S(1)}, u32[]{:S(2)}, u32[]{:S(2)}) %all-to-all-start.1) | async-done | bytes 917536 | tf_op jit(solution)/shard_map/all_to_all | solution.py:211
  81.6 0.0 copy-start
  81.6 0.9 copy-done
  82.5 2.1 %collect.1 = (bf16[2,64,1024]{2,1,0:T(8,128)(2,1)}, bf16[2,64,256]{2,1,0:T(8,128)(2,1)}) custom-call(bf16[64,56,128]{2,1,0:T(8,128)(2,1)} %copy-done), custom_call_target="tpu_custom_call" | custom-call | tf_op jit(solution)/shard_map/collect/pallas_call | solution.py:213
  84.6 1.5 broadcast_in_dim.38
  86.1 4.7 %all-to-all-start.2 = ((bf16[4,128,256]{2,1,0:T(8,128)(2,1)}), bf16[4,128,256]{2,1,0:T(8,128)(2,1)S(1)}, u32[]{:S(2)}, u32[]{:S(2)}) async-start(bf16[4,128,256]{2,1,0:T(8,128)(2,1)} %broadcast_in_dim.38), calls=%async_computation.2 | async-start | bytes 524288 | tf_op jit(solution)/shard_map/all_to_all | solution.py:227
  90.8 0.0 copy-done.1
  90.8 0.1 constant_dynamic-slice_fusion.1
  90.9 3.4 %collective-permute-start = (bf16[128,1024]{1,0:T(8,128)(2,1)S(1)}, bf16[128,1024]{1,0:T(8,128)(2,1)S(1)}, u32[]{:S(2)}, u32[]{:S(2)}) collective-permute-start(bf16[128,1024]{1,0:T(8,128)(2,1)S(1)} %get-tuple-element.8), channel_id=1, source_target_pairs={{0,128},{128,256},{256,384},{384,0},{1,129},{129,257},{257,385},{3... | collective-permute-start | bytes 786440 | tf_op jit(solution)/shard_map/ppermute | solution.py:170
  94.3 2.5 %collective-permute-start.2 = (bf16[128,1024]{1,0:T(8,128)(2,1)S(1)}, bf16[128,1024]{1,0:T(8,128)(2,1)S(1)}, u32[]{:S(2)}, u32[]{:S(2)}) collective-permute-start(bf16[128,1024]{1,0:T(8,128)(2,1)S(1)} %get-tuple-element.7), channel_id=1, source_target_pairs={{0,384},{128,0},{256,128},{384,256},{1,385},{129,1},{257,129},{385... | collective-permute-start | bytes 786440 | tf_op jit(solution)/shard_map/ppermute | solution.py:170
  96.7 4.0 %collective-permute-start.1 = (bf16[128,1024]{1,0:T(8,128)(2,1)S(1)}, bf16[128,1024]{1,0:T(8,128)(2,1)S(1)}, u32[]{:S(2)}, u32[]{:S(2)}) collective-permute-start(bf16[128,1024]{1,0:T(8,128)(2,1)S(1)} %get-tuple-element.6), channel_id=1, source_target_pairs={{0,256},{128,384},{256,0},{384,128},{1,257},{129,385},{257,1},{385... | collective-permute-start | bytes 786440 | tf_op jit(solution)/shard_map/ppermute | solution.py:170
  100.8 0.0 all-to-all-done.2
  100.8 0.3 fusion.1
  101.1 0.0 collective-permute-done
  101.2 0.3 convolution_add_fusion.1
  101.5 3.2 %collective-permute-done.2 = bf16[128,1024]{1,0:T(8,128)(2,1)S(1)} collective-permute-done((bf16[128,1024]{1,0:T(8,128)(2,1)S(1)}, bf16[128,1024]{1,0:T(8,128)(2,1)S(1)}, u32[]{:S(2)}, u32[]{:S(2)}) %collective-permute-start.2) | collective-permute-done | bytes 262176 | tf_op jit(solution)/shard_map/ppermute | solution.py:170
  104.7 0.3 fusion.3
  105.0 3.8 %collective-permute-done.1 = bf16[128,1024]{1,0:T(8,128)(2,1)S(1)} collective-permute-done((bf16[128,1024]{1,0:T(8,128)(2,1)S(1)}, bf16[128,1024]{1,0:T(8,128)(2,1)S(1)}, u32[]{:S(2)}, u32[]{:S(2)}) %collective-permute-start.1) | collective-permute-done | bytes 262176 | tf_op jit(solution)/shard_map/ppermute | solution.py:170
  108.7 0.3 fusion
  109.1 1.9 %collective-permute-start.3 = (f32[16,32,256]{2,1,0:T(8,128)S(1)}, f32[16,32,256]{2,1,0:T(8,128)S(1)}, u32[]{:S(2)}, u32[]{:S(2)}) collective-permute-start(f32[16,32,256]{2,1,0:T(8,128)S(1)} %dynamic-slice_bitcast_fusion), channel_id=1, source_target_pairs={{0,1},{1,0},{2,3},{3,2},{4,5},{5,4},{6,7},{7,6},{8,9},{9,8},{10,11... | collective-permute-start | bytes 1572872 | tf_op jit(solution)/shard_map/ppermute | solution.py:240
  111.1 1.9 %collective-permute-done.3 = f32[16,32,256]{2,1,0:T(8,128)S(1)} collective-permute-done((f32[16,32,256]{2,1,0:T(8,128)S(1)}, f32[16,32,256]{2,1,0:T(8,128)S(1)}, u32[]{:S(2)}, u32[]{:S(2)}) %collective-permute-start.3) | collective-permute-done | bytes 524320 | tf_op jit(solution)/shard_map/ppermute | solution.py:240
  112.9 0.1 bitcast_add_fusion
  113.0 20.7 %all_to_all.25 = f32[16,32,256]{2,1,0:T(8,128)S(1)} all-to-all(f32[16,32,256]{2,1,0:T(8,128)S(1)} %bitcast_add_fusion), channel_id=1, replica_groups=mesh['x'=4,'zl'=4,'y'=4,'zh'=4,'core'=2] {'zl','y'}, dimensions={0} | all-to-all | bytes 1048576 | tf_op jit(solution)/shard_map/all_to_all | solution.py:241
  133.7 34.2 %all_to_all.26 = f32[8,32,256]{2,1,0:T(8,128)S(1)} all-to-all(f32[8,32,256]{2,1,0:T(8,128)S(1)} %broadcast_in_dim.39), channel_id=1, replica_groups=mesh['x'=4,'zl'=4,'y'=4,'zh'=4,'core'=2] {'zh','core'}, dimensions={0} | all-to-all | bytes 524288 | tf_op jit(solution)/shard_map/all_to_all | solution.py:243
  167.9 0.6 bitcast_reduce_fusion
  (6 shorter events, 0.1 us)
Async XLA Ops:
  3.3 11.8 %copy-start.2 = (s32[2,4096]{1,0:T(2,128)S(1)}, s32[2,4096]{1,0:T(2,128)}, u32[]{:S(2)}) copy-start(s32[2,4096]{1,0:T(2,128)} %param.15) | copy-start | bytes 98308
  3.3 11.8 %copy-start.3 = (s32[2,4096]{1,0:T(2,128)S(1)}, s32[2,4096]{1,0:T(2,128)}, u32[]{:S(2)}) copy-start(s32[2,4096]{1,0:T(2,128)} %param.14) | copy-start | bytes 98308
  3.3 40.8 %all-to-all-start = ((bf16[64,72,128]{2,1,0:T(8,128)(2,1)}), bf16[64,72,128]{2,1,0:T(8,128)(2,1)S(1)}, u32[]{:S(2)}, u32[]{:S(2)}) async-start(bf16[64,72,128]{2,1,0:T(8,128)(2,1)} %pack.1), calls=%async_computation | async-start | bytes 2359296 | tf_op jit(solution)/shard_map/all_to_all | solution.py:183
  50.3 31.3 %all-to-all-start.1 = ((bf16[64,56,128]{2,1,0:T(8,128)(2,1)}), bf16[64,56,128]{2,1,0:T(8,128)(2,1)S(1)}, u32[]{:S(2)}, u32[]{:S(2)}) async-start(bf16[64,56,128]{2,1,0:T(8,128)(2,1)} %attend.1), calls=%async_computation.1 | async-start | bytes 1835008 | tf_op jit(solution)/shard_map/all_to_all | solution.py:211
  58.4 32.4 %copy-start.1 = (bf16[2,64,4096]{2,1,0:T(8,128)(2,1)S(1)}, bf16[2,64,4096]{2,1,0:T(8,128)(2,1)}, u32[]{:S(2)}) copy-start(bf16[2,64,4096]{2,1,0:T(8,128)(2,1)} %param.8) | copy-start | bytes 3145732
  81.6 0.9 copy-start
  86.1 14.7 %all-to-all-start.2 = ((bf16[4,128,256]{2,1,0:T(8,128)(2,1)}), bf16[4,128,256]{2,1,0:T(8,128)(2,1)S(1)}, u32[]{:S(2)}, u32[]{:S(2)}) async-start(bf16[4,128,256]{2,1,0:T(8,128)(2,1)} %broadcast_in_dim.38), calls=%async_computation.2 | async-start | bytes 524288 | tf_op jit(solution)/shard_map/all_to_all | solution.py:227
  90.9 10.3 %collective-permute-start = (bf16[128,1024]{1,0:T(8,128)(2,1)S(1)}, bf16[128,1024]{1,0:T(8,128)(2,1)S(1)}, u32[]{:S(2)}, u32[]{:S(2)}) collective-permute-start(bf16[128,1024]{1,0:T(8,128)(2,1)S(1)} %get-tuple-element.8), channel_id=1, source_target_pairs={{0,128},{128,256},{256,384},{384,0},{1,129},{129,257},{257,385},{3... | collective-permute-start | bytes 786440 | tf_op jit(solution)/shard_map/ppermute | solution.py:170
  94.3 10.4 %collective-permute-start.2 = (bf16[128,1024]{1,0:T(8,128)(2,1)S(1)}, bf16[128,1024]{1,0:T(8,128)(2,1)S(1)}, u32[]{:S(2)}, u32[]{:S(2)}) collective-permute-start(bf16[128,1024]{1,0:T(8,128)(2,1)S(1)} %get-tuple-element.7), channel_id=1, source_target_pairs={{0,384},{128,0},{256,128},{384,256},{1,385},{129,1},{257,129},{385... | collective-permute-start | bytes 786440 | tf_op jit(solution)/shard_map/ppermute | solution.py:170
  96.7 12.0 %collective-permute-start.1 = (bf16[128,1024]{1,0:T(8,128)(2,1)S(1)}, bf16[128,1024]{1,0:T(8,128)(2,1)S(1)}, u32[]{:S(2)}, u32[]{:S(2)}) collective-permute-start(bf16[128,1024]{1,0:T(8,128)(2,1)S(1)} %get-tuple-element.6), channel_id=1, source_target_pairs={{0,256},{128,384},{256,0},{384,128},{1,257},{129,385},{257,1},{385... | collective-permute-start | bytes 786440 | tf_op jit(solution)/shard_map/ppermute | solution.py:170
  109.1 3.8 %collective-permute-start.3 = (f32[16,32,256]{2,1,0:T(8,128)S(1)}, f32[16,32,256]{2,1,0:T(8,128)S(1)}, u32[]{:S(2)}, u32[]{:S(2)}) collective-permute-start(f32[16,32,256]{2,1,0:T(8,128)S(1)} %dynamic-slice_bitcast_fusion), channel_id=1, source_target_pairs={{0,1},{1,0},{2,3},{3,2},{4,5},{5,4},{6,7},{7,6},{8,9},{9,8},{10,11... | collective-permute-start | bytes 1572872 | tf_op jit(solution)/shard_map/ppermute | solution.py:240

commit v2 on v1

--- a/solution.py
+++ b/solution.py
@@ -145,7 +145,31 @@
     for part in range(2):
         halo = in_ref[:, 16 + 16 * part : 32 + 16 * part, :].reshape(PAIRS * HALO, HD)
         total = dot(window, halo) + dot(one_hot(here & (slot // 2 == part)), extra)
-        kv_ref[0, :, part * HD : (part + 1) * HD] = total.astype(BF)
+        for copy in range(8):
+            kv_ref[copy, :, part * HD : (part + 1) * HD] = total.astype(BF)
+
+
+def columns_kernel(in_ref, out_ref, choice):
+    narrow, wide = out_ref.shape[2], in_ref.shape[2]
+
+    @pl.when(pl.program_id(0) == 0)
+    def _():
+        target, source = iota((narrow, wide), 0), iota((narrow, wide), 1)
+        base = target % 128 // 32 * 256 + target // 128 * 64 + target % 32
+        for core in range(2):
+            choice[core] = one_hot(source == base + 32 * core)
+
+    rows = in_ref[...].reshape(2 * ROWS, wide)
+    for core in range(2):
+        out_ref[0, core] = dot_t(choice[core], rows).astype(BF)
+
+
+def weigh_kernel(from_ref, *refs):
+    piece_refs, grads_ref, out_ref = refs[:8], refs[8], refs[9]
+    total = dot(piece_refs[0][...], grads_ref[from_ref[0]])
+    for step in range(1, 8):
+        total = total + dot(piece_refs[step][...], grads_ref[from_ref[step]])
+    out_ref[...] = total
 
 
 def whole(shape):
@@ -159,16 +183,32 @@
     index = lax.axis_index(ctx)
     sequence, pair = index // PAIRS, index % PAIRS
 
-    x_at = lax.axis_index("x")
     model = layer_input.shape[2]
-    quarter = model // 4
-    flat_input = layer_input.reshape(2 * ROWS, model)
-    pieces = []
+    picked = pl.pallas_call(
+        columns_kernel,
+        out_shape=jax.ShapeDtypeStruct((4, 2, model // 8, 2 * ROWS), BF),
+        grid=(4,),
+        in_specs=[pl.BlockSpec((2, ROWS, model // 4), lambda i: (0, 0, i))],
+        out_specs=pl.BlockSpec((1, 2, model // 8, 2 * ROWS), lambda i: (i, 0, 0, 0)),
+        scratch_shapes=[pltpu.VMEM((2, model // 8, model // 4), BF)],
+        name="columns",
+    )(layer_input)
+    picked = picked.reshape(8, model // 8, 2 * ROWS)
+    x_at, core = lax.axis_index("x"), lax.axis_index("core")
+    columns, origins = [], []
     for step in range(4):
-        piece = lax.dynamic_slice_in_dim(flat_input, (x_at + step) % 4 * quarter, quarter, 1)
-        if step:
-            piece = lax.ppermute(piece, "x", [(i, (i + step) % 4) for i in range(4)])
-        pieces.append(piece)
+        for swap in range(2):
+            target = (x_at + step) % 4 * 2 + (core + swap) % 2
+            piece = lax.dynamic_index_in_dim(picked, target, 0, keepdims=False)
+            if step or swap:
+                route = [
+                    (2 * i + j, (i + step) % 4 * 2 + (j + swap) % 2)
+                    for i in range(4)
+                    for j in range(2)
+                ]
+                piece = lax.ppermute(piece, ("x", "core"), route)
+            columns.append(piece)
+            origins.append((x_at - step) % 4 * 2 + (core + swap) % 2)
 
     row_spec = lambda width: pl.BlockSpec((1, ROWS, width), lambda s: (s, 0, 0))
     sent = pl.pallas_call(
@@ -181,6 +221,7 @@
         name="pack",
     )(queries, out_grad, attn_output, key_states, value_states)
     arrived = lax.all_to_all(sent, ctx, 0, 0, tiled=True)
+    arrived, *columns = lax.optimization_barrier((arrived, *columns))
 
     docs = lax.dynamic_index_in_dim(doc_ids, sequence, 0, keepdims=False)
     places = lax.dynamic_index_in_dim(positions, sequence, 0, keepdims=False).reshape(CTX, ROWS)
@@ -214,36 +255,35 @@
         collect_kernel,
         out_shape=(
             jax.ShapeDtypeStruct((2, ROWS, HEADS * HD), BF),
-            jax.ShapeDtypeStruct((2, ROWS, 2 * HD), BF),
+            jax.ShapeDtypeStruct((8, 2 * ROWS, 2 * HD), BF),
         ),
         grid=(2,),
         in_specs=[pl.BlockSpec((PAIRS, BACK, HD), lambda s: (s, 0, 0))],
-        out_specs=(row_spec(HEADS * HD), row_spec(2 * HD)),
+        out_specs=(
+            row_spec(HEADS * HD),
+            pl.BlockSpec((8, ROWS, 2 * HD), lambda s: (0, s, 0)),
+        ),
         scratch_shapes=[pltpu.VMEM((PAIRS * 16, HD), F32)],
         name="collect",
     )(home)
 
-    flat_grad = kv_grad.reshape(2 * ROWS, 2 * HD)
-    grads = lax.all_to_all(
-        jnp.broadcast_to(flat_grad[None], (4, 2 * ROWS, 2 * HD)), "x", 0, 0, tiled=True
+    grads = lax.all_to_all(kv_grad, ("x", "core"), 0, 0, tiled=True)
+    vmem = pl.BlockSpec(memory_space=pltpu.VMEM)
+    part = pl.pallas_call(
+        weigh_kernel,
+        out_shape=jax.ShapeDtypeStruct((model // 8, 2 * HD), F32),
+        in_specs=[pl.BlockSpec(memory_space=pltpu.SMEM)] + [vmem] * 9,
+        out_specs=vmem,
+        name="weigh",
+    )(jnp.stack(origins), *columns, grads)
+    part = lax.all_to_all(part.reshape(4, 128, 2 * HD), "y", 0, 0, tiled=True)
+    part = jnp.sum(part, axis=0)
+    part = lax.all_to_all(part.reshape(16, 8, 2 * HD), ("zl", "zh"), 0, 0, tiled=True)
+    part = jnp.sum(part, axis=0)
+    shares = lax.all_to_all(
+        jnp.broadcast_to(part[None], (8, 8, 2 * HD)), ("zh", "core"), 0, 0, tiled=True
     )
-    part = jnp.zeros((quarter, 2 * HD), F32)
-    for step in range(4):
-        grad = lax.dynamic_index_in_dim(grads, (x_at - step) % 4, 0, keepdims=False)
-        part = part + lax.dot_general(
-            pieces[step], grad, (((0,), (0,)), ((), ())), preferred_element_type=F32
-        )
-    core = lax.axis_index("core")
-    halves = part.reshape(16, 2, 32, 2 * HD)
-    mine = lax.dynamic_index_in_dim(halves, core, 1, keepdims=False)
-    other = lax.dynamic_index_in_dim(halves, 1 - core, 1, keepdims=False)
-    mine = mine + lax.ppermute(other, "core", [(0, 1), (1, 0)])
-    mine = jnp.sum(lax.all_to_all(mine, ("zl", "y"), 0, 0, tiled=True), axis=0)
-    dp = lax.axis_size("zh") * 2
-    shares = lax.all_to_all(
-        jnp.broadcast_to(mine[None], (dp, 32, 2 * HD)), ("zh", "core"), 0, 0, tiled=True
-    )
-    weight_grad = jnp.sum(shares.reshape(dp // 2, 64, 2 * HD), axis=0)
+    weight_grad = shares.reshape(4, 2, 8, 2 * HD).transpose(1, 0, 2, 3).reshape(64, 2 * HD)
     return (query_grad, weight_grad)
 
 

time: 169 us -> 171 us (1.012)
  the two profiles are of different devices: /device:TPU:34 before, /device:TPU:1 now
where the time goes in v2:
time: 171 us; the launch traced here: 170 us
  blocking collectives  91.3 us (53%)
  starting transfers between devices  40.1 us (23%)
  Pallas kernels  18.6 us (11%)
  waiting for transfers between devices  13.8 us (8%)
  local copies, waits for them, and re-layouts  5.17 us (3%)
    all_to_all x1, blocking collectives, local(): home = lax.all_to_all(back, ctx, 0, 0, tiled=True)  34.8 us
    all_to_all x1, blocking collectives, local(): lax.all_to_all(part.reshape(16, 8, 2 * HD), ('zl', 'zh'), 0, 0, tiled=True)  24.4 us
    ppermute x7, starting transfers between devices, local(): piece = lax.ppermute(piece, ('x', 'core'), route)  22.1 us
    all_to_all x1, blocking collectives, local(): lax.all_to_all(jnp.broadcast_to(part[None], (8, 8, 2 * HD)), ('zh', 'core...  20 us
    all_to_all x1, starting transfers between devices, local(): arrived = lax.all_to_all(sent, ctx, 0, 0, tiled=True)  12.6 us
    all_to_all x1, blocking collectives, local(): part = lax.all_to_all(part.reshape(4, 128, 2 * HD), 'y', 0, 0, tiled=True)  12 us
    all_to_all x1, waiting for transfers between devices, local(): grads = lax.all_to_all(kv_grad, ('x', 'core'), 0, 0, tiled=True)  8.84 us
    pallas_call x1, Pallas kernels, local(): pl.pallas_call(columns_kernel, out_shape=jax.ShapeDtypeStruct((4, 2, mode...  5.42 us
  transfers between devices with their start and end apart: 9, of which 4 were waited for; matrix products, arithmetic and copies ran while one was open for 2% of the time, Pallas kernels for 3%

profile of v2, /device:TPU:1, one launch (start us, length us, event | category | flops | bytes accessed | tf_op | source)
XLA Modules:
  0.0 170.3 jit_solution(17848157471279296022)
XLA Ops:
  0.6 2.7 %pack.1 = bf16[64,72,128]{2,1,0:T(8,128)(2,1)} custom-call(bf16[2,64,1024]{2,1,0:T(8,128)(2,1)} %q_ref.1, bf16[2,64,1024]{2,1,0:T(8,128)(2,1)} %g_ref.1, bf16[2,64,1024]{2,1,0:T(8,128)(2,1)} %o_ref.1, bf16[2,64,128]{2,1,0:T(8,128)(2,1)} %k_ref.1, bf16[2,64,128]{2,1,0:T(8,128)(2,1)} %v_ref.1), custom_call_target="tpu_custom_call" | custom-call | tf_op jit(solution)/shard_map/pack/pallas_call | solution.py:214
  3.3 12.6 %all-to-all-start = ((bf16[64,72,128]{2,1,0:T(8,128)(2,1)}), bf16[64,72,128]{2,1,0:T(8,128)(2,1)S(1)}, u32[]{:S(2)}, u32[]{:S(2)}) async-start(bf16[64,72,128]{2,1,0:T(8,128)(2,1)} %pack.1), calls=%async_computation | async-start | bytes 2359296 | tf_op jit(solution)/shard_map/all_to_all | solution.py:223
  16.0 5.4 %columns.1 = bf16[4,2,512,128]{3,2,1,0:T(8,128)(2,1)} custom-call(bf16[2,64,4096]{2,1,0:T(8,128)(2,1)} %in_ref.1), custom_call_target="tpu_custom_call" | custom-call | tf_op jit(solution)/shard_map/columns/pallas_call | solution.py:187
  21.4 2.0 %dynamic-slice_bitcast_fusion = (bf16[512,128]{1,0:T(8,128)(2,1)S(1)}, bf16[512,128]{1,0:T(8,128)(2,1)S(1)}, bf16[512,128]{1,0:T(8,128)(2,1)S(1)}, bf16[512,128]...) fusion(bf16[8,512,128]{2,1,0:T(8,128)(2,1)} %bitcast.32, ...), kind=kLoop, calls=%fused_computation.2 | loop fusion | bytes 2097184 | tf_op jit(solution)/shard_map/jit(dynamic_index_in_dim)/squeeze | solution.py:202
  23.4 2.8 %collective-permute-start = (bf16[512,128]{1,0:T(8,128)(2,1)S(1)}, bf16[512,128]{1,0:T(8,128)(2,1)S(1)}, u32[]{:S(2)}, u32[]{:S(2)}) collective-permute-start(bf16[512,128]{1,0:T(8,128)(2,1)S(1)} %get-tuple-element.30), channel_id=1, source_target_pairs={{0,1},{1,0},{128,129},{129,128},{256,257},{257,256},{384,385},{385... | collective-permute-start | bytes 393224 | tf_op jit(solution)/shard_map/ppermute | solution.py:209
  26.3 3.2 %collective-permute-start.1 = (bf16[512,128]{1,0:T(8,128)(2,1)S(1)}, bf16[512,128]{1,0:T(8,128)(2,1)S(1)}, u32[]{:S(2)}, u32[]{:S(2)}) collective-permute-start(bf16[512,128]{1,0:T(8,128)(2,1)S(1)} %get-tuple-element.29), channel_id=1, source_target_pairs={{0,128},{1,129},{128,256},{129,257},{256,384},{257,385},{384,0},{3... | collective-permute-start | bytes 393224 | tf_op jit(solution)/shard_map/ppermute | solution.py:209
  29.5 3.4 %collective-permute-start.2 = (bf16[512,128]{1,0:T(8,128)(2,1)S(1)}, bf16[512,128]{1,0:T(8,128)(2,1)S(1)}, u32[]{:S(2)}, u32[]{:S(2)}) collective-permute-start(bf16[512,128]{1,0:T(8,128)(2,1)S(1)} %get-tuple-element.28), channel_id=1, source_target_pairs={{0,129},{1,128},{128,257},{129,256},{256,385},{257,384},{384,1},{3... | collective-permute-start | bytes 393224 | tf_op jit(solution)/shard_map/ppermute | solution.py:209
  32.9 3.2 %collective-permute-start.3 = (bf16[512,128]{1,0:T(8,128)(2,1)S(1)}, bf16[512,128]{1,0:T(8,128)(2,1)S(1)}, u32[]{:S(2)}, u32[]{:S(2)}) collective-permute-start(bf16[512,128]{1,0:T(8,128)(2,1)S(1)} %get-tuple-element.27), channel_id=1, source_target_pairs={{0,256},{1,257},{128,384},{129,385},{256,0},{257,1},{384,128},{385... | collective-permute-start | bytes 393224 | tf_op jit(solution)/shard_map/ppermute | solution.py:209
  36.1 4.0 %collective-permute-start.4 = (bf16[512,128]{1,0:T(8,128)(2,1)S(1)}, bf16[512,128]{1,0:T(8,128)(2,1)S(1)}, u32[]{:S(2)}, u32[]{:S(2)}) collective-permute-start(bf16[512,128]{1,0:T(8,128)(2,1)S(1)} %get-tuple-element.26), channel_id=1, source_target_pairs={{0,257},{1,256},{128,385},{129,384},{256,1},{257,0},{384,129},{385... | collective-permute-start | bytes 393224 | tf_op jit(solution)/shard_map/ppermute | solution.py:209
  40.1 0.1 dynamic-slice_reduce_fusion
  40.2 0.1 reshape.89
  40.2 0.1 pad_dynamic-slice_fusion
  40.3 0.1 convert_reduce_fusion
  40.5 0.1 pad_dynamic-slice_fusion.1
  40.6 0.1 concatenate.15
  40.7 0.1 reshape.90
  40.8 0.1 concatenate.14
  40.9 0.1 broadcast_in_dim.16
  41.0 0.1 convert_element_type.18.qpos_ref
  41.1 0.1 select_reduce_fusion
  41.2 0.1 broadcast_in_dim.18
  41.3 0.1 convert_element_type.21.qlow_ref
  41.4 0.0 collective-permute-done.refs_1_
  41.4 0.0 copy-start.1
  41.4 3.3 %collective-permute-start.5 = (bf16[512,128]{1,0:T(8,128)(2,1)S(1)}, bf16[512,128]{1,0:T(8,128)(2,1)S(1)}, u32[]{:S(2)}, u32[]{:S(2)}) collective-permute-start(bf16[512,128]{1,0:T(8,128)(2,1)S(1)} %get-tuple-element.25), channel_id=1, source_target_pairs={{0,384},{1,385},{128,0},{129,1},{256,128},{257,129},{384,256},{385... | collective-permute-start | bytes 393224 | tf_op jit(solution)/shard_map/ppermute | solution.py:209
  44.7 0.0 collective-permute-done.1.refs_2_
  44.8 0.0 copy-start.2
  44.8 2.3 %collective-permute-start.6 = (bf16[512,128]{1,0:T(8,128)(2,1)S(1)}, bf16[512,128]{1,0:T(8,128)(2,1)S(1)}, u32[]{:S(2)}, u32[]{:S(2)}) collective-permute-start(bf16[512,128]{1,0:T(8,128)(2,1)S(1)} %get-tuple-element.24), channel_id=1, source_target_pairs={{0,385},{1,384},{128,1},{129,0},{256,129},{257,128},{384,257},{385... | collective-permute-start | bytes 393224 | tf_op jit(solution)/shard_map/ppermute | solution.py:209
  47.0 0.0 collective-permute-done.2.refs_3_
  47.1 0.0 collective-permute-done.3.refs_4_
  47.1 0.0 copy-start.4
  47.1 0.2 collective-permute-done.4.refs_5_
  47.3 1.1 collective-permute-done.5.refs_6_
  48.4 3.6 %collective-permute-done.6.refs_7_ = bf16[512,128]{1,0:T(8,128)(2,1)S(1)} collective-permute-done((bf16[512,128]{1,0:T(8,128)(2,1)S(1)}, bf16[512,128]{1,0:T(8,128)(2,1)S(1)}, u32[]{:S(2)}, u32[]{:S(2)}) %collective-permute-start.6) | collective-permute-done | bytes 131104 | tf_op jit(solution)/shard_map/ppermute | solution.py:209
  52.1 0.0 all-to-all-done.in_ref
  52.1 5.3 %attend.1 = bf16[64,56,128]{2,1,0:T(8,128)(2,1)S(1)} custom-call(bf16[64,72,128]{2,1,0:T(8,128)(2,1)S(1)} %all-to-all-done.in_ref, f32[1,1152]{1,0:T(1,128)S(1)} %add_convert_fusion.kpos_ref, f32[1,1024]{1,0:T(1,128)S(1)} %convert_element_type.18.qpos_ref, f32[1,1024]{1,0:T(1,128)S(1)} %convert_element_type.21.qlow_ref), custom_call_target="tpu_custom_call" | custom-call | tf_op jit(solution)/shard_map/attend/pallas_call | solution.py:237
  57.4 34.8 %all_to_all.30.in_ref = bf16[64,56,128]{2,1,0:T(8,128)(2,1)} all-to-all(bf16[64,56,128]{2,1,0:T(8,128)(2,1)S(1)} %attend.1), channel_id=1, replica_groups=mesh['x'=4,'zl'=4,'y'=4,'zh'=4,'core'=2] {'x','zl','y'}, dimensions={0} | all-to-all | bytes 1835008 | tf_op jit(solution)/shard_map/all_to_all | solution.py:252
  92.1 0.0 copy-done.1
  92.2 2.2 %collect.1 = (bf16[2,64,1024]{2,1,0:T(8,128)(2,1)}, bf16[8,128,256]{2,1,0:T(8,128)(2,1)}) custom-call(bf16[64,56,128]{2,1,0:T(8,128)(2,1)} %all_to_all.30.in_ref), custom_call_target="tpu_custom_call" | custom-call | tf_op jit(solution)/shard_map/collect/pallas_call | solution.py:254
  94.4 5.4 %all-to-all-start.2 = ((bf16[8,128,256]{2,1,0:T(8,128)(2,1)}), bf16[8,128,256]{2,1,0:T(8,128)(2,1)S(1)}, u32[]{:S(2)}, u32[]{:S(2)}) async-start(bf16[8,128,256]{2,1,0:T(8,128)(2,1)} %get-tuple-element.23), calls=%async_computation.2 | async-start | bytes 1048576 | tf_op jit(solution)/shard_map/all_to_all | solution.py:270
  99.8 0.7 stack.35.from_ref
  100.5 8.8 %all-to-all-done.2.refs_8_ = bf16[8,128,256]{2,1,0:T(8,128)(2,1)S(1)} async-done(((bf16[8,128,256]{2,1,0:T(8,128)(2,1)}), bf16[8,128,256]{2,1,0:T(8,128)(2,1)S(1)}, u32[]{:S(2)}, u32[]{:S(2)}) %all-to-all-start.2) | async-done | bytes 524320 | tf_op jit(solution)/shard_map/all_to_all | solution.py:270
  109.3 0.8 copy-done
  110.1 2.9 %weigh.1 = f32[512,256]{1,0:T(8,128)} custom-call(s32[8]{0:T(128)} %stack.35.from_ref, bf16[512,128]{1,0:T(8,128)(2,1)} %get-tuple-element.15.refs_0_, bf16[512,128]{1,0:T(8,128)(2,1)} %copy-done.1, bf16[512,128]{1,0:T(8,128)(2,1)} %copy-done.2, bf16[512,128]{1,0:T(8,128)(2,1)} %copy-done.3, bf16[512,128]{1,0:T(8,128)(2,1)} %copy-done.4, ...), custom_call_target="tpu_custom_call" | custom-call | tf_op jit(solution)/shard_map/weigh/pallas_call | solution.py:272
  113.1 12.0 %all_to_all.31 = f32[4,128,256]{2,1,0:T(8,128)S(1)} all-to-all(f32[4,128,256]{2,1,0:T(8,128)} %bitcast.33), channel_id=1, replica_groups=mesh['x'=4,'zl'=4,'y'=4,'zh'=4,'core'=2] {'y'}, dimensions={0} | all-to-all | bytes 1048576 | tf_op jit(solution)/shard_map/all_to_all | solution.py:279
  125.1 24.4 %all_to_all.32 = f32[16,8,256]{2,1,0:T(8,128)S(1)} all-to-all(f32[16,8,256]{2,1,0:T(8,128)S(1)} %bitcast.34), channel_id=1, replica_groups=mesh['x'=4,'zl'=4,'y'=4,'zh'=4,'core'=2] {'zl','zh'}, dimensions={0} | all-to-all | bytes 262144 | tf_op jit(solution)/shard_map/all_to_all | solution.py:281
  149.6 20.0 %all_to_all.33 = f32[8,8,256]{2,1,0:T(8,128)S(1)} all-to-all(f32[8,8,256]{2,1,0:T(8,128)S(1)} %broadcast_in_dim.30), channel_id=1, replica_groups=mesh['x'=4,'zl'=4,'y'=4,'zh'=4,'core'=2] {'zh','core'}, dimensions={0} | all-to-all | bytes 131072 | tf_op jit(solution)/shard_map/all_to_all | solution.py:283
  169.6 0.6 copy.11
  (21 shorter events, 0.1 us)
Async XLA Ops:
  3.3 48.7 %all-to-all-start = ((bf16[64,72,128]{2,1,0:T(8,128)(2,1)}), bf16[64,72,128]{2,1,0:T(8,128)(2,1)S(1)}, u32[]{:S(2)}, u32[]{:S(2)}) async-start(bf16[64,72,128]{2,1,0:T(8,128)(2,1)} %pack.1), calls=%async_computation | async-start | bytes 2359296 | tf_op jit(solution)/shard_map/all_to_all | solution.py:223
  21.4 18.7 %copy-start.8 = (s32[2,4096]{1,0:T(2,128)S(1)}, s32[2,4096]{1,0:T(2,128)}, u32[]{:S(2)}) copy-start(s32[2,4096]{1,0:T(2,128)} %param.15) | copy-start | bytes 98308
  21.4 18.7 %copy-start.9 = (s32[2,4096]{1,0:T(2,128)S(1)}, s32[2,4096]{1,0:T(2,128)}, u32[]{:S(2)}) copy-start(s32[2,4096]{1,0:T(2,128)} %param.14) | copy-start | bytes 98308
  23.4 18.0 %collective-permute-start = (bf16[512,128]{1,0:T(8,128)(2,1)S(1)}, bf16[512,128]{1,0:T(8,128)(2,1)S(1)}, u32[]{:S(2)}, u32[]{:S(2)}) collective-permute-start(bf16[512,128]{1,0:T(8,128)(2,1)S(1)} %get-tuple-element.30), channel_id=1, source_target_pairs={{0,1},{1,0},{128,129},{129,128},{256,257},{257,256},{384,385},{385... | collective-permute-start | bytes 393224 | tf_op jit(solution)/shard_map/ppermute | solution.py:209
  26.3 18.5 %collective-permute-start.1 = (bf16[512,128]{1,0:T(8,128)(2,1)S(1)}, bf16[512,128]{1,0:T(8,128)(2,1)S(1)}, u32[]{:S(2)}, u32[]{:S(2)}) collective-permute-start(bf16[512,128]{1,0:T(8,128)(2,1)S(1)} %get-tuple-element.29), channel_id=1, source_target_pairs={{0,128},{1,129},{128,256},{129,257},{256,384},{257,385},{384,0},{3... | collective-permute-start | bytes 393224 | tf_op jit(solution)/shard_map/ppermute | solution.py:209
  29.5 17.5 %collective-permute-start.2 = (bf16[512,128]{1,0:T(8,128)(2,1)S(1)}, bf16[512,128]{1,0:T(8,128)(2,1)S(1)}, u32[]{:S(2)}, u32[]{:S(2)}) collective-permute-start(bf16[512,128]{1,0:T(8,128)(2,1)S(1)} %get-tuple-element.28), channel_id=1, source_target_pairs={{0,129},{1,128},{128,257},{129,256},{256,385},{257,384},{384,1},{3... | collective-permute-start | bytes 393224 | tf_op jit(solution)/shard_map/ppermute | solution.py:209
  32.9 14.2 %collective-permute-start.3 = (bf16[512,128]{1,0:T(8,128)(2,1)S(1)}, bf16[512,128]{1,0:T(8,128)(2,1)S(1)}, u32[]{:S(2)}, u32[]{:S(2)}) collective-permute-start(bf16[512,128]{1,0:T(8,128)(2,1)S(1)} %get-tuple-element.27), channel_id=1, source_target_pairs={{0,256},{1,257},{128,384},{129,385},{256,0},{257,1},{384,128},{385... | collective-permute-start | bytes 393224 | tf_op jit(solution)/shard_map/ppermute | solution.py:209
  36.1 11.2 %collective-permute-start.4 = (bf16[512,128]{1,0:T(8,128)(2,1)S(1)}, bf16[512,128]{1,0:T(8,128)(2,1)S(1)}, u32[]{:S(2)}, u32[]{:S(2)}) collective-permute-start(bf16[512,128]{1,0:T(8,128)(2,1)S(1)} %get-tuple-element.26), channel_id=1, source_target_pairs={{0,257},{1,256},{128,385},{129,384},{256,1},{257,0},{384,129},{385... | collective-permute-start | bytes 393224 | tf_op jit(solution)/shard_map/ppermute | solution.py:209
  41.4 50.7 %copy-start.1 = (bf16[512,128]{1,0:T(8,128)(2,1)}, bf16[512,128]{1,0:T(8,128)(2,1)S(1)}, u32[]{:S(2)}) copy-start(bf16[512,128]{1,0:T(8,128)(2,1)S(1)} %collective-permute-done.refs_1_) | copy-start | bytes 393220
  41.4 7.0 %collective-permute-start.5 = (bf16[512,128]{1,0:T(8,128)(2,1)S(1)}, bf16[512,128]{1,0:T(8,128)(2,1)S(1)}, u32[]{:S(2)}, u32[]{:S(2)}) collective-permute-start(bf16[512,128]{1,0:T(8,128)(2,1)S(1)} %get-tuple-element.25), channel_id=1, source_target_pairs={{0,384},{1,385},{128,0},{129,1},{256,128},{257,129},{384,256},{385... | collective-permute-start | bytes 393224 | tf_op jit(solution)/shard_map/ppermute | solution.py:209
  44.8 47.4 %copy-start.2 = (bf16[512,128]{1,0:T(8,128)(2,1)}, bf16[512,128]{1,0:T(8,128)(2,1)S(1)}, u32[]{:S(2)}) copy-start(bf16[512,128]{1,0:T(8,128)(2,1)S(1)} %collective-permute-done.1.refs_2_) | copy-start | bytes 393220
  44.8 7.3 %collective-permute-start.6 = (bf16[512,128]{1,0:T(8,128)(2,1)S(1)}, bf16[512,128]{1,0:T(8,128)(2,1)S(1)}, u32[]{:S(2)}, u32[]{:S(2)}) collective-permute-start(bf16[512,128]{1,0:T(8,128)(2,1)S(1)} %get-tuple-element.24), channel_id=1, source_target_pairs={{0,385},{1,384},{128,1},{129,0},{256,129},{257,128},{384,257},{385... | collective-permute-start | bytes 393224 | tf_op jit(solution)/shard_map/ppermute | solution.py:209
  47.0 45.1 %copy-start.3 = (bf16[512,128]{1,0:T(8,128)(2,1)}, bf16[512,128]{1,0:T(8,128)(2,1)S(1)}, u32[]{:S(2)}) copy-start(bf16[512,128]{1,0:T(8,128)(2,1)S(1)} %collective-permute-done.2.refs_3_) | copy-start | bytes 393220
  47.1 45.1 %copy-start.4 = (bf16[512,128]{1,0:T(8,128)(2,1)}, bf16[512,128]{1,0:T(8,128)(2,1)S(1)}, u32[]{:S(2)}) copy-start(bf16[512,128]{1,0:T(8,128)(2,1)S(1)} %collective-permute-done.3.refs_4_) | copy-start | bytes 393220
  47.3 44.9 %copy-start.5 = (bf16[512,128]{1,0:T(8,128)(2,1)}, bf16[512,128]{1,0:T(8,128)(2,1)S(1)}, u32[]{:S(2)}) copy-start(bf16[512,128]{1,0:T(8,128)(2,1)S(1)} %collective-permute-done.4.refs_5_) | copy-start | bytes 393220
  48.4 43.7 %copy-start.6 = (bf16[512,128]{1,0:T(8,128)(2,1)}, bf16[512,128]{1,0:T(8,128)(2,1)S(1)}, u32[]{:S(2)}) copy-start(bf16[512,128]{1,0:T(8,128)(2,1)S(1)} %collective-permute-done.5.refs_6_) | copy-start | bytes 393220
  52.1 40.1 %copy-start.7 = (bf16[512,128]{1,0:T(8,128)(2,1)}, bf16[512,128]{1,0:T(8,128)(2,1)S(1)}, u32[]{:S(2)}) copy-start(bf16[512,128]{1,0:T(8,128)(2,1)S(1)} %collective-permute-done.6.refs_7_) | copy-start | bytes 393220
  94.4 14.9 %all-to-all-start.2 = ((bf16[8,128,256]{2,1,0:T(8,128)(2,1)}), bf16[8,128,256]{2,1,0:T(8,128)(2,1)S(1)}, u32[]{:S(2)}, u32[]{:S(2)}) async-start(bf16[8,128,256]{2,1,0:T(8,128)(2,1)} %get-tuple-element.23), calls=%async_computation.2 | async-start | bytes 1048576 | tf_op jit(solution)/shard_map/all_to_all | solution.py:270
  109.3 0.8 copy-start

commit v3 on v1

--- a/solution.py
+++ b/solution.py
@@ -145,7 +145,8 @@
     for part in range(2):
         halo = in_ref[:, 16 + 16 * part : 32 + 16 * part, :].reshape(PAIRS * HALO, HD)
         total = dot(window, halo) + dot(one_hot(here & (slot // 2 == part)), extra)
-        kv_ref[0, :, part * HD : (part + 1) * HD] = total.astype(BF)
+        for copy in range(4):
+            kv_ref[copy, :, part * HD : (part + 1) * HD] = total.astype(BF)
 
 
 def whole(shape):
@@ -159,16 +160,15 @@
     index = lax.axis_index(ctx)
     sequence, pair = index // PAIRS, index % PAIRS
 
-    x_at = lax.axis_index("x")
-    model = layer_input.shape[2]
-    quarter = model // 4
-    flat_input = layer_input.reshape(2 * ROWS, model)
-    pieces = []
+    quarter = layer_input.shape[2] // 4
+    x_at, core = lax.axis_index("x"), lax.axis_index("core")
+    flat_input = layer_input.reshape(2 * ROWS, 4 * quarter)
+    columns = []
     for step in range(4):
         piece = lax.dynamic_slice_in_dim(flat_input, (x_at + step) % 4 * quarter, quarter, 1)
         if step:
             piece = lax.ppermute(piece, "x", [(i, (i + step) % 4) for i in range(4)])
-        pieces.append(piece)
+        columns.append(piece)
 
     row_spec = lambda width: pl.BlockSpec((1, ROWS, width), lambda s: (s, 0, 0))
     sent = pl.pallas_call(
@@ -181,6 +181,7 @@
         name="pack",
     )(queries, out_grad, attn_output, key_states, value_states)
     arrived = lax.all_to_all(sent, ctx, 0, 0, tiled=True)
+    arrived, *columns = lax.optimization_barrier((arrived, *columns))
 
     docs = lax.dynamic_index_in_dim(doc_ids, sequence, 0, keepdims=False)
     places = lax.dynamic_index_in_dim(positions, sequence, 0, keepdims=False).reshape(CTX, ROWS)
@@ -214,36 +215,36 @@
         collect_kernel,
         out_shape=(
             jax.ShapeDtypeStruct((2, ROWS, HEADS * HD), BF),
-            jax.ShapeDtypeStruct((2, ROWS, 2 * HD), BF),
+            jax.ShapeDtypeStruct((4, 2 * ROWS, 2 * HD), BF),
         ),
         grid=(2,),
         in_specs=[pl.BlockSpec((PAIRS, BACK, HD), lambda s: (s, 0, 0))],
-        out_specs=(row_spec(HEADS * HD), row_spec(2 * HD)),
+        out_specs=(
+            row_spec(HEADS * HD),
+            pl.BlockSpec((4, ROWS, 2 * HD), lambda s: (0, s, 0)),
+        ),
         scratch_shapes=[pltpu.VMEM((PAIRS * 16, HD), F32)],
         name="collect",
     )(home)
 
-    flat_grad = kv_grad.reshape(2 * ROWS, 2 * HD)
-    grads = lax.all_to_all(
-        jnp.broadcast_to(flat_grad[None], (4, 2 * ROWS, 2 * HD)), "x", 0, 0, tiled=True
-    )
+    grads = lax.all_to_all(kv_grad, "x", 0, 0, tiled=True)
     part = jnp.zeros((quarter, 2 * HD), F32)
     for step in range(4):
         grad = lax.dynamic_index_in_dim(grads, (x_at - step) % 4, 0, keepdims=False)
         part = part + lax.dot_general(
-            pieces[step], grad, (((0,), (0,)), ((), ())), preferred_element_type=F32
+            columns[step], grad, (((0,), (0,)), ((), ())), preferred_element_type=F32
         )
-    core = lax.axis_index("core")
     halves = part.reshape(16, 2, 32, 2 * HD)
     mine = lax.dynamic_index_in_dim(halves, core, 1, keepdims=False)
     other = lax.dynamic_index_in_dim(halves, 1 - core, 1, keepdims=False)
-    mine = mine + lax.ppermute(other, "core", [(0, 1), (1, 0)])
-    mine = jnp.sum(lax.all_to_all(mine, ("zl", "y"), 0, 0, tiled=True), axis=0)
-    dp = lax.axis_size("zh") * 2
-    shares = lax.all_to_all(
-        jnp.broadcast_to(mine[None], (dp, 32, 2 * HD)), ("zh", "core"), 0, 0, tiled=True
+    mine = (mine + lax.ppermute(other, "core", [(0, 1), (1, 0)])).astype(BF)
+    mine = lax.all_to_all(mine, ("zl", "y"), 0, 0, tiled=True)
+    mine = jnp.sum(mine.astype(F32), axis=0)
+    mine = lax.all_to_all(
+        jnp.broadcast_to(mine[None], (4, 32, 2 * HD)), "zh", 0, 0, tiled=True
     )
-    weight_grad = jnp.sum(shares.reshape(dp // 2, 64, 2 * HD), axis=0)
+    mine = jnp.sum(mine, axis=0)
+    weight_grad = lax.all_gather(mine, "core", axis=0, tiled=True)
     return (query_grad, weight_grad)
 
 

time: 169 us -> 147 us (0.87)
  the two profiles are of different devices: /device:TPU:34 before, /device:TPU:1 now
where the time goes in v3:
time: 147 us; the launch traced here: 146 us
  blocking collectives  74.1 us (50%)
  starting transfers between devices  31.8 us (22%)
  waiting for transfers between devices  25.7 us (17%)
  Pallas kernels  10.1 us (7%)
  local copies, waits for them, and re-layouts  1.81 us (1%)
    all_to_all x1, blocking collectives, local(): home = lax.all_to_all(back, ctx, 0, 0, tiled=True)  31.6 us
    all_to_all x1, blocking collectives, local(): lax.all_to_all(jnp.broadcast_to(mine[None], (4, 32, 2 * HD)), 'zh', 0, 0,...  25.3 us
    ppermute x3, waiting for transfers between devices, local(): piece = lax.ppermute(piece, 'x', [(i, (i + step) % 4) for i in range(4)])  14.8 us
    all_to_all x1, blocking collectives, local(): mine = lax.all_to_all(mine, ('zl', 'y'), 0, 0, tiled=True)  12.7 us
    all_to_all x1, starting transfers between devices, local(): arrived = lax.all_to_all(sent, ctx, 0, 0, tiled=True)  12.7 us
    ppermute x3, starting transfers between devices, local(): piece = lax.ppermute(piece, 'x', [(i, (i + step) % 4) for i in range(4)])  10.4 us
    all_to_all x1, waiting for transfers between devices, local(): grads = lax.all_to_all(kv_grad, 'x', 0, 0, tiled=True)  5.42 us
    ppermute x1, starting transfers between devices, local(): mine = (mine + lax.ppermute(other, 'core', [(0, 1), (1, 0)])).astype(BF)  5.35 us
  transfers between devices with their start and end apart: 6, of which 5 were waited for; matrix products, arithmetic and copies ran while one was open for 1% of the time, Pallas kernels for 0%

profile of v3, /device:TPU:1, one launch (start us, length us, event | category | flops | bytes accessed | tf_op | source)
XLA Modules:
  0.0 146.3 jit_solution(4942038118986182747)
XLA Ops:
  0.6 2.7 %pack.1 = bf16[64,72,128]{2,1,0:T(8,128)(2,1)} custom-call(bf16[2,64,1024]{2,1,0:T(8,128)(2,1)} %q_ref.1, bf16[2,64,1024]{2,1,0:T(8,128)(2,1)} %g_ref.1, bf16[2,64,1024]{2,1,0:T(8,128)(2,1)} %o_ref.1, bf16[2,64,128]{2,1,0:T(8,128)(2,1)} %k_ref.1, bf16[2,64,128]{2,1,0:T(8,128)(2,1)} %v_ref.1), custom_call_target="tpu_custom_call" | custom-call | tf_op jit(solution)/shard_map/pack/pallas_call | solution.py:174
  3.3 0.0 copy-start
  3.3 12.7 %all-to-all-start = ((bf16[64,72,128]{2,1,0:T(8,128)(2,1)}), bf16[64,72,128]{2,1,0:T(8,128)(2,1)S(1)}, u32[]{:S(2)}, u32[]{:S(2)}) async-start(bf16[64,72,128]{2,1,0:T(8,128)(2,1)} %pack.1), calls=%async_computation | async-start | bytes 2359296 | tf_op jit(solution)/shard_map/all_to_all | solution.py:183
  16.0 0.0 copy-start.1
  16.0 0.0 copy-start.2
  16.1 0.0 copy-done
  16.1 0.1 constant_dynamic-slice_fusion.1
  16.2 2.9 %collective-permute-start = (bf16[128,1024]{1,0:T(8,128)(2,1)S(1)}, bf16[128,1024]{1,0:T(8,128)(2,1)S(1)}, u32[]{:S(2)}, u32[]{:S(2)}) collective-permute-start(bf16[128,1024]{1,0:T(8,128)(2,1)S(1)} %get-tuple-element.18), channel_id=1, source_target_pairs={{0,128},{128,256},{256,384},{384,0},{1,129},{129,257},{257,385},{3... | collective-permute-start | bytes 786440 | tf_op jit(solution)/shard_map/ppermute | solution.py:170
  19.1 4.5 %collective-permute-start.1 = (bf16[128,1024]{1,0:T(8,128)(2,1)S(1)}, bf16[128,1024]{1,0:T(8,128)(2,1)S(1)}, u32[]{:S(2)}, u32[]{:S(2)}) collective-permute-start(bf16[128,1024]{1,0:T(8,128)(2,1)S(1)} %get-tuple-element.17), channel_id=1, source_target_pairs={{0,256},{128,384},{256,0},{384,128},{1,257},{129,385},{257,1},{385... | collective-permute-start | bytes 786440 | tf_op jit(solution)/shard_map/ppermute | solution.py:170
  23.7 3.0 %collective-permute-start.2 = (bf16[128,1024]{1,0:T(8,128)(2,1)S(1)}, bf16[128,1024]{1,0:T(8,128)(2,1)S(1)}, u32[]{:S(2)}, u32[]{:S(2)}) collective-permute-start(bf16[128,1024]{1,0:T(8,128)(2,1)S(1)} %get-tuple-element.16), channel_id=1, source_target_pairs={{0,384},{128,0},{256,128},{384,256},{1,385},{129,1},{257,129},{385... | collective-permute-start | bytes 786440 | tf_op jit(solution)/shard_map/ppermute | solution.py:170
  26.7 0.0 copy-done.1
  26.7 0.0 copy-done.2
  26.7 0.1 dynamic-slice_reduce_fusion
  26.8 0.1 reshape.80
  26.8 0.1 pad_dynamic-slice_fusion.1
  26.9 0.1 reshape.81
  27.1 0.1 convert_reduce_fusion.1
  27.2 0.1 select_reduce_fusion
  27.3 0.1 pad_dynamic-slice_fusion
  27.4 0.1 concatenate.15
  27.5 0.1 concatenate.14
  27.6 0.1 broadcast_in_dim.16
  27.7 0.1 convert_element_type.24.qpos_ref
  27.8 0.1 broadcast_in_dim.18
  27.9 0.1 convert_element_type.27.qlow_ref
  28.0 6.7 %collective-permute-done = bf16[128,1024]{1,0:T(8,128)(2,1)S(1)} collective-permute-done((bf16[128,1024]{1,0:T(8,128)(2,1)S(1)}, bf16[128,1024]{1,0:T(8,128)(2,1)S(1)}, u32[]{:S(2)}, u32[]{:S(2)}) %collective-permute-start) | collective-permute-done | bytes 262176 | tf_op jit(solution)/shard_map/ppermute | solution.py:170
  34.7 8.1 %collective-permute-done.1 = bf16[128,1024]{1,0:T(8,128)(2,1)S(1)} collective-permute-done((bf16[128,1024]{1,0:T(8,128)(2,1)S(1)}, bf16[128,1024]{1,0:T(8,128)(2,1)S(1)}, u32[]{:S(2)}, u32[]{:S(2)}) %collective-permute-start.1) | collective-permute-done | bytes 262176 | tf_op jit(solution)/shard_map/ppermute | solution.py:170
  42.8 0.0 collective-permute-done.2
  42.8 4.0 %all-to-all-done.in_ref = bf16[64,72,128]{2,1,0:T(8,128)(2,1)S(1)} async-done(((bf16[64,72,128]{2,1,0:T(8,128)(2,1)}), bf16[64,72,128]{2,1,0:T(8,128)(2,1)S(1)}, u32[]{:S(2)}, u32[]{:S(2)}) %all-to-all-start) | async-done | bytes 1179680 | tf_op jit(solution)/shard_map/all_to_all | solution.py:183
  46.8 5.3 %attend.1 = bf16[64,56,128]{2,1,0:T(8,128)(2,1)S(1)} custom-call(bf16[64,72,128]{2,1,0:T(8,128)(2,1)S(1)} %all-to-all-done.in_ref, f32[1,1152]{1,0:T(1,128)S(1)} %add_convert_fusion.kpos_ref, f32[1,1024]{1,0:T(1,128)S(1)} %convert_element_type.24.qpos_ref, f32[1,1024]{1,0:T(1,128)S(1)} %convert_element_type.27.qlow_ref), custom_call_target="tpu_custom_call" | custom-call | tf_op jit(solution)/shard_map/attend/pallas_call | solution.py:197
  52.1 31.6 %all_to_all.25.in_ref = bf16[64,56,128]{2,1,0:T(8,128)(2,1)} all-to-all(bf16[64,56,128]{2,1,0:T(8,128)(2,1)S(1)} %attend.1), channel_id=1, replica_groups=mesh['x'=4,'zl'=4,'y'=4,'zh'=4,'core'=2] {'x','zl','y'}, dimensions={0} | all-to-all | bytes 1835008 | tf_op jit(solution)/shard_map/all_to_all | solution.py:212
  83.7 2.1 %collect.1 = (bf16[2,64,1024]{2,1,0:T(8,128)(2,1)}, bf16[4,128,256]{2,1,0:T(8,128)(2,1)}) custom-call(bf16[64,56,128]{2,1,0:T(8,128)(2,1)} %all_to_all.25.in_ref), custom_call_target="tpu_custom_call" | custom-call | tf_op jit(solution)/shard_map/collect/pallas_call | solution.py:214
  85.8 3.4 %all-to-all-start.2 = ((bf16[4,128,256]{2,1,0:T(8,128)(2,1)}), bf16[4,128,256]{2,1,0:T(8,128)(2,1)S(1)}, u32[]{:S(2)}, u32[]{:S(2)}) async-start(bf16[4,128,256]{2,1,0:T(8,128)(2,1)} %get-tuple-element.12), calls=%async_computation.2 | async-start | bytes 524288 | tf_op jit(solution)/shard_map/all_to_all | solution.py:230
  89.3 5.4 %all-to-all-done.2 = bf16[4,128,256]{2,1,0:T(8,128)(2,1)S(1)} async-done(((bf16[4,128,256]{2,1,0:T(8,128)(2,1)}), bf16[4,128,256]{2,1,0:T(8,128)(2,1)S(1)}, u32[]{:S(2)}, u32[]{:S(2)}) %all-to-all-start.2) | async-done | bytes 262176 | tf_op jit(solution)/shard_map/all_to_all | solution.py:230
  94.7 0.3 fusion.3
  95.1 0.3 fusion.5
  95.4 0.3 fusion.7
  95.7 0.3 fusion.1
  96.1 5.3 %collective-permute-start.3 = (f32[16,32,256]{2,1,0:T(8,128)S(1)}, f32[16,32,256]{2,1,0:T(8,128)S(1)}, u32[]{:S(2)}, u32[]{:S(2)}) collective-permute-start(f32[16,32,256]{2,1,0:T(8,128)S(1)} %dynamic-slice_bitcast_fusion), channel_id=1, source_target_pairs={{0,1},{1,0},{2,3},{3,2},{4,5},{5,4},{6,7},{7,6},{8,9},{9,8},{10,11... | collective-permute-start | bytes 1572872 | tf_op jit(solution)/shard_map/ppermute | solution.py:240
  101.5 1.5 %collective-permute-done.3 = f32[16,32,256]{2,1,0:T(8,128)S(1)} collective-permute-done((f32[16,32,256]{2,1,0:T(8,128)S(1)}, f32[16,32,256]{2,1,0:T(8,128)S(1)}, u32[]{:S(2)}, u32[]{:S(2)}) %collective-permute-start.3) | collective-permute-done | bytes 524320 | tf_op jit(solution)/shard_map/ppermute | solution.py:240
  103.0 0.1 fusion.2
  103.1 12.7 %all_to_all.26 = bf16[16,32,256]{2,1,0:T(8,128)(2,1)S(1)} all-to-all(bf16[16,32,256]{2,1,0:T(8,128)(2,1)S(1)} %fusion.2), channel_id=1, replica_groups=mesh['x'=4,'zl'=4,'y'=4,'zh'=4,'core'=2] {'zl','y'}, dimensions={0} | all-to-all | bytes 524288 | tf_op jit(solution)/shard_map/all_to_all | solution.py:241
  115.9 25.3 %all_to_all.27 = f32[4,32,256]{2,1,0:T(8,128)S(1)} all-to-all(f32[4,32,256]{2,1,0:T(8,128)S(1)} %broadcast_in_dim.30), channel_id=1, replica_groups=mesh['x'=4,'zl'=4,'y'=4,'zh'=4,'core'=2] {'zh'}, dimensions={0} | all-to-all | bytes 262144 | tf_op jit(solution)/shard_map/all_to_all | solution.py:243
  141.2 4.5 %all_gather.3 = f32[64,256]{1,0:T(8,128)S(1)} all-gather(f32[32,256]{1,0:T(8,128)S(1)} %reduce_sum.29), channel_id=1, replica_groups=mesh['x'=4,'zl'=4,'y'=4,'zh'=4,'core'=2] {'core'}, dimensions={0}, use_global_device_ids=true | all-gather | bytes 98304 | tf_op jit(solution)/shard_map/all_gather | solution.py:247
  145.7 0.6 copy.11
  (7 shorter events, 0.1 us)
Async XLA Ops:
  3.3 12.8 %copy-start = (bf16[2,64,4096]{2,1,0:T(8,128)(2,1)S(1)}, bf16[2,64,4096]{2,1,0:T(8,128)(2,1)}, u32[]{:S(2)}) copy-start(bf16[2,64,4096]{2,1,0:T(8,128)(2,1)} %param.8) | copy-start | bytes 3145732
  3.3 43.5 %all-to-all-start = ((bf16[64,72,128]{2,1,0:T(8,128)(2,1)}), bf16[64,72,128]{2,1,0:T(8,128)(2,1)S(1)}, u32[]{:S(2)}, u32[]{:S(2)}) async-start(bf16[64,72,128]{2,1,0:T(8,128)(2,1)} %pack.1), calls=%async_computation | async-start | bytes 2359296 | tf_op jit(solution)/shard_map/all_to_all | solution.py:183
  16.0 10.7 %copy-start.1 = (s32[2,4096]{1,0:T(2,128)S(1)}, s32[2,4096]{1,0:T(2,128)}, u32[]{:S(2)}) copy-start(s32[2,4096]{1,0:T(2,128)} %param.15) | copy-start | bytes 98308
  16.0 10.7 %copy-start.2 = (s32[2,4096]{1,0:T(2,128)S(1)}, s32[2,4096]{1,0:T(2,128)}, u32[]{:S(2)}) copy-start(s32[2,4096]{1,0:T(2,128)} %param.14) | copy-start | bytes 98308
  16.2 18.5 %collective-permute-start = (bf16[128,1024]{1,0:T(8,128)(2,1)S(1)}, bf16[128,1024]{1,0:T(8,128)(2,1)S(1)}, u32[]{:S(2)}, u32[]{:S(2)}) collective-permute-start(bf16[128,1024]{1,0:T(8,128)(2,1)S(1)} %get-tuple-element.18), channel_id=1, source_target_pairs={{0,128},{128,256},{256,384},{384,0},{1,129},{129,257},{257,385},{3... | collective-permute-start | bytes 786440 | tf_op jit(solution)/shard_map/ppermute | solution.py:170
  19.1 23.7 %collective-permute-start.1 = (bf16[128,1024]{1,0:T(8,128)(2,1)S(1)}, bf16[128,1024]{1,0:T(8,128)(2,1)S(1)}, u32[]{:S(2)}, u32[]{:S(2)}) collective-permute-start(bf16[128,1024]{1,0:T(8,128)(2,1)S(1)} %get-tuple-element.17), channel_id=1, source_target_pairs={{0,256},{128,384},{256,0},{384,128},{1,257},{129,385},{257,1},{385... | collective-permute-start | bytes 786440 | tf_op jit(solution)/shard_map/ppermute | solution.py:170
  23.7 19.2 %collective-permute-start.2 = (bf16[128,1024]{1,0:T(8,128)(2,1)S(1)}, bf16[128,1024]{1,0:T(8,128)(2,1)S(1)}, u32[]{:S(2)}, u32[]{:S(2)}) collective-permute-start(bf16[128,1024]{1,0:T(8,128)(2,1)S(1)} %get-tuple-element.16), channel_id=1, source_target_pairs={{0,384},{128,0},{256,128},{384,256},{1,385},{129,1},{257,129},{385... | collective-permute-start | bytes 786440 | tf_op jit(solution)/shard_map/ppermute | solution.py:170
  85.8 8.9 %all-to-all-start.2 = ((bf16[4,128,256]{2,1,0:T(8,128)(2,1)}), bf16[4,128,256]{2,1,0:T(8,128)(2,1)S(1)}, u32[]{:S(2)}, u32[]{:S(2)}) async-start(bf16[4,128,256]{2,1,0:T(8,128)(2,1)} %get-tuple-element.12), calls=%async_computation.2 | async-start | bytes 524288 | tf_op jit(solution)/shard_map/all_to_all | solution.py:230
  96.1 6.9 %collective-permute-start.3 = (f32[16,32,256]{2,1,0:T(8,128)S(1)}, f32[16,32,256]{2,1,0:T(8,128)S(1)}, u32[]{:S(2)}, u32[]{:S(2)}) collective-permute-start(f32[16,32,256]{2,1,0:T(8,128)S(1)} %dynamic-slice_bitcast_fusion), channel_id=1, source_target_pairs={{0,1},{1,0},{2,3},{3,2},{4,5},{5,4},{6,7},{7,6},{8,9},{9,8},{10,11... | collective-permute-start | bytes 1572872 | tf_op jit(solution)/shard_map/ppermute | solution.py:240

commit v4 on v3

--- a/solution.py
+++ b/solution.py
@@ -133,20 +133,22 @@
 
 
 def collect_kernel(in_ref, q_ref, kv_ref, split):
-    split[...] = in_ref[:, 0:16, :].astype(F32).reshape(PAIRS * 16, HD)
-    for h in range(HEADS):
-        q_ref[0, :, h * HD : (h + 1) * HD] = split[pl.ds(h, ROWS, stride=HEADS), :].astype(BF)
     row, source = iota((ROWS, PAIRS * HALO), 0), iota((ROWS, PAIRS * HALO), 1)
     window = one_hot(row == 2 * (source // HALO) + source % HALO - HALO)
     row, source = iota((ROWS, PAIRS * 8), 0), iota((ROWS, PAIRS * 8), 1)
     slot = source % 8
     here = row == 2 * (source // 8) + slot % 2
-    extra = in_ref[:, 48:56, :].astype(F32).reshape(PAIRS * 8, HD).astype(BF)
-    for part in range(2):
-        halo = in_ref[:, 16 + 16 * part : 32 + 16 * part, :].reshape(PAIRS * HALO, HD)
-        total = dot(window, halo) + dot(one_hot(here & (slot // 2 == part)), extra)
-        for copy in range(4):
-            kv_ref[copy, :, part * HD : (part + 1) * HD] = total.astype(BF)
+    for s in range(2):
+        mine = slice(s * PAIRS, (s + 1) * PAIRS)
+        extra = in_ref[mine, 48:56, :].astype(F32).reshape(PAIRS * 8, HD).astype(BF)
+        for part in range(2):
+            halo = in_ref[mine, 16 + 16 * part : 32 + 16 * part, :].reshape(PAIRS * HALO, HD)
+            total = dot(window, halo) + dot(one_hot(here & (slot // 2 == part)), extra)
+            for copy in range(4):
+                kv_ref[copy, part, s * ROWS : (s + 1) * ROWS] = total.astype(BF)
+        split[...] = in_ref[mine, 0:16, :].astype(F32).reshape(PAIRS * 16, HD)
+        for h in range(HEADS):
+            q_ref[s, :, h * HD : (h + 1) * HD] = split[pl.ds(h, ROWS, stride=HEADS), :].astype(BF)
 
 
 def whole(shape):
@@ -210,41 +212,40 @@
         name="attend",
     )(arrived, kpos.astype(F32), qpos.astype(F32), qlow.astype(F32))
     home = lax.all_to_all(back, ctx, 0, 0, tiled=True)
+    twin = lax.ppermute(jnp.stack(columns), "core", [(0, 1), (1, 0)])
+    home, twin = lax.optimization_barrier((home, twin))
 
     query_grad, kv_grad = pl.pallas_call(
         collect_kernel,
         out_shape=(
             jax.ShapeDtypeStruct((2, ROWS, HEADS * HD), BF),
-            jax.ShapeDtypeStruct((4, 2 * ROWS, 2 * HD), BF),
+            jax.ShapeDtypeStruct((4, 2, 2 * ROWS, HD), BF),
         ),
-        grid=(2,),
-        in_specs=[pl.BlockSpec((PAIRS, BACK, HD), lambda s: (s, 0, 0))],
-        out_specs=(
-            row_spec(HEADS * HD),
-            pl.BlockSpec((4, ROWS, 2 * HD), lambda s: (0, s, 0)),
-        ),
+        grid=(1,),
+        in_specs=[whole((CTX, BACK, HD))],
+        out_specs=(whole((2, ROWS, HEADS * HD)), whole((4, 2, 2 * ROWS, HD))),
         scratch_shapes=[pltpu.VMEM((PAIRS * 16, HD), F32)],
         name="collect",
     )(home)
 
-    grads = lax.all_to_all(kv_grad, "x", 0, 0, tiled=True)
-    part = jnp.zeros((quarter, 2 * HD), F32)
+    grads = lax.all_to_all(
+        kv_grad.reshape(8, 2 * ROWS, HD), ("x", "core"), 0, 0, tiled=True
+    )
+    part = jnp.zeros((quarter, HD), F32)
     for step in range(4):
-        grad = lax.dynamic_index_in_dim(grads, (x_at - step) % 4, 0, keepdims=False)
-        part = part + lax.dot_general(
-            columns[step], grad, (((0,), (0,)), ((), ())), preferred_element_type=F32
-        )
-    halves = part.reshape(16, 2, 32, 2 * HD)
-    mine = lax.dynamic_index_in_dim(halves, core, 1, keepdims=False)
-    other = lax.dynamic_index_in_dim(halves, 1 - core, 1, keepdims=False)
-    mine = (mine + lax.ppermute(other, "core", [(0, 1), (1, 0)])).astype(BF)
-    mine = lax.all_to_all(mine, ("zl", "y"), 0, 0, tiled=True)
-    mine = jnp.sum(mine.astype(F32), axis=0)
-    mine = lax.all_to_all(
-        jnp.broadcast_to(mine[None], (4, 32, 2 * HD)), "zh", 0, 0, tiled=True
-    )
-    mine = jnp.sum(mine, axis=0)
-    weight_grad = lax.all_gather(mine, "core", axis=0, tiled=True)
+        for piece, at in ((columns[step], core), (twin[step], 1 - core)):
+            grad = lax.dynamic_index_in_dim(
+                grads, (x_at - step) % 4 * 2 + at, 0, keepdims=False
+            )
+            part = part + lax.dot_general(
+                piece, grad, (((0,), (0,)), ((), ())), preferred_element_type=F32
+            )
+    part = part.reshape(16, 64, HD).astype(BF)
+    part = lax.all_to_all(part, ("zl", "y"), 0, 0, tiled=True)
+    part = jnp.sum(part.astype(F32), axis=0).astype(BF)
+    part = lax.all_to_all(jnp.broadcast_to(part[None], (4, 64, HD)), "zh", 0, 0, tiled=True)
+    part = jnp.sum(part.astype(F32), axis=0)
+    weight_grad = lax.all_gather(part, "core", axis=1, tiled=True)
     return (query_grad, weight_grad)
 
 

time: 147 us -> 145 us (0.986)
  blocking collectives: 74.1 us -> 40.9 us
  waiting for transfers between devices: 25.7 us -> 45.8 us
  starting transfers between devices: 31.8 us -> 39.1 us
  local copies, waits for them, and re-layouts: 1.81 us -> 4.28 us
    all_to_all x3 -> x2, blocking collectives: 69.6 us -> 35.7 us  [the longest x1 23.8 us: local(): lax.all_to_all(jnp.broadcast_to(part[None], (4, 64, HD)), 'zh', 0, 0, til...]
    all_to_all x1 -> x2, waiting for transfers between devices: 5.42 us -> 26.3 us  [the longest x1 19.8 us: local(): home = lax.all_to_all(back, ctx, 0, 0, tiled=True)]
    all_to_all x1 -> x2, starting transfers between devices: 3.4 us -> 13 us  [the longest x1 7.37 us: local(): home = lax.all_to_all(back, ctx, 0, 0, tiled=True)]
    ppermute x1, starting transfers between devices: 5.35 us -> 3.06 us  [local(): twin = lax.ppermute(jnp.stack(columns), 'core', [(0, 1), (1, 0)])]
    ppermute x3, waiting for transfers between devices: 14.8 us -> 13.3 us  [local(): piece = lax.ppermute(piece, 'x', [(i, (i + step) % 4) for i in range(4)])]
  transfers between devices with their start and end apart: 6 -> 7, of which waited for: 5 -> 6; matrix products, arithmetic and copies ran while one was open for 1% -> 2% of each run, Pallas kernels for 0% -> 0%
where the time goes in v4:
time: 145 us
  waiting for transfers between devices  45.8 us (32%)
  blocking collectives  40.9 us (28%)
  starting transfers between devices  39.1 us (27%)
  Pallas kernels  11.2 us (8%)
  local copies, waits for them, and re-layouts  4.28 us (3%)
  matrix products  2.05 us (1%)
    all_to_all x1, blocking collectives, local(): lax.all_to_all(jnp.broadcast_to(part[None], (4, 64, HD)), 'zh', 0, 0, til...  23.8 us
    all_to_all x1, waiting for transfers between devices, local(): home = lax.all_to_all(back, ctx, 0, 0, tiled=True)  19.8 us
    ppermute x3, waiting for transfers between devices, local(): piece = lax.ppermute(piece, 'x', [(i, (i + step) % 4) for i in range(4)])  13.3 us
    all_to_all x1, starting transfers between devices, local(): arrived = lax.all_to_all(sent, ctx, 0, 0, tiled=True)  12.7 us
    all_to_all x1, blocking collectives, local(): part = lax.all_to_all(part, ('zl', 'y'), 0, 0, tiled=True)  12 us
    ppermute x3, starting transfers between devices, local(): piece = lax.ppermute(piece, 'x', [(i, (i + step) % 4) for i in range(4)])  10.4 us
    all_to_all x1, starting transfers between devices, local(): home = lax.all_to_all(back, ctx, 0, 0, tiled=True)  7.37 us
    all_to_all x1, waiting for transfers between devices, local(): lax.all_to_all(kv_grad.reshape(8, 2 * ROWS, HD), ('x', 'core'), 0, 0, til...  6.52 us
  transfers between devices with their start and end apart: 7, of which 6 were waited for; matrix products, arithmetic and copies ran while one was open for 2% of the time, Pallas kernels for 0%

profile of v4, /device:TPU:1, one launch (start us, length us, event | category | flops | bytes accessed | tf_op | source)
XLA Modules:
  0.0 144.8 jit_solution(3896060982494052863)
XLA Ops:
  0.6 2.7 %pack.1 = bf16[64,72,128]{2,1,0:T(8,128)(2,1)} custom-call(bf16[2,64,1024]{2,1,0:T(8,128)(2,1)} %q_ref.1, bf16[2,64,1024]{2,1,0:T(8,128)(2,1)} %g_ref.1, bf16[2,64,1024]{2,1,0:T(8,128)(2,1)} %o_ref.1, bf16[2,64,128]{2,1,0:T(8,128)(2,1)} %k_ref.1, bf16[2,64,128]{2,1,0:T(8,128)(2,1)} %v_ref.1), custom_call_target="tpu_custom_call" | custom-call | tf_op jit(solution)/shard_map/pack/pallas_call | solution.py:176
  3.3 0.0 copy-start.1
  3.3 12.7 %all-to-all-start = ((bf16[64,72,128]{2,1,0:T(8,128)(2,1)}), bf16[64,72,128]{2,1,0:T(8,128)(2,1)S(1)}, u32[]{:S(2)}, u32[]{:S(2)}) async-start(bf16[64,72,128]{2,1,0:T(8,128)(2,1)} %pack.1), calls=%async_computation | async-start | bytes 2359296 | tf_op jit(solution)/shard_map/all_to_all | solution.py:185
  16.1 0.0 copy-done.1
  16.1 0.9 constant_dynamic-slice_fusion.1
  17.0 2.9 %collective-permute-start = (bf16[128,1024]{1,0:T(8,128)(2,1)}, bf16[128,1024]{1,0:T(8,128)(2,1)S(1)}, u32[]{:S(2)}, u32[]{:S(2)}) collective-permute-start(bf16[128,1024]{1,0:T(8,128)(2,1)} %get-tuple-element.22), channel_id=1, source_target_pairs={{0,128},{128,256},{256,384},{384,0},{1,129},{129,257},{257,385},{3... | collective-permute-start | bytes 786440 | tf_op jit(solution)/shard_map/ppermute | solution.py:172
  19.9 4.5 %collective-permute-start.1 = (bf16[128,1024]{1,0:T(8,128)(2,1)}, bf16[128,1024]{1,0:T(8,128)(2,1)S(1)}, u32[]{:S(2)}, u32[]{:S(2)}) collective-permute-start(bf16[128,1024]{1,0:T(8,128)(2,1)} %get-tuple-element.21), channel_id=1, source_target_pairs={{0,256},{128,384},{256,0},{384,128},{1,257},{129,385},{257,1},{385... | collective-permute-start | bytes 786440 | tf_op jit(solution)/shard_map/ppermute | solution.py:172
  24.4 3.0 %collective-permute-start.2 = (bf16[128,1024]{1,0:T(8,128)(2,1)S(1)}, bf16[128,1024]{1,0:T(8,128)(2,1)S(1)}, u32[]{:S(2)}, u32[]{:S(2)}) collective-permute-start(bf16[128,1024]{1,0:T(8,128)(2,1)S(1)} %get-tuple-element.20), channel_id=1, source_target_pairs={{0,384},{128,0},{256,128},{384,256},{1,385},{129,1},{257,129},{385... | collective-permute-start | bytes 786440 | tf_op jit(solution)/shard_map/ppermute | solution.py:172
  27.5 0.8 dynamic-slice_reduce_fusion
  28.3 0.1 reshape.82
  28.4 0.1 pad_dynamic-slice_fusion.1
  28.4 0.1 reshape.83
  28.6 0.1 convert_reduce_fusion
  28.7 0.1 select_reduce_fusion
  28.8 0.1 pad_dynamic-slice_fusion
  28.9 0.1 concatenate.15
  29.1 0.1 concatenate.14
  29.2 0.1 broadcast_in_dim.18
  29.2 0.1 convert_element_type.32.qlow_ref
  29.3 0.1 broadcast_in_dim.16
  29.4 0.1 convert_element_type.29.qpos_ref
  29.5 5.9 %collective-permute-done = bf16[128,1024]{1,0:T(8,128)(2,1)S(1)} collective-permute-done((bf16[128,1024]{1,0:T(8,128)(2,1)}, bf16[128,1024]{1,0:T(8,128)(2,1)S(1)}, u32[]{:S(2)}, u32[]{:S(2)}) %collective-permute-start) | collective-permute-done | bytes 262176 | tf_op jit(solution)/shard_map/ppermute | solution.py:172
  35.4 7.4 %collective-permute-done.1 = bf16[128,1024]{1,0:T(8,128)(2,1)S(1)} collective-permute-done((bf16[128,1024]{1,0:T(8,128)(2,1)}, bf16[128,1024]{1,0:T(8,128)(2,1)S(1)}, u32[]{:S(2)}, u32[]{:S(2)}) %collective-permute-start.1) | collective-permute-done | bytes 262176 | tf_op jit(solution)/shard_map/ppermute | solution.py:172
  42.9 0.0 collective-permute-done.2
  42.9 4.0 %all-to-all-done.in_ref = bf16[64,72,128]{2,1,0:T(8,128)(2,1)S(1)} async-done(((bf16[64,72,128]{2,1,0:T(8,128)(2,1)}), bf16[64,72,128]{2,1,0:T(8,128)(2,1)S(1)}, u32[]{:S(2)}, u32[]{:S(2)}) %all-to-all-start) | async-done | bytes 1179680 | tf_op jit(solution)/shard_map/all_to_all | solution.py:185
  46.8 6.2 %attend.1 = bf16[64,56,128]{2,1,0:T(8,128)(2,1)} custom-call(bf16[64,72,128]{2,1,0:T(8,128)(2,1)S(1)} %all-to-all-done.in_ref, f32[1,1152]{1,0:T(1,128)S(1)} %add_convert_fusion.kpos_ref, f32[1,1024]{1,0:T(1,128)S(1)} %convert_element_type.29.qpos_ref, f32[1,1024]{1,0:T(1,128)S(1)} %convert_element_type.32.qlow_ref), custom_call_target="tpu_custom_call" | custom-call | tf_op jit(solution)/shard_map/attend/pallas_call | solution.py:199
  53.1 7.4 %all-to-all-start.1 = ((bf16[64,56,128]{2,1,0:T(8,128)(2,1)}), bf16[64,56,128]{2,1,0:T(8,128)(2,1)S(1)}, u32[]{:S(2)}, u32[]{:S(2)}) async-start(bf16[64,56,128]{2,1,0:T(8,128)(2,1)} %attend.1), calls=%async_computation.1 | async-start | bytes 1835008 | tf_op jit(solution)/shard_map/all_to_all | solution.py:214
  60.4 0.1 pad_maximum_fusion
  60.6 3.1 %collective-permute-start.3 = (bf16[4,128,1024]{2,1,0:T(8,128)(2,1)S(1)}, bf16[4,128,1024]{2,1,0:T(8,128)(2,1)S(1)}, u32[]{:S(2)}, u32[]{:S(2)}) collective-permute-start(bf16[4,128,1024]{2,1,0:T(8,128)(2,1)S(1)} %pad_maximum_fusion), channel_id=1, source_target_pairs={{0,1},{1,0},{2,3},{3,2},{4,5},{5,4},{6,7},{7,6},{8,9},{9,8},{10,11... | collective-permute-start | bytes 3145736 | tf_op jit(solution)/shard_map/ppermute | solution.py:215
  63.6 2.3 %collective-permute-done.3 = bf16[4,128,1024]{2,1,0:T(8,128)(2,1)S(1)} collective-permute-done((bf16[4,128,1024]{2,1,0:T(8,128)(2,1)S(1)}, bf16[4,128,1024]{2,1,0:T(8,128)(2,1)S(1)}, u32[]{:S(2)}, u32[]{:S(2)}) %collective-permute-start.3) | collective-permute-done | bytes 1048608 | tf_op jit(solution)/shard_map/ppermute | solution.py:215
  65.9 19.8 %all-to-all-done.1.in_ref = bf16[64,56,128]{2,1,0:T(8,128)(2,1)S(1)} async-done(((bf16[64,56,128]{2,1,0:T(8,128)(2,1)}), bf16[64,56,128]{2,1,0:T(8,128)(2,1)S(1)}, u32[]{:S(2)}, u32[]{:S(2)}) %all-to-all-start.1) | async-done | bytes 917536 | tf_op jit(solution)/shard_map/all_to_all | solution.py:214
  85.7 0.0 copy-start
  85.7 0.9 copy-done
  86.6 2.3 %collect.1 = (bf16[2,64,1024]{2,1,0:T(8,128)(2,1)}, bf16[4,2,128,128]{3,2,1,0:T(8,128)(2,1)}) custom-call(bf16[64,56,128]{2,1,0:T(8,128)(2,1)} %copy-done), custom_call_target="tpu_custom_call" | custom-call | tf_op jit(solution)/shard_map/collect/pallas_call | solution.py:218
  88.9 5.6 %all-to-all-start.2 = ((bf16[8,128,128]{2,1,0:T(8,128)(2,1)}), bf16[8,128,128]{2,1,0:T(8,128)(2,1)S(1)}, u32[]{:S(2)}, u32[]{:S(2)}) async-start(bf16[8,128,128]{2,1,0:T(8,128)(2,1)} %bitcast.54), calls=%async_computation.2 | async-start | bytes 524288 | tf_op jit(solution)/shard_map/all_to_all | solution.py:231
  94.5 6.5 %all-to-all-done.2 = bf16[8,128,128]{2,1,0:T(8,128)(2,1)S(1)} async-done(((bf16[8,128,128]{2,1,0:T(8,128)(2,1)}), bf16[8,128,128]{2,1,0:T(8,128)(2,1)S(1)}, u32[]{:S(2)}, u32[]{:S(2)}) %all-to-all-start.2) | async-done | bytes 262176 | tf_op jit(solution)/shard_map/all_to_all | solution.py:231
  101.0 0.2 fusion.22
  101.3 0.3 fusion.11
  101.5 0.3 fusion.9
  101.8 0.2 fusion.7
  102.1 0.3 fusion.5
  102.3 0.3 fusion.1
  102.6 0.3 fusion.2
  102.8 0.3 fusion.4
  103.1 12.0 %all_to_all.25 = bf16[16,64,128]{2,1,0:T(8,128)(2,1)S(1)} all-to-all(bf16[16,64,128]{2,1,0:T(8,128)(2,1)S(1)} %bitcast.50), channel_id=1, replica_groups=mesh['x'=4,'zl'=4,'y'=4,'zh'=4,'core'=2] {'zl','y'}, dimensions={0} | all-to-all | bytes 524288 | tf_op jit(solution)/shard_map/all_to_all | solution.py:244
  115.1 23.8 %all_to_all.26 = bf16[4,64,128]{2,1,0:T(8,128)(2,1)S(1)} all-to-all(bf16[4,64,128]{2,1,0:T(8,128)(2,1)S(1)} %broadcast_in_dim.30), channel_id=1, replica_groups=mesh['x'=4,'zl'=4,'y'=4,'zh'=4,'core'=2] {'zh'}, dimensions={0} | all-to-all | bytes 131072 | tf_op jit(solution)/shard_map/all_to_all | solution.py:246
  138.9 5.2 %all_gather.3 = f32[64,256]{1,0:T(8,128)S(1)} all-gather(f32[64,128]{1,0:T(8,128)S(1)} %convert_reduce_fusion.1), channel_id=1, replica_groups=mesh['x'=4,'zl'=4,'y'=4,'zh'=4,'core'=2] {'core'}, dimensions={1}, use_global_device_ids=true | all-gather | bytes 98304 | tf_op jit(solution)/shard_map/all_gather | solution.py:248
  144.1 0.6 copy.11
  (6 shorter events, 0.1 us)
Async XLA Ops:
  3.3 12.8 %copy-start.1 = (bf16[2,64,4096]{2,1,0:T(8,128)(2,1)S(1)}, bf16[2,64,4096]{2,1,0:T(8,128)(2,1)}, u32[]{:S(2)}) copy-start(bf16[2,64,4096]{2,1,0:T(8,128)(2,1)} %param.8) | copy-start | bytes 3145732
  3.3 43.5 %all-to-all-start = ((bf16[64,72,128]{2,1,0:T(8,128)(2,1)}), bf16[64,72,128]{2,1,0:T(8,128)(2,1)S(1)}, u32[]{:S(2)}, u32[]{:S(2)}) async-start(bf16[64,72,128]{2,1,0:T(8,128)(2,1)} %pack.1), calls=%async_computation | async-start | bytes 2359296 | tf_op jit(solution)/shard_map/all_to_all | solution.py:185
  17.0 18.4 %collective-permute-start = (bf16[128,1024]{1,0:T(8,128)(2,1)}, bf16[128,1024]{1,0:T(8,128)(2,1)S(1)}, u32[]{:S(2)}, u32[]{:S(2)}) collective-permute-start(bf16[128,1024]{1,0:T(8,128)(2,1)} %get-tuple-element.22), channel_id=1, source_target_pairs={{0,128},{128,256},{256,384},{384,0},{1,129},{129,257},{257,385},{3... | collective-permute-start | bytes 786440 | tf_op jit(solution)/shard_map/ppermute | solution.py:172
  19.9 22.9 %collective-permute-start.1 = (bf16[128,1024]{1,0:T(8,128)(2,1)}, bf16[128,1024]{1,0:T(8,128)(2,1)S(1)}, u32[]{:S(2)}, u32[]{:S(2)}) collective-permute-start(bf16[128,1024]{1,0:T(8,128)(2,1)} %get-tuple-element.21), channel_id=1, source_target_pairs={{0,256},{128,384},{256,0},{384,128},{1,257},{129,385},{257,1},{385... | collective-permute-start | bytes 786440 | tf_op jit(solution)/shard_map/ppermute | solution.py:172
  24.4 18.4 %collective-permute-start.2 = (bf16[128,1024]{1,0:T(8,128)(2,1)S(1)}, bf16[128,1024]{1,0:T(8,128)(2,1)S(1)}, u32[]{:S(2)}, u32[]{:S(2)}) collective-permute-start(bf16[128,1024]{1,0:T(8,128)(2,1)S(1)} %get-tuple-element.20), channel_id=1, source_target_pairs={{0,384},{128,0},{256,128},{384,256},{1,385},{129,1},{257,129},{385... | collective-permute-start | bytes 786440 | tf_op jit(solution)/shard_map/ppermute | solution.py:172
  53.1 32.6 %all-to-all-start.1 = ((bf16[64,56,128]{2,1,0:T(8,128)(2,1)}), bf16[64,56,128]{2,1,0:T(8,128)(2,1)S(1)}, u32[]{:S(2)}, u32[]{:S(2)}) async-start(bf16[64,56,128]{2,1,0:T(8,128)(2,1)} %attend.1), calls=%async_computation.1 | async-start | bytes 1835008 | tf_op jit(solution)/shard_map/all_to_all | solution.py:214
  60.6 5.3 %collective-permute-start.3 = (bf16[4,128,1024]{2,1,0:T(8,128)(2,1)S(1)}, bf16[4,128,1024]{2,1,0:T(8,128)(2,1)S(1)}, u32[]{:S(2)}, u32[]{:S(2)}) collective-permute-start(bf16[4,128,1024]{2,1,0:T(8,128)(2,1)S(1)} %pad_maximum_fusion), channel_id=1, source_target_pairs={{0,1},{1,0},{2,3},{3,2},{4,5},{5,4},{6,7},{7,6},{8,9},{9,8},{10,11... | collective-permute-start | bytes 3145736 | tf_op jit(solution)/shard_map/ppermute | solution.py:215
  85.7 0.9 copy-start
  88.9 12.1 %all-to-all-start.2 = ((bf16[8,128,128]{2,1,0:T(8,128)(2,1)}), bf16[8,128,128]{2,1,0:T(8,128)(2,1)S(1)}, u32[]{:S(2)}, u32[]{:S(2)}) async-start(bf16[8,128,128]{2,1,0:T(8,128)(2,1)} %bitcast.54), calls=%async_computation.2 | async-start | bytes 524288 | tf_op jit(solution)/shard_map/all_to_all | solution.py:231

commit v5 on v4

v5 whole, which is shorter than its diff:
```python
import math

import jax
import jax.numpy as jnp
from jax import lax
from jax.experimental import pallas as pl
from jax.experimental.pallas import tpu as pltpu
from jax.sharding import Mesh
from jax.sharding import PartitionSpec as P

BF = jnp.bfloat16
F32 = jnp.float32
HEADS = 8
HD = 128
ROWS = 64
PEERS = 32
OWN = 4
GROUPS = ROWS // OWN
HALO = 16
SEND = 152
BACK = 112
TOKENS = PEERS * OWN
QN = TOKENS * HEADS
KH = PEERS * HALO
KN = 2 * KH + 2 * TOKENS
NEG = -1e30
FAR = 1 << 20
SCALE = 1.0 / math.sqrt(HD)
LOG2E = math.log2(math.e)


def iota(shape, dim):
    return lax.broadcasted_iota(jnp.int32, shape, dim)


def one_hot(condition):
    return jnp.where(condition, 1.0, 0.0).astype(BF)


def dot(a, b):
    return lax.dot_general(a, b, (((1,), (0,)), ((), ())), preferred_element_type=F32)


def dot_t(a, b):
    return lax.dot_general(a, b, (((1,), (1,)), ((), ())), preferred_element_type=F32)


def window_rows(keys, values):
    target, row = iota((GROUPS * HALO, ROWS), 0), iota((GROUPS * HALO, ROWS), 1)
    window = one_hot(row == OWN * (target // HALO) + target % HALO - HALO)
    target, row = iota((GROUPS * 8, ROWS), 0), iota((GROUPS * 8, ROWS), 1)
    here = row == OWN * (target // 8) + target % OWN
    own = dot(one_hot(here & (target % 8 < OWN)), keys)
    own = own + dot(one_hot(here & (target % 8 >= OWN)), values)
    return (
        dot(window, keys).reshape(GROUPS, HALO, HD).astype(BF),
        dot(window, values).reshape(GROUPS, HALO, HD).astype(BF),
        own.reshape(GROUPS, 8, HD).astype(BF),
    )


def pack_kernel(q_ref, g_ref, o_ref, k_ref, v_ref, out_ref, split):
    def heads_to_rows(ref, at):
        wide = ref[0].astype(F32)
        for h in range(HEADS):
            split[pl.ds(h, ROWS, stride=HEADS), :] = wide[:, h * HD : (h + 1) * HD]
        out_ref[:, at : at + 32, :] = split[...].reshape(GROUPS, 32, HD).astype(BF)

    heads_to_rows(q_ref, 0)
    heads_to_rows(g_ref, 32)
    product = g_ref[0].astype(F32) * o_ref[0].astype(F32)
    lane = iota((ROWS, HD), 1)
    delta = jnp.zeros((ROWS, HD), F32)
    for h in range(HEADS):
        total = jnp.sum(product[:, h * HD : (h + 1) * HD], axis=1, keepdims=True)
        delta = jnp.where(lane % HEADS == h, total, delta)
    high = delta.astype(BF).astype(F32)
    rest = delta - high
    middle = rest.astype(BF).astype(F32)
    low = rest - middle
    pieces = jnp.where(lane < 8, high, jnp.where(lane < 16, middle, low))
    pieces = jnp.where(lane < 24, -pieces, 0.0).astype(BF)
    out_ref[:, 64:80, :], out_ref[:, 80:96, :], out_ref[:, 96:104, :] = window_rows(
        k_ref[0], v_ref[0]
    )
    target, row = iota((GROUPS * 8, ROWS), 0), iota((GROUPS * 8, ROWS), 1)
    here = (row == OWN * (target // 8) + target % OWN) & (target % 8 < OWN)
    out_ref[:, 104:112, :] = dot(one_hot(here), pieces).reshape(GROUPS, 8, HD).astype(BF)


def pack_other_kernel(kv_ref, in_ref, out_ref, block, sem):
    for s in range(2):
        to = slice(s * GROUPS, (s + 1) * GROUPS)
        block[to, 0:16, :], block[to, 16:32, :], block[to, 32:40, :] = window_rows(
            kv_ref[s, :, 0:HD], kv_ref[s, :, HD : 2 * HD]
        )
    copy = pltpu.make_async_copy(block, out_ref.at[:, 112:152, :], sem)
    copy.start()
    copy.wait()


def attend_kernel(in_ref, kpos_ref, qpos_ref, qlow_ref, out_ref, keys, values, dkey, dvalue):
    token, source = iota((TOKENS, PEERS * 8), 0), iota((TOKENS, PEERS * 8), 1)
    home = token // OWN * 8 + token % OWN

    def picked(row, offset):
        extra = in_ref[:, row : row + 8, :].astype(F32).reshape(PEERS * 8, HD).astype(BF)
        return dot(one_hot(source == home + offset), extra).astype(BF)

    for half, (halo, own) in enumerate(((64, 96), (112, 144))):
        to = slice(half * KH, (half + 1) * KH)
        keys[to, :] = in_ref[:, halo : halo + 16, :].reshape(KH, HD)
        values[to, 0:HD] = in_ref[:, halo + 16 : halo + 32, :].reshape(KH, HD)
        to = slice(2 * KH + half * TOKENS, 2 * KH + (half + 1) * TOKENS)
        keys[to, :] = picked(own, 0)
        values[to, 0:HD] = picked(own, OWN)
    values[:, HD : 2 * HD] = one_hot(iota((KN, HD), 1) < 24)
    delta = picked(104, 0)
    kpos = jnp.broadcast_to(kpos_ref[...], (HD, KN)).T
    kpos = jnp.concatenate([kpos, kpos], axis=1)
    key_columns = keys[...].astype(F32).T.astype(BF)
    count = 256
    srcs = count // (OWN * HEADS)
    for c in range(QN // count):
        first = c * srcs
        qc = in_ref[first : first + srcs, 0:32, :].reshape(count, HD)
        gc = in_ref[first : first + srcs, 32:64, :].reshape(count, HD)
        row, col = iota((count, HD), 0), iota((count, HD), 1)
        spread = dot(one_hot(col == c * (count // HEADS) + row // HEADS), delta)
        spread = jnp.where(col % HEADS == row % HEADS, spread, 0.0).astype(BF)
        scores = dot_t(keys[...], qc)
        at = slice(c * count, (c + 1) * count)
        scores = jnp.where((kpos <= qpos_ref[:, at]) & (kpos >= qlow_ref[:, at]), scores, NEG)
        top = jnp.max(scores, axis=0, keepdims=True)
        probs = jnp.exp2((scores - top) * (SCALE * LOG2E))
        probs = probs * (1.0 / jnp.sum(probs, axis=0, keepdims=True))
        change = dot_t(values[...], jnp.concatenate([gc, spread], axis=1))
        sgrad = (probs * change).astype(BF)
        value_part = dot(probs.astype(BF), gc)
        key_part = dot(sgrad, qc)
        if c == 0:
            dvalue[...] = value_part
            dkey[...] = key_part
        else:
            dvalue[...] += value_part
            dkey[...] += key_part
        qgrad = (dot(key_columns, sgrad) * SCALE).T
        out_ref[first : first + srcs, 0:32, :] = qgrad.reshape(srcs, 32, HD).astype(BF)
    source, token = iota((PEERS * 8, TOKENS), 0), iota((PEERS * 8, TOKENS), 1)
    home = token // OWN * 8 + token % OWN
    for half in range(2):
        at = slice(half * KH, (half + 1) * KH)
        halo = 32 + 32 * half
        out_ref[:, halo : halo + 16, :] = (dkey[at, :] * SCALE).reshape(PEERS, HALO, HD).astype(BF)
        out_ref[:, halo + 16 : halo + 32, :] = dvalue[at, :].reshape(PEERS, HALO, HD).astype(BF)
        at = slice(2 * KH + half * TOKENS, 2 * KH + (half + 1) * TOKENS)
        own = dot(one_hot(source == home), (dkey[at, :] * SCALE).astype(BF))
        own = own + dot(one_hot(source == home + OWN), dvalue[at, :].astype(BF))
        own = own.reshape(PEERS, 8, HD).astype(BF)
        out_ref[:, 96 + 8 * half : 104 + 8 * half, :] = own


def collect_kernel(half_ref, in_ref, q_ref, kv_ref, split):
    row, source = iota((ROWS, GROUPS * HALO), 0), iota((ROWS, GROUPS * HALO), 1)
    window = one_hot(row == OWN * (source // HALO) + source % HALO - HALO)
    row, source = iota((ROWS, GROUPS * 8), 0), iota((ROWS, GROUPS * 8), 1)
    here = row == OWN * (source // 8) + source % OWN
    for s in range(2):
        mine = slice(s * GROUPS, (s + 1) * GROUPS)
        for half in range(2):
            slot = half_ref[0] if half == 0 else 1 - half_ref[0]
            extra = in_ref[mine, 96 + 8 * half : 104 + 8 * half, :]
            extra = extra.astype(F32).reshape(GROUPS * 8, HD).astype(BF)
            for part in range(2):
                at = 32 + 32 * half + 16 * part
                halo = in_ref[mine, at : at + 16, :].reshape(GROUPS * HALO, HD)
                total = dot(window, halo)
                total = total + dot(one_hot(here & (source % 8 // OWN == part)), extra)
                for copy in range(4):
                    kv_ref[copy, slot, part, s * ROWS : (s + 1) * ROWS] = total.astype(BF)
        split[...] = in_ref[mine, 0:32, :].astype(F32).reshape(GROUPS * 32, HD)
        for h in range(HEADS):
            q_ref[s, :, h * HD : (h + 1) * HD] = split[pl.ds(h, ROWS, stride=HEADS), :].astype(BF)


def whole(shape):
    return pl.BlockSpec(shape, lambda *_: (0,) * len(shape))


def local(
    layer_input, queries, key_states, value_states, attn_output, out_grad, doc_ids, positions
):
    peers = ("x", "zd", "y")
    index = lax.axis_index(peers)
    half = lax.axis_index("zu")
    sequence, group = index // GROUPS, index % GROUPS

    quarter = layer_input.shape[2] // 4
    x_at, core = lax.axis_index("x"), lax.axis_index("core")
    flat_input = layer_input.reshape(2 * ROWS, 4 * quarter)
    columns = []
    for step in range(4):
        piece = lax.dynamic_slice_in_dim(flat_input, (x_at + step) % 4 * quarter, quarter, 1)
        if step:
            piece = lax.ppermute(piece, "x", [(i, (i + step) % 4) for i in range(4)])
        columns.append(piece)

    row_spec = lambda width: pl.BlockSpec((1, ROWS, width), lambda s: (s, 0, 0))
    other = lax.ppermute(
        jnp.concatenate([key_states, value_states], axis=2), "zu", [(0, 1), (1, 0)]
    )
    sent = pl.pallas_call(
        pack_kernel,
        out_shape=jax.ShapeDtypeStruct((PEERS, SEND, HD), BF),
        grid=(2,),
        in_specs=[row_spec(1024), row_spec(1024), row_spec(1024), row_spec(HD), row_spec(HD)],
        out_specs=pl.BlockSpec((GROUPS, SEND, HD), lambda s: (s, 0, 0)),
        scratch_shapes=[pltpu.VMEM((ROWS * HEADS, HD), F32)],
        name="pack",
    )(queries, out_grad, attn_output, key_states, value_states)
    hbm = pl.BlockSpec(memory_space=pltpu.HBM)
    sent = pl.pallas_call(
        pack_other_kernel,
        out_shape=jax.ShapeDtypeStruct((PEERS, SEND, HD), BF),
        in_specs=[whole((2, ROWS, 2 * HD)), hbm],
        out_specs=hbm,
        scratch_shapes=[pltpu.VMEM((PEERS, 40, HD), BF), pltpu.SemaphoreType.DMA(())],
        input_output_aliases={1: 0},
        grid=(1,),
        compiler_params=pltpu.CompilerParams(vmem_limit_bytes=32 << 20),
        name="pack_other",
    )(other, sent)
    arrived = lax.all_to_all(sent, peers, 0, 0, tiled=True)
    arrived, *columns = lax.optimization_barrier((arrived, *columns))

    docs = lax.dynamic_index_in_dim(doc_ids, sequence, 0, keepdims=False)
    places = lax.dynamic_index_in_dim(positions, sequence, 0, keepdims=False)
    places = places.reshape(4, 2, 8, ROWS)
    places = jnp.pad(places, ((0, 0), (0, 0), (0, 0), (HALO, 0)), constant_values=FAR)
    places = lax.dynamic_slice_in_dim(places, OWN * group, HALO + OWN, 3)
    near = lax.dynamic_index_in_dim(places, half, 1, keepdims=False)
    far = lax.dynamic_index_in_dim(places, 1 - half, 1, keepdims=False)
    own = near[:, :, HALO:].reshape(TOKENS)
    kpos = [near[:, :, :HALO].reshape(KH), far[:, :, :HALO].reshape(KH)]
    kpos = jnp.concatenate(kpos + [own, far[:, :, HALO:].reshape(TOKENS)])[None, :]
    starts = jnp.sum(docs[None, :] < jnp.arange(16)[:, None], axis=1)
    low = jnp.max(jnp.where(starts[:, None] <= own[None, :], starts[:, None], 0), axis=0)
    qpos = jnp.repeat(own, HEADS)[None, :]
    qlow = jnp.repeat(low, HEADS)[None, :]

    back = pl.pallas_call(
        attend_kernel,
        out_shape=jax.ShapeDtypeStruct((PEERS, BACK, HD), BF),
        grid=(1,),
        in_specs=[whole((PEERS, SEND, HD)), whole((1, KN)), whole((1, QN)), whole((1, QN))],
        out_specs=whole((PEERS, BACK, HD)),
        scratch_shapes=[
            pltpu.VMEM((KN, HD), BF),
            pltpu.VMEM((KN, 2 * HD), BF),
            pltpu.VMEM((KN, HD), F32),
            pltpu.VMEM((KN, HD), F32),
        ],
        compiler_params=pltpu.CompilerParams(vmem_limit_bytes=48 << 20),
        name="attend",
    )(arrived, kpos.astype(F32), qpos.astype(F32), qlow.astype(F32))
    home = lax.all_to_all(back, peers, 0, 0, tiled=True)
    twin = lax.ppermute(jnp.stack(columns), "core", [(0, 1), (1, 0)])
    home, twin = lax.optimization_barrier((home, twin))

    query_grad, kv_grad = pl.pallas_call(
        collect_kernel,
        out_shape=(
            jax.ShapeDtypeStruct((2, ROWS, HEADS * HD), BF),
            jax.ShapeDtypeStruct((4, 2, 2, 2 * ROWS, HD), BF),
        ),
        grid=(1,),
        in_specs=[pl.BlockSpec(memory_space=pltpu.SMEM), whole((PEERS, BACK, HD))],
        out_specs=(whole((2, ROWS, HEADS * HD)), whole((4, 2, 2, 2 * ROWS, HD))),
        scratch_shapes=[pltpu.VMEM((GROUPS * 32, HD), F32)],
        compiler_params=pltpu.CompilerParams(vmem_limit_bytes=32 << 20),
        name="collect",
    )(half[None], home)

    grads = lax.all_to_all(
        kv_grad.reshape(16, 2 * ROWS, HD), ("x", "zu", "core"), 0, 0, tiled=True
    )
    grads = jnp.sum(grads.reshape(4, 2, 2, 2 * ROWS, HD).astype(F32), axis=1).astype(BF)
    grads = grads.reshape(8, 2 * ROWS, HD)
    part = jnp.zeros((quarter, HD), F32)
    for step in range(4):
        for piece, at in ((columns[step], core), (twin[step], 1 - core)):
            grad = lax.dynamic_index_in_dim(
                grads, (x_at - step) % 4 * 2 + at, 0, keepdims=False
            )
            part = part + lax.dot_general(
                piece, grad, (((0,), (0,)), ((), ())), preferred_element_type=F32
            )
    part = part.reshape(16, 64, HD).astype(BF)
    part = lax.all_to_all(part, ("zu", "zd", "y"), 0, 0, tiled=True)
    part = jnp.sum(part.astype(F32), axis=0).astype(BF)
    part = lax.all_to_all(jnp.broadcast_to(part[None], (4, 64, HD)), "zh", 0, 0, tiled=True)
    part = jnp.sum(part.astype(F32), axis=0)
    weight_grad = lax.all_gather(part, "core", axis=1, tiled=True)
    return (query_grad, weight_grad)


def solution(mesh):
    devices = mesh.devices.reshape(4, 2, 2, 4, -1, 2)
    inner = Mesh(devices, ("x", "zu", "zd", "y", "zh", "core"))
    ctx, dp = ("x", "zu", "zd", "y"), ("zh", "core")
    rows = P(dp, ctx, None)
    whole_rows = P(dp, None)
    return jax.shard_map(
        local,
        mesh=inner,
        in_specs=(rows,) * 6 + (whole_rows,) * 2,
        out_specs=(rows, P(ctx, None)),
        check_vma=False,
    )
```

time: 145 us -> 145 us (level)
  waiting for transfers between devices: 45.8 us -> 41 us
  starting transfers between devices: 39.1 us -> 42.9 us
    ppermute x0 -> x1, starting transfers between devices: none -> 5.73 us  [local(): lax.ppermute(jnp.concatenate([key_states, value_states], axis=2), 'zu', [...]
    all_to_all x3, waiting for transfers between devices: 30.2 us -> 24.7 us  [the longest x1 16.4 us: local(): lax.all_to_all(kv_grad.reshape(16, 2 * ROWS, HD), ('x', 'zu', 'core'), 0,...]
    all_to_all x3, starting transfers between devices: 25.7 us -> 23.5 us  [the longest x1 8.53 us: local(): arrived = lax.all_to_all(sent, peers, 0, 0, tiled=True)]
    unnamed x5 -> x11, local copies, waits for them, and re-layouts: 1.56 us -> 2.97 us
    pallas_call x2 -> x3, Pallas kernels: 8.93 us -> 9.47 us  [the longest x1 6.59 us: local(): pl.pallas_call(attend_kernel, out_shape=jax.ShapeDtypeStruct((PEERS, BACK...]
  transfers between devices with their start and end apart: 7 -> 8, of which waited for: 6 -> 5; matrix products, arithmetic and copies ran while one was open for 2% -> 2% of each run, Pallas kernels for 0% -> 2%
where the time goes in v5:
time: 145 us; the launch traced here: 144 us
  starting transfers between devices  42.9 us (30%)
  waiting for transfers between devices  41 us (28%)
  blocking collectives  40.4 us (28%)
  Pallas kernels  10.7 us (7%)
  local copies, waits for them, and re-layouts  5.11 us (4%)
  matrix products  2.05 us (1%)
    all_to_all x1, blocking collectives, local(): lax.all_to_all(jnp.broadcast_to(part[None], (4, 64, HD)), 'zh', 0, 0, til...  22.7 us
    all_to_all x1, waiting for transfers between devices, local(): lax.all_to_all(kv_grad.reshape(16, 2 * ROWS, HD), ('x', 'zu', 'core'), 0,...  16.4 us
    ppermute x3, waiting for transfers between devices, local(): piece = lax.ppermute(piece, 'x', [(i, (i + step) % 4) for i in range(4)])  14 us
    all_to_all x1, blocking collectives, local(): part = lax.all_to_all(part, ('zu', 'zd', 'y'), 0, 0, tiled=True)  12.7 us
    ppermute x3, starting transfers between devices, local(): piece = lax.ppermute(piece, 'x', [(i, (i + step) % 4) for i in range(4)])  10.5 us
    all_to_all x1, starting transfers between devices, local(): arrived = lax.all_to_all(sent, peers, 0, 0, tiled=True)  8.53 us
    all_to_all x1, waiting for transfers between devices, local(): home = lax.all_to_all(back, peers, 0, 0, tiled=True)  8.25 us
    all_to_all x1, starting transfers between devices, local(): lax.all_to_all(kv_grad.reshape(16, 2 * ROWS, HD), ('x', 'zu', 'core'), 0,...  8.09 us
  transfers between devices with their start and end apart: 8, of which 5 were waited for; matrix products, arithmetic and copies ran while one was open for 2% of the time, Pallas kernels for 2%

profile of v5, /device:TPU:1, one launch (start us, length us, event | category | flops | bytes accessed | tf_op | source)
XLA Modules:
  0.0 144.3 jit_solution(17405558056915612969)
XLA Ops:
  0.6 0.8 pad_maximum_fusion.1
  1.4 5.7 %collective-permute-start = (bf16[2,64,256]{2,1,0:T(8,128)(2,1)S(1)}, bf16[2,64,256]{2,1,0:T(8,128)(2,1)S(1)}, u32[]{:S(2)}, u32[]{:S(2)}) collective-permute-start(bf16[2,64,256]{2,1,0:T(8,128)(2,1)S(1)} %pad_maximum_fusion.1), channel_id=1, source_target_pairs={{0,64},{64,0},{1,65},{65,1},{2,66},{66,2},{3,67},{67,3},{4,68},{68... | collective-permute-start | bytes 196616 | tf_op jit(solution)/shard_map/ppermute | solution.py:209
  7.2 2.6 %pack.1.in_ref = bf16[32,152,128]{2,1,0:T(8,128)(2,1)} custom-call(bf16[2,64,1024]{2,1,0:T(8,128)(2,1)} %q_ref.1, bf16[2,64,1024]{2,1,0:T(8,128)(2,1)} %g_ref.1, bf16[2,64,1024]{2,1,0:T(8,128)(2,1)} %o_ref.1, bf16[2,64,128]{2,1,0:T(8,128)(2,1)} %k_ref.1, bf16[2,64,128]{2,1,0:T(8,128)(2,1)} %v_ref.1), custom_call_target="tpu_custom_call" | custom-call | tf_op jit(solution)/shard_map/pack/pallas_call | solution.py:212
  9.8 1.3 copy-done
  11.0 0.3 pack_other.1
  11.4 1.0 copy-done.1
  12.4 8.5 %all-to-all-start = ((bf16[32,152,128]{2,1,0:T(8,128)(2,1)}), bf16[32,152,128]{2,1,0:T(8,128)(2,1)S(1)}, u32[]{:S(2)}, u32[]{:S(2)}) async-start(bf16[32,152,128]{2,1,0:T(8,128)(2,1)} %copy-done.1), calls=%async_computation | async-start | bytes 2490368 | tf_op jit(solution)/shard_map/all_to_all | solution.py:233
  21.0 0.9 constant_dynamic-slice_fusion.1
  21.9 3.1 %collective-permute-start.1 = (bf16[128,1024]{1,0:T(8,128)(2,1)}, bf16[128,1024]{1,0:T(8,128)(2,1)S(1)}, u32[]{:S(2)}, u32[]{:S(2)}) collective-permute-start(bf16[128,1024]{1,0:T(8,128)(2,1)} %get-tuple-element.22), channel_id=1, source_target_pairs={{0,128},{128,256},{256,384},{384,0},{1,129},{129,257},{257,385},{3... | collective-permute-start | bytes 786440 | tf_op jit(solution)/shard_map/ppermute | solution.py:205
  25.1 4.3 %collective-permute-start.2 = (bf16[128,1024]{1,0:T(8,128)(2,1)}, bf16[128,1024]{1,0:T(8,128)(2,1)S(1)}, u32[]{:S(2)}, u32[]{:S(2)}) collective-permute-start(bf16[128,1024]{1,0:T(8,128)(2,1)} %get-tuple-element.21), channel_id=1, source_target_pairs={{0,256},{128,384},{256,0},{384,128},{1,257},{129,385},{257,1},{385... | collective-permute-start | bytes 786440 | tf_op jit(solution)/shard_map/ppermute | solution.py:205
  29.4 3.1 %collective-permute-start.3 = (bf16[128,1024]{1,0:T(8,128)(2,1)}, bf16[128,1024]{1,0:T(8,128)(2,1)S(1)}, u32[]{:S(2)}, u32[]{:S(2)}) collective-permute-start(bf16[128,1024]{1,0:T(8,128)(2,1)} %get-tuple-element.20), channel_id=1, source_target_pairs={{0,384},{128,0},{256,128},{384,256},{1,385},{129,1},{257,129},{385... | collective-permute-start | bytes 786440 | tf_op jit(solution)/shard_map/ppermute | solution.py:205
  32.7 0.1 fusion.34
  32.8 0.1 slice.34
  32.8 0.1 reshape.119
  33.0 0.1 convert_reduce_fusion
  33.1 0.1 select_reduce_fusion
  33.2 0.1 concatenate.24
  33.4 0.1 concatenate.25
  33.5 0.1 concatenate.22
  33.6 0.1 concatenate.23
  33.7 0.1 broadcast_in_dim.33
  33.7 0.1 convert_element_type.34.qlow_ref
  33.9 0.1 broadcast_in_dim.19
  33.9 0.1 convert_element_type.31.qpos_ref
  34.1 8.9 %collective-permute-done.1 = bf16[128,1024]{1,0:T(8,128)(2,1)S(1)} collective-permute-done((bf16[128,1024]{1,0:T(8,128)(2,1)}, bf16[128,1024]{1,0:T(8,128)(2,1)S(1)}, u32[]{:S(2)}, u32[]{:S(2)}) %collective-permute-start.1) | collective-permute-done | bytes 262176 | tf_op jit(solution)/shard_map/ppermute | solution.py:205
  43.0 5.1 %collective-permute-done.2 = bf16[128,1024]{1,0:T(8,128)(2,1)S(1)} collective-permute-done((bf16[128,1024]{1,0:T(8,128)(2,1)}, bf16[128,1024]{1,0:T(8,128)(2,1)S(1)}, u32[]{:S(2)}, u32[]{:S(2)}) %collective-permute-start.2) | collective-permute-done | bytes 262176 | tf_op jit(solution)/shard_map/ppermute | solution.py:205
  48.1 6.6 %attend.1 = bf16[32,112,128]{2,1,0:T(8,128)(2,1)} custom-call(bf16[32,152,128]{2,1,0:T(8,128)(2,1)S(1)} %all-to-all-done.in_ref, f32[1,1280]{1,0:T(1,128)S(1)} %add_convert_fusion.kpos_ref, f32[1,1024]{1,0:T(1,128)S(1)} %convert_element_type.31.qpos_ref, f32[1,1024]{1,0:T(1,128)S(1)} %convert_element_type.34.qlow_ref), custom_call_target="tpu_custom_call" | custom-call | tf_op jit(solution)/shard_map/attend/pallas_call | solution.py:251
  54.7 6.9 %all-to-all-start.1 = ((bf16[32,112,128]{2,1,0:T(8,128)(2,1)}), bf16[32,112,128]{2,1,0:T(8,128)(2,1)S(1)}, u32[]{:S(2)}, u32[]{:S(2)}) async-start(bf16[32,112,128]{2,1,0:T(8,128)(2,1)} %attend.1), calls=%async_computation.1 | async-start | bytes 1835008 | tf_op jit(solution)/shard_map/all_to_all | solution.py:266
  61.6 0.1 pad_maximum_fusion
  61.7 3.1 %collective-permute-start.4 = (bf16[4,128,1024]{2,1,0:T(8,128)(2,1)S(1)}, bf16[4,128,1024]{2,1,0:T(8,128)(2,1)S(1)}, u32[]{:S(2)}, u32[]{:S(2)}) collective-permute-start(bf16[4,128,1024]{2,1,0:T(8,128)(2,1)S(1)} %pad_maximum_fusion), channel_id=1, source_target_pairs={{0,1},{1,0},{2,3},{3,2},{4,5},{5,4},{6,7},{7,6},{8,9},{9,8},{10,11... | collective-permute-start | bytes 3145736 | tf_op jit(solution)/shard_map/ppermute | solution.py:267
  64.8 2.3 %collective-permute-done.4 = bf16[4,128,1024]{2,1,0:T(8,128)(2,1)S(1)} collective-permute-done((bf16[4,128,1024]{2,1,0:T(8,128)(2,1)S(1)}, bf16[4,128,1024]{2,1,0:T(8,128)(2,1)S(1)}, u32[]{:S(2)}, u32[]{:S(2)}) %collective-permute-start.4) | collective-permute-done | bytes 1048608 | tf_op jit(solution)/shard_map/ppermute | solution.py:267
  67.1 8.2 %all-to-all-done.1.in_ref = bf16[32,112,128]{2,1,0:T(8,128)(2,1)S(1)} async-done(((bf16[32,112,128]{2,1,0:T(8,128)(2,1)}), bf16[32,112,128]{2,1,0:T(8,128)(2,1)S(1)}, u32[]{:S(2)}, u32[]{:S(2)}) %all-to-all-start.1) | async-done | bytes 917536 | tf_op jit(solution)/shard_map/all_to_all | solution.py:266
  75.3 1.2 collect.1
  76.6 8.1 %all-to-all-start.2 = ((bf16[16,128,128]{2,1,0:T(8,128)(2,1)}), bf16[16,128,128]{2,1,0:T(8,128)(2,1)S(1)}, u32[]{:S(2)}, u32[]{:S(2)}) async-start(bf16[16,128,128]{2,1,0:T(8,128)(2,1)} %bitcast.9), calls=%async_computation.2 | async-start | bytes 1048576 | tf_op jit(solution)/shard_map/all_to_all | solution.py:284
  84.7 16.4 %all-to-all-done.2 = bf16[16,128,128]{2,1,0:T(8,128)(2,1)S(1)} async-done(((bf16[16,128,128]{2,1,0:T(8,128)(2,1)}), bf16[16,128,128]{2,1,0:T(8,128)(2,1)S(1)}, u32[]{:S(2)}, u32[]{:S(2)}) %all-to-all-start.2) | async-done | bytes 524320 | tf_op jit(solution)/shard_map/all_to_all | solution.py:284
  101.1 0.1 reduce_sum.43
  101.2 0.3 fusion.22
  101.4 0.3 fusion.11
  101.7 0.3 fusion.9
  101.9 0.3 fusion.7
  102.2 0.2 fusion.5
  102.5 0.3 fusion.1
  102.7 0.3 fusion.2
  103.0 0.3 fusion.4
  103.3 12.7 %all_to_all.25 = bf16[16,64,128]{2,1,0:T(8,128)(2,1)S(1)} all-to-all(bf16[16,64,128]{2,1,0:T(8,128)(2,1)S(1)} %bitcast.68), channel_id=1, replica_groups=mesh['x'=4,'zu'=2,'zd'=2,'y'=4,'zh'=4,'core'=2] {'zu','zd','y'}, dimensions={0} | all-to-all | bytes 524288 | tf_op jit(solution)/shard_map/all_to_all | solution.py:299
  116.0 22.7 %all_to_all.26 = bf16[4,64,128]{2,1,0:T(8,128)(2,1)S(1)} all-to-all(bf16[4,64,128]{2,1,0:T(8,128)(2,1)S(1)} %broadcast_in_dim.34), channel_id=1, replica_groups=mesh['x'=4,'zu'=2,'zd'=2,'y'=4,'zh'=4,'core'=2] {'zh'}, dimensions={0} | all-to-all | bytes 131072 | tf_op jit(solution)/shard_map/all_to_all | solution.py:301
  138.7 5.0 %all_gather.3 = f32[64,256]{1,0:T(8,128)S(1)} all-gather(f32[64,128]{1,0:T(8,128)S(1)} %convert_reduce_fusion.1), channel_id=1, replica_groups=mesh['x'=4,'zu'=2,'zd'=2,'y'=4,'zh'=4,'core'=2] {'core'}, dimensions={1}, use_global_device_ids=true | all-gather | bytes 98304 | tf_op jit(solution)/shard_map/all_gather | solution.py:303
  143.7 0.6 copy.13
  (20 shorter events, 0.3 us)
Async XLA Ops:
  1.4 8.3 %collective-permute-start = (bf16[2,64,256]{2,1,0:T(8,128)(2,1)S(1)}, bf16[2,64,256]{2,1,0:T(8,128)(2,1)S(1)}, u32[]{:S(2)}, u32[]{:S(2)}) collective-permute-start(bf16[2,64,256]{2,1,0:T(8,128)(2,1)S(1)} %pad_maximum_fusion.1), channel_id=1, source_target_pairs={{0,64},{64,0},{1,65},{65,1},{2,66},{66,2},{3,67},{67,3},{4,68},{68... | collective-permute-start | bytes 196616 | tf_op jit(solution)/shard_map/ppermute | solution.py:209
  9.7 1.3 copy-start
  11.3 1.0 copy-start.1
  12.4 8.6 %copy-start.2 = (bf16[2,64,4096]{2,1,0:T(8,128)(2,1)S(1)}, bf16[2,64,4096]{2,1,0:T(8,128)(2,1)}, u32[]{:S(2)}) copy-start(bf16[2,64,4096]{2,1,0:T(8,128)(2,1)} %param.8) | copy-start | bytes 3145732
  12.4 35.7 %all-to-all-start = ((bf16[32,152,128]{2,1,0:T(8,128)(2,1)}), bf16[32,152,128]{2,1,0:T(8,128)(2,1)S(1)}, u32[]{:S(2)}, u32[]{:S(2)}) async-start(bf16[32,152,128]{2,1,0:T(8,128)(2,1)} %copy-done.1), calls=%async_computation | async-start | bytes 2490368 | tf_op jit(solution)/shard_map/all_to_all | solution.py:233
  20.9 11.6 %copy-start.3 = (s32[2,4096]{1,0:T(2,128)S(1)}, s32[2,4096]{1,0:T(2,128)}, u32[]{:S(2)}) copy-start(s32[2,4096]{1,0:T(2,128)} %param.15) | copy-start | bytes 98308
  20.9 11.6 %copy-start.4 = (s32[2,4096]{1,0:T(2,128)S(1)}, s32[2,4096]{1,0:T(2,128)}, u32[]{:S(2)}) copy-start(s32[2,4096]{1,0:T(2,128)} %param.14) | copy-start | bytes 98308
  21.9 21.0 %collective-permute-start.1 = (bf16[128,1024]{1,0:T(8,128)(2,1)}, bf16[128,1024]{1,0:T(8,128)(2,1)S(1)}, u32[]{:S(2)}, u32[]{:S(2)}) collective-permute-start(bf16[128,1024]{1,0:T(8,128)(2,1)} %get-tuple-element.22), channel_id=1, source_target_pairs={{0,128},{128,256},{256,384},{384,0},{1,129},{129,257},{257,385},{3... | collective-permute-start | bytes 786440 | tf_op jit(solution)/shard_map/ppermute | solution.py:205
  25.1 23.0 %collective-permute-start.2 = (bf16[128,1024]{1,0:T(8,128)(2,1)}, bf16[128,1024]{1,0:T(8,128)(2,1)S(1)}, u32[]{:S(2)}, u32[]{:S(2)}) collective-permute-start(bf16[128,1024]{1,0:T(8,128)(2,1)} %get-tuple-element.21), channel_id=1, source_target_pairs={{0,256},{128,384},{256,0},{384,128},{1,257},{129,385},{257,1},{385... | collective-permute-start | bytes 786440 | tf_op jit(solution)/shard_map/ppermute | solution.py:205
  29.4 18.7 %collective-permute-start.3 = (bf16[128,1024]{1,0:T(8,128)(2,1)}, bf16[128,1024]{1,0:T(8,128)(2,1)S(1)}, u32[]{:S(2)}, u32[]{:S(2)}) collective-permute-start(bf16[128,1024]{1,0:T(8,128)(2,1)} %get-tuple-element.20), channel_id=1, source_target_pairs={{0,384},{128,0},{256,128},{384,256},{1,385},{129,1},{257,129},{385... | collective-permute-start | bytes 786440 | tf_op jit(solution)/shard_map/ppermute | solution.py:205
  54.7 20.7 %all-to-all-start.1 = ((bf16[32,112,128]{2,1,0:T(8,128)(2,1)}), bf16[32,112,128]{2,1,0:T(8,128)(2,1)S(1)}, u32[]{:S(2)}, u32[]{:S(2)}) async-start(bf16[32,112,128]{2,1,0:T(8,128)(2,1)} %attend.1), calls=%async_computation.1 | async-start | bytes 1835008 | tf_op jit(solution)/shard_map/all_to_all | solution.py:266
  61.7 5.4 %collective-permute-start.4 = (bf16[4,128,1024]{2,1,0:T(8,128)(2,1)S(1)}, bf16[4,128,1024]{2,1,0:T(8,128)(2,1)S(1)}, u32[]{:S(2)}, u32[]{:S(2)}) collective-permute-start(bf16[4,128,1024]{2,1,0:T(8,128)(2,1)S(1)} %pad_maximum_fusion), channel_id=1, source_target_pairs={{0,1},{1,0},{2,3},{3,2},{4,5},{5,4},{6,7},{7,6},{8,9},{9,8},{10,11... | collective-permute-start | bytes 3145736 | tf_op jit(solution)/shard_map/ppermute | solution.py:267
  76.6 24.5 %all-to-all-start.2 = ((bf16[16,128,128]{2,1,0:T(8,128)(2,1)}), bf16[16,128,128]{2,1,0:T(8,128)(2,1)S(1)}, u32[]{:S(2)}, u32[]{:S(2)}) async-start(bf16[16,128,128]{2,1,0:T(8,128)(2,1)} %bitcast.9), calls=%async_computation.2 | async-start | bytes 1048576 | tf_op jit(solution)/shard_map/all_to_all | solution.py:284

commit v6 on v5

--- a/solution.py
+++ b/solution.py
@@ -160,7 +160,7 @@
         out_ref[:, 96 + 8 * half : 104 + 8 * half, :] = own
 
 
-def collect_kernel(half_ref, in_ref, q_ref, kv_ref, split):
+def collect_kernel(in_ref, q_ref, near_ref, far_ref, split):
     row, source = iota((ROWS, GROUPS * HALO), 0), iota((ROWS, GROUPS * HALO), 1)
     window = one_hot(row == OWN * (source // HALO) + source % HALO - HALO)
     row, source = iota((ROWS, GROUPS * 8), 0), iota((ROWS, GROUPS * 8), 1)
@@ -168,7 +168,6 @@
     for s in range(2):
         mine = slice(s * GROUPS, (s + 1) * GROUPS)
         for half in range(2):
-            slot = half_ref[0] if half == 0 else 1 - half_ref[0]
             extra = in_ref[mine, 96 + 8 * half : 104 + 8 * half, :]
             extra = extra.astype(F32).reshape(GROUPS * 8, HD).astype(BF)
             for part in range(2):
@@ -176,8 +175,8 @@
                 halo = in_ref[mine, at : at + 16, :].reshape(GROUPS * HALO, HD)
                 total = dot(window, halo)
                 total = total + dot(one_hot(here & (source % 8 // OWN == part)), extra)
-                for copy in range(4):
-                    kv_ref[copy, slot, part, s * ROWS : (s + 1) * ROWS] = total.astype(BF)
+                to = near_ref if half == 0 else far_ref
+                to[part, s * ROWS : (s + 1) * ROWS] = total.astype(to.dtype)
         split[...] = in_ref[mine, 0:32, :].astype(F32).reshape(GROUPS * 32, HD)
         for h in range(HEADS):
             q_ref[s, :, h * HD : (h + 1) * HD] = split[pl.ds(h, ROWS, stride=HEADS), :].astype(BF)
@@ -198,12 +197,18 @@
     quarter = layer_input.shape[2] // 4
     x_at, core = lax.axis_index("x"), lax.axis_index("core")
     flat_input = layer_input.reshape(2 * ROWS, 4 * quarter)
-    columns = []
-    for step in range(4):
-        piece = lax.dynamic_slice_in_dim(flat_input, (x_at + step) % 4 * quarter, quarter, 1)
-        if step:
-            piece = lax.ppermute(piece, "x", [(i, (i + step) % 4) for i in range(4)])
-        columns.append(piece)
+    columns = [
+        lax.dynamic_slice_in_dim(flat_input, (x_at + step) % 4 * quarter, quarter, 1)
+        for step in range(4)
+    ]
+
+    def along_x(step):
+        return lax.ppermute(columns[step], "x", [(i, (i + step) % 4) for i in range(4)])
+
+    def other_core(x):
+        return lax.ppermute(x, "core", [(0, 1), (1, 0)])
+
+    columns[1], columns[3] = along_x(1), along_x(3)
 
     row_spec = lambda width: pl.BlockSpec((1, ROWS, width), lambda s: (s, 0, 0))
     other = lax.ppermute(
@@ -218,20 +223,19 @@
         scratch_shapes=[pltpu.VMEM((ROWS * HEADS, HD), F32)],
         name="pack",
     )(queries, out_grad, attn_output, key_states, value_states)
-    hbm = pl.BlockSpec(memory_space=pltpu.HBM)
+    hbm = pl.BlockSpec(memory_space=pl.ANY)
     sent = pl.pallas_call(
         pack_other_kernel,
         out_shape=jax.ShapeDtypeStruct((PEERS, SEND, HD), BF),
-        in_specs=[whole((2, ROWS, 2 * HD)), hbm],
+        in_specs=[pl.BlockSpec(memory_space=pltpu.VMEM), hbm],
         out_specs=hbm,
         scratch_shapes=[pltpu.VMEM((PEERS, 40, HD), BF), pltpu.SemaphoreType.DMA(())],
         input_output_aliases={1: 0},
-        grid=(1,),
-        compiler_params=pltpu.CompilerParams(vmem_limit_bytes=32 << 20),
         name="pack_other",
     )(other, sent)
     arrived = lax.all_to_all(sent, peers, 0, 0, tiled=True)
     arrived, *columns = lax.optimization_barrier((arrived, *columns))
+    columns[2] = along_x(2)
 
     docs = lax.dynamic_index_in_dim(doc_ids, sequence, 0, keepdims=False)
     places = lax.dynamic_index_in_dim(positions, sequence, 0, keepdims=False)
@@ -264,28 +268,34 @@
         name="attend",
     )(arrived, kpos.astype(F32), qpos.astype(F32), qlow.astype(F32))
     home = lax.all_to_all(back, peers, 0, 0, tiled=True)
-    twin = lax.ppermute(jnp.stack(columns), "core", [(0, 1), (1, 0)])
-    home, twin = lax.optimization_barrier((home, twin))
-
-    query_grad, kv_grad = pl.pallas_call(
+    twin = other_core(jnp.stack([columns[0], columns[1], columns[3]]))
+    home, twin, columns[2] = lax.optimization_barrier((home, twin, columns[2]))
+    twin = [twin[0], twin[1], other_core(columns[2]), twin[2]]
+
+    query_grad, near_grad, far_grad = pl.pallas_call(
         collect_kernel,
         out_shape=(
             jax.ShapeDtypeStruct((2, ROWS, HEADS * HD), BF),
-            jax.ShapeDtypeStruct((4, 2, 2, 2 * ROWS, HD), BF),
+            jax.ShapeDtypeStruct((2, 2 * ROWS, HD), F32),
+            jax.ShapeDtypeStruct((2, 2 * ROWS, HD), BF),
         ),
         grid=(1,),
-        in_specs=[pl.BlockSpec(memory_space=pltpu.SMEM), whole((PEERS, BACK, HD))],
-        out_specs=(whole((2, ROWS, HEADS * HD)), whole((4, 2, 2, 2 * ROWS, HD))),
+        in_specs=[whole((PEERS, BACK, HD))],
+        out_specs=(
+            whole((2, ROWS, HEADS * HD)),
+            whole((2, 2 * ROWS, HD)),
+            whole((2, 2 * ROWS, HD)),
+        ),
         scratch_shapes=[pltpu.VMEM((GROUPS * 32, HD), F32)],
         compiler_params=pltpu.CompilerParams(vmem_limit_bytes=32 << 20),
         name="collect",
-    )(half[None], home)
-
+    )(home)
+    kv_grad = (near_grad + lax.ppermute(far_grad, "zu", [(0, 1), (1, 0)])).astype(BF)
+
+    kv_grad = jnp.broadcast_to(kv_grad[None], (4, 2, 2 * ROWS, HD))
     grads = lax.all_to_all(
-        kv_grad.reshape(16, 2 * ROWS, HD), ("x", "zu", "core"), 0, 0, tiled=True
-    )
-    grads = jnp.sum(grads.reshape(4, 2, 2, 2 * ROWS, HD).astype(F32), axis=1).astype(BF)
-    grads = grads.reshape(8, 2 * ROWS, HD)
+        kv_grad.reshape(8, 2 * ROWS, HD), ("x", "core"), 0, 0, tiled=True
+    )
     part = jnp.zeros((quarter, HD), F32)
     for step in range(4):
         for piece, at in ((columns[step], core), (twin[step], 1 - core)):

time: 145 us -> 144 us (level)
  waiting for transfers between devices: 41 us -> 28.9 us
  starting transfers between devices: 42.9 us -> 48.4 us
  blocking collectives: 40.4 us -> 44.9 us
    all_to_all x1, waiting for transfers between devices: 16.4 us -> 4.52 us  [local(): lax.all_to_all(kv_grad.reshape(8, 2 * ROWS, HD), ('x', 'core'), 0, 0, til...]
    all_to_all x1, waiting for transfers between devices: 8.25 us -> 0.01 us  [local(): home = lax.all_to_all(back, peers, 0, 0, tiled=True)]
    ppermute x4 -> x6, waiting for transfers between devices: 16.3 us -> 24.4 us  [the longest x3 22.8 us: along_x(): lax.ppermute(columns[step], 'x', [(i, (i + step) % 4) for i in range(4)])]
    ppermute x4 -> x6, starting transfers between devices: 13.6 us -> 21.4 us  [the longest x3 11.4 us: along_x(): lax.ppermute(columns[step], 'x', [(i, (i + step) % 4) for i in range(4)])]
    all_to_all x1, blocking collectives: 12.7 us -> 16.8 us  [local(): part = lax.all_to_all(part, ('zu', 'zd', 'y'), 0, 0, tiled=True)]
    all_to_all x1, starting transfers between devices: 8.09 us -> 6.1 us  [local(): lax.all_to_all(kv_grad.reshape(8, 2 * ROWS, HD), ('x', 'core'), 0, 0, til...]
    unnamed x11, local copies, waits for them, and re-layouts: 2.97 us -> 1.28 us
    pallas_call x1, Pallas kernels: 0.3 us -> 1.88 us  [local(): pl.pallas_call(pack_other_kernel, out_shape=jax.ShapeDtypeStruct((PEERS,...]
  transfers between devices with their start and end apart: 8 -> 10, of which waited for: 5 -> 4; matrix products, arithmetic and copies ran while one was open for 2% -> 3% of each run, Pallas kernels for 2% -> 2%
where the time goes in v6:
time: 144 us
  starting transfers between devices  48.4 us (34%)
  blocking collectives  44.9 us (31%)
  waiting for transfers between devices  28.9 us (20%)
  Pallas kernels  12.1 us (8%)
  local copies, waits for them, and re-layouts  4.04 us (3%)
  matrix products  3.04 us (2%)
    all_to_all x1, blocking collectives, local(): lax.all_to_all(jnp.broadcast_to(part[None], (4, 64, HD)), 'zh', 0, 0, til...  23.1 us
    ppermute x3, waiting for transfers between devices, along_x(): lax.ppermute(columns[step], 'x', [(i, (i + step) % 4) for i in range(4)])  22.8 us
    all_to_all x1, blocking collectives, local(): part = lax.all_to_all(part, ('zu', 'zd', 'y'), 0, 0, tiled=True)  16.8 us
    ppermute x3, starting transfers between devices, along_x(): lax.ppermute(columns[step], 'x', [(i, (i + step) % 4) for i in range(4)])  11.4 us
    all_to_all x1, starting transfers between devices, local(): arrived = lax.all_to_all(sent, peers, 0, 0, tiled=True)  8.54 us
    pallas_call x1, Pallas kernels, local(): pl.pallas_call(attend_kernel, out_shape=jax.ShapeDtypeStruct((PEERS, BACK...  6.62 us
    all_to_all x1, starting transfers between devices, local(): home = lax.all_to_all(back, peers, 0, 0, tiled=True)  6.6 us
    all_to_all x1, starting transfers between devices, local(): lax.all_to_all(kv_grad.reshape(8, 2 * ROWS, HD), ('x', 'core'), 0, 0, til...  6.1 us
  transfers between devices with their start and end apart: 10, of which 4 were waited for; matrix products, arithmetic and copies ran while one was open for 3% of the time, Pallas kernels for 2%

profile of v6, /device:TPU:1, one launch (start us, length us, event | category | flops | bytes accessed | tf_op | source)
XLA Modules:
  0.0 143.6 jit_solution(13924550399981994858)
XLA Ops:
  0.6 0.8 pad_maximum_fusion.1
  1.4 5.7 %collective-permute-start = (bf16[2,64,256]{2,1,0:T(8,128)(2,1)S(1)}, bf16[2,64,256]{2,1,0:T(8,128)(2,1)S(1)}, u32[]{:S(2)}, u32[]{:S(2)}) collective-permute-start(bf16[2,64,256]{2,1,0:T(8,128)(2,1)S(1)} %pad_maximum_fusion.1), channel_id=1, source_target_pairs={{0,64},{64,0},{1,65},{65,1},{2,66},{66,2},{3,67},{67,3},{4,68},{68... | collective-permute-start | bytes 196616 | tf_op jit(solution)/shard_map/ppermute | solution.py:214
  7.2 2.6 %pack.1.in_ref = bf16[32,152,128]{2,1,0:T(8,128)(2,1)} custom-call(bf16[2,64,1024]{2,1,0:T(8,128)(2,1)} %q_ref.1, bf16[2,64,1024]{2,1,0:T(8,128)(2,1)} %g_ref.1, bf16[2,64,1024]{2,1,0:T(8,128)(2,1)} %o_ref.1, bf16[2,64,128]{2,1,0:T(8,128)(2,1)} %k_ref.1, bf16[2,64,128]{2,1,0:T(8,128)(2,1)} %v_ref.1), custom_call_target="tpu_custom_call" | custom-call | tf_op jit(solution)/shard_map/pack/pallas_call | solution.py:217
  9.7 0.6 copy-done.2
  10.4 1.9 %pack_other.1 = bf16[32,152,128]{2,1,0:T(8,128)(2,1)} custom-call(bf16[2,64,256]{2,1,0:T(8,128)(2,1)} %copy-done.2, bf16[32,152,128]{2,1,0:T(8,128)(2,1)} %pack.1.in_ref), custom_call_target="tpu_custom_call", output_to_operand_aliasing={{}: (1, {})} | custom-call | tf_op jit(solution)/shard_map/pack_other/pallas_call | solution.py:227
  12.2 8.5 %all-to-all-start = ((bf16[32,152,128]{2,1,0:T(8,128)(2,1)}), bf16[32,152,128]{2,1,0:T(8,128)(2,1)S(1)}, u32[]{:S(2)}, u32[]{:S(2)}) async-start(bf16[32,152,128]{2,1,0:T(8,128)(2,1)} %pack_other.1), calls=%async_computation | async-start | bytes 2490368 | tf_op jit(solution)/shard_map/all_to_all | solution.py:236
  20.9 0.8 constant_dynamic-slice_fusion.1
  21.7 3.1 %collective-permute-start.1 = (bf16[128,1024]{1,0:T(8,128)(2,1)S(1)}, bf16[128,1024]{1,0:T(8,128)(2,1)S(1)}, u32[]{:S(2)}, u32[]{:S(2)}) collective-permute-start(bf16[128,1024]{1,0:T(8,128)(2,1)S(1)} %get-tuple-element.26), channel_id=1, source_target_pairs={{0,128},{128,256},{256,384},{384,0},{1,129},{129,257},{257,385},{3... | collective-permute-start | bytes 786440 | tf_op jit(solution)/shard_map/ppermute | solution.py:206
  24.8 3.4 %collective-permute-start.2 = (bf16[128,1024]{1,0:T(8,128)(2,1)S(1)}, bf16[128,1024]{1,0:T(8,128)(2,1)S(1)}, u32[]{:S(2)}, u32[]{:S(2)}) collective-permute-start(bf16[128,1024]{1,0:T(8,128)(2,1)S(1)} %get-tuple-element.24), channel_id=1, source_target_pairs={{0,384},{128,0},{256,128},{384,256},{1,385},{129,1},{257,129},{385... | collective-permute-start | bytes 786440 | tf_op jit(solution)/shard_map/ppermute | solution.py:206
  28.4 0.1 fusion.34
  28.5 0.1 slice.30
  28.5 0.1 reshape.114
  28.7 0.1 convert_reduce_fusion
  28.8 0.1 select_reduce_fusion
  28.9 0.1 concatenate.24
  29.1 0.1 concatenate.25
  29.2 0.1 concatenate.22
  29.3 0.1 concatenate.23
  29.4 0.1 broadcast_in_dim.20
  29.4 0.1 convert_element_type.38.qlow_ref
  29.6 0.1 broadcast_in_dim.18
  29.6 0.1 convert_element_type.35.qpos_ref
  29.8 12.8 %collective-permute-done.1 = bf16[128,1024]{1,0:T(8,128)(2,1)S(1)} collective-permute-done((bf16[128,1024]{1,0:T(8,128)(2,1)S(1)}, bf16[128,1024]{1,0:T(8,128)(2,1)S(1)}, u32[]{:S(2)}, u32[]{:S(2)}) %collective-permute-start.1) | collective-permute-done | bytes 262176 | tf_op jit(solution)/shard_map/ppermute | solution.py:206
  42.6 6.6 %attend.1 = bf16[32,112,128]{2,1,0:T(8,128)(2,1)} custom-call(bf16[32,152,128]{2,1,0:T(8,128)(2,1)S(1)} %all-to-all-done.in_ref, f32[1,1280]{1,0:T(1,128)S(1)} %add_convert_fusion.1.kpos_ref, f32[1,1024]{1,0:T(1,128)S(1)} %convert_element_type.35.qpos_ref, f32[1,1024]{1,0:T(1,128)S(1)} %convert_element_type.38.qlow_ref), custom_call_target="tpu_custom_call" | custom-call | tf_op jit(solution)/shard_map/attend/pallas_call | solution.py:255
  49.2 6.6 %all-to-all-start.1 = ((bf16[32,112,128]{2,1,0:T(8,128)(2,1)}), bf16[32,112,128]{2,1,0:T(8,128)(2,1)S(1)}, u32[]{:S(2)}, u32[]{:S(2)}) async-start(bf16[32,112,128]{2,1,0:T(8,128)(2,1)} %attend.1), calls=%async_computation.1 | async-start | bytes 1835008 | tf_op jit(solution)/shard_map/all_to_all | solution.py:270
  55.8 0.1 pad_maximum_fusion
  55.9 3.1 %collective-permute-start.3 = (bf16[3,128,1024]{2,1,0:T(8,128)(2,1)S(1)}, bf16[3,128,1024]{2,1,0:T(8,128)(2,1)S(1)}, u32[]{:S(2)}, u32[]{:S(2)}) collective-permute-start(bf16[3,128,1024]{2,1,0:T(8,128)(2,1)S(1)} %pad_maximum_fusion), channel_id=1, source_target_pairs={{0,1},{1,0},{2,3},{3,2},{4,5},{5,4},{6,7},{7,6},{8,9},{9,8},{10,11... | collective-permute-start | bytes 2359304 | tf_op jit(solution)/shard_map/ppermute | solution.py:209
  59.1 4.9 %collective-permute-start.4 = (bf16[128,1024]{1,0:T(8,128)(2,1)S(1)}, bf16[128,1024]{1,0:T(8,128)(2,1)S(1)}, u32[]{:S(2)}, u32[]{:S(2)}) collective-permute-start(bf16[128,1024]{1,0:T(8,128)(2,1)S(1)} %copy-done.1), channel_id=1, source_target_pairs={{0,256},{128,384},{256,0},{384,128},{1,257},{129,385},{257,1},{385... | collective-permute-start | bytes 786440 | tf_op jit(solution)/shard_map/ppermute | solution.py:206
  64.0 9.9 %collective-permute-done.4 = bf16[128,1024]{1,0:T(8,128)(2,1)S(1)} collective-permute-done((bf16[128,1024]{1,0:T(8,128)(2,1)S(1)}, bf16[128,1024]{1,0:T(8,128)(2,1)S(1)}, u32[]{:S(2)}, u32[]{:S(2)}) %collective-permute-start.4) | collective-permute-done | bytes 262176 | tf_op jit(solution)/shard_map/ppermute | solution.py:206
  74.0 1.0 collect.1
  75.0 4.9 %collective-permute-start.5 = (bf16[2,128,128]{2,1,0:T(8,128)(2,1)S(1)}, bf16[2,128,128]{2,1,0:T(8,128)(2,1)S(1)}, u32[]{:S(2)}, u32[]{:S(2)}) collective-permute-start(bf16[2,128,128]{2,1,0:T(8,128)(2,1)S(1)} %get-tuple-element.21), channel_id=1, source_target_pairs={{0,64},{64,0},{1,65},{65,1},{2,66},{66,2},{3,67},{67,3},{4,68},{68... | collective-permute-start | bytes 196616 | tf_op jit(solution)/shard_map/ppermute | solution.py:293
  79.9 1.6 %collective-permute-done.5 = bf16[2,128,128]{2,1,0:T(8,128)(2,1)S(1)} collective-permute-done((bf16[2,128,128]{2,1,0:T(8,128)(2,1)S(1)}, bf16[2,128,128]{2,1,0:T(8,128)(2,1)S(1)}, u32[]{:S(2)}, u32[]{:S(2)}) %collective-permute-start.5) | collective-permute-done | bytes 65568 | tf_op jit(solution)/shard_map/ppermute | solution.py:293
  81.6 0.7 broadcast_in_dim.21
  82.3 6.1 %all-to-all-start.2 = ((bf16[8,128,128]{2,1,0:T(8,128)(2,1)}), bf16[8,128,128]{2,1,0:T(8,128)(2,1)S(1)}, u32[]{:S(2)}, u32[]{:S(2)}) async-start(bf16[8,128,128]{2,1,0:T(8,128)(2,1)} %bitcast.7), calls=%async_computation.2 | async-start | bytes 524288 | tf_op jit(solution)/shard_map/all_to_all | solution.py:296
  88.4 2.0 %collective-permute-start.6 = (bf16[128,1024]{1,0:T(8,128)(2,1)S(1)}, bf16[128,1024]{1,0:T(8,128)(2,1)}, u32[]{:S(2)}, u32[]{:S(2)}) collective-permute-start(bf16[128,1024]{1,0:T(8,128)(2,1)S(1)} %collective-permute-done.4), channel_id=1, source_target_pairs={{0,1},{1,0},{2,3},{3,2},{4,5},{5,4},{6,7},{7,6},{8,9},{9,8},{10,11... | collective-permute-start | bytes 786440 | tf_op jit(solution)/shard_map/ppermute | solution.py:209
  90.4 4.5 %all-to-all-done.2 = bf16[8,128,128]{2,1,0:T(8,128)(2,1)S(1)} async-done(((bf16[8,128,128]{2,1,0:T(8,128)(2,1)}), bf16[8,128,128]{2,1,0:T(8,128)(2,1)S(1)}, u32[]{:S(2)}, u32[]{:S(2)}) %all-to-all-start.2) | async-done | bytes 262176 | tf_op jit(solution)/shard_map/all_to_all | solution.py:296
  94.9 0.2 fusion.22
  95.2 0.3 fusion.10
  95.4 0.3 fusion.8
  95.7 0.3 fusion.16
  95.9 0.3 fusion.6
  96.2 1.2 fusion.18
  97.4 0.3 fusion.1
  97.7 0.3 fusion.5
  98.0 16.8 %all_to_all.25 = bf16[16,64,128]{2,1,0:T(8,128)(2,1)S(1)} all-to-all(bf16[16,64,128]{2,1,0:T(8,128)(2,1)S(1)} %bitcast.53), channel_id=1, replica_groups=mesh['x'=4,'zu'=2,'zd'=2,'y'=4,'zh'=4,'core'=2] {'zu','zd','y'}, dimensions={0} | all-to-all | bytes 524288 | tf_op jit(solution)/shard_map/all_to_all | solution.py:309
  114.8 23.1 %all_to_all.26 = bf16[4,64,128]{2,1,0:T(8,128)(2,1)S(1)} all-to-all(bf16[4,64,128]{2,1,0:T(8,128)(2,1)S(1)} %broadcast_in_dim.22), channel_id=1, replica_groups=mesh['x'=4,'zu'=2,'zd'=2,'y'=4,'zh'=4,'core'=2] {'zh'}, dimensions={0} | all-to-all | bytes 131072 | tf_op jit(solution)/shard_map/all_to_all | solution.py:311
  137.9 5.1 %all_gather.3 = f32[64,256]{1,0:T(8,128)S(1)} all-gather(f32[64,128]{1,0:T(8,128)S(1)} %convert_reduce_fusion.1), channel_id=1, replica_groups=mesh['x'=4,'zu'=2,'zd'=2,'y'=4,'zh'=4,'core'=2] {'core'}, dimensions={1}, use_global_device_ids=true | all-gather | bytes 98304 | tf_op jit(solution)/shard_map/all_gather | solution.py:313
  143.0 0.6 copy.13
  (25 shorter events, 0.3 us)
Async XLA Ops:
  1.4 8.3 %collective-permute-start = (bf16[2,64,256]{2,1,0:T(8,128)(2,1)S(1)}, bf16[2,64,256]{2,1,0:T(8,128)(2,1)S(1)}, u32[]{:S(2)}, u32[]{:S(2)}) collective-permute-start(bf16[2,64,256]{2,1,0:T(8,128)(2,1)S(1)} %pad_maximum_fusion.1), channel_id=1, source_target_pairs={{0,64},{64,0},{1,65},{65,1},{2,66},{66,2},{3,67},{67,3},{4,68},{68... | collective-permute-start | bytes 196616 | tf_op jit(solution)/shard_map/ppermute | solution.py:214
  9.7 0.6 copy-start.2
  12.2 8.6 %copy-start = (bf16[2,64,4096]{2,1,0:T(8,128)(2,1)S(1)}, bf16[2,64,4096]{2,1,0:T(8,128)(2,1)}, u32[]{:S(2)}) copy-start(bf16[2,64,4096]{2,1,0:T(8,128)(2,1)} %param.8) | copy-start | bytes 3145732
  12.2 30.3 %all-to-all-start = ((bf16[32,152,128]{2,1,0:T(8,128)(2,1)}), bf16[32,152,128]{2,1,0:T(8,128)(2,1)S(1)}, u32[]{:S(2)}, u32[]{:S(2)}) async-start(bf16[32,152,128]{2,1,0:T(8,128)(2,1)} %pack_other.1), calls=%async_computation | async-start | bytes 2490368 | tf_op jit(solution)/shard_map/all_to_all | solution.py:236
  20.8 7.4 %copy-start.3 = (s32[2,4096]{1,0:T(2,128)S(1)}, s32[2,4096]{1,0:T(2,128)}, u32[]{:S(2)}) copy-start(s32[2,4096]{1,0:T(2,128)} %param.15) | copy-start | bytes 98308
  20.8 7.4 %copy-start.4 = (s32[2,4096]{1,0:T(2,128)S(1)}, s32[2,4096]{1,0:T(2,128)}, u32[]{:S(2)}) copy-start(s32[2,4096]{1,0:T(2,128)} %param.14) | copy-start | bytes 98308
  21.7 20.9 %collective-permute-start.1 = (bf16[128,1024]{1,0:T(8,128)(2,1)S(1)}, bf16[128,1024]{1,0:T(8,128)(2,1)S(1)}, u32[]{:S(2)}, u32[]{:S(2)}) collective-permute-start(bf16[128,1024]{1,0:T(8,128)(2,1)S(1)} %get-tuple-element.26), channel_id=1, source_target_pairs={{0,128},{128,256},{256,384},{384,0},{1,129},{129,257},{257,385},{3... | collective-permute-start | bytes 786440 | tf_op jit(solution)/shard_map/ppermute | solution.py:206
  24.8 17.8 %collective-permute-start.2 = (bf16[128,1024]{1,0:T(8,128)(2,1)S(1)}, bf16[128,1024]{1,0:T(8,128)(2,1)S(1)}, u32[]{:S(2)}, u32[]{:S(2)}) collective-permute-start(bf16[128,1024]{1,0:T(8,128)(2,1)S(1)} %get-tuple-element.24), channel_id=1, source_target_pairs={{0,384},{128,0},{256,128},{384,256},{1,385},{129,1},{257,129},{385... | collective-permute-start | bytes 786440 | tf_op jit(solution)/shard_map/ppermute | solution.py:206
  49.2 24.8 %all-to-all-start.1 = ((bf16[32,112,128]{2,1,0:T(8,128)(2,1)}), bf16[32,112,128]{2,1,0:T(8,128)(2,1)S(1)}, u32[]{:S(2)}, u32[]{:S(2)}) async-start(bf16[32,112,128]{2,1,0:T(8,128)(2,1)} %attend.1), calls=%async_computation.1 | async-start | bytes 1835008 | tf_op jit(solution)/shard_map/all_to_all | solution.py:270
  55.8 3.3 %copy-start.1 = (bf16[128,1024]{1,0:T(8,128)(2,1)S(1)}, bf16[128,1024]{1,0:T(8,128)(2,1)}, u32[]{:S(2)}) copy-start(bf16[128,1024]{1,0:T(8,128)(2,1)} %get-tuple-element.17) | copy-start | bytes 786436
  55.9 18.0 %collective-permute-start.3 = (bf16[3,128,1024]{2,1,0:T(8,128)(2,1)S(1)}, bf16[3,128,1024]{2,1,0:T(8,128)(2,1)S(1)}, u32[]{:S(2)}, u32[]{:S(2)}) collective-permute-start(bf16[3,128,1024]{2,1,0:T(8,128)(2,1)S(1)} %pad_maximum_fusion), channel_id=1, source_target_pairs={{0,1},{1,0},{2,3},{3,2},{4,5},{5,4},{6,7},{7,6},{8,9},{9,8},{10,11... | collective-permute-start | bytes 2359304 | tf_op jit(solution)/shard_map/ppermute | solution.py:209
  59.1 14.9 %collective-permute-start.4 = (bf16[128,1024]{1,0:T(8,128)(2,1)S(1)}, bf16[128,1024]{1,0:T(8,128)(2,1)S(1)}, u32[]{:S(2)}, u32[]{:S(2)}) collective-permute-start(bf16[128,1024]{1,0:T(8,128)(2,1)S(1)} %copy-done.1), channel_id=1, source_target_pairs={{0,256},{128,384},{256,0},{384,128},{1,257},{129,385},{257,1},{385... | collective-permute-start | bytes 786440 | tf_op jit(solution)/shard_map/ppermute | solution.py:206
  75.0 6.5 %collective-permute-start.5 = (bf16[2,128,128]{2,1,0:T(8,128)(2,1)S(1)}, bf16[2,128,128]{2,1,0:T(8,128)(2,1)S(1)}, u32[]{:S(2)}, u32[]{:S(2)}) collective-permute-start(bf16[2,128,128]{2,1,0:T(8,128)(2,1)S(1)} %get-tuple-element.21), channel_id=1, source_target_pairs={{0,64},{64,0},{1,65},{65,1},{2,66},{66,2},{3,67},{67,3},{4,68},{68... | collective-permute-start | bytes 196616 | tf_op jit(solution)/shard_map/ppermute | solution.py:293
  82.3 12.6 %all-to-all-start.2 = ((bf16[8,128,128]{2,1,0:T(8,128)(2,1)}), bf16[8,128,128]{2,1,0:T(8,128)(2,1)S(1)}, u32[]{:S(2)}, u32[]{:S(2)}) async-start(bf16[8,128,128]{2,1,0:T(8,128)(2,1)} %bitcast.7), calls=%async_computation.2 | async-start | bytes 524288 | tf_op jit(solution)/shard_map/all_to_all | solution.py:296
  88.4 7.8 %collective-permute-start.6 = (bf16[128,1024]{1,0:T(8,128)(2,1)S(1)}, bf16[128,1024]{1,0:T(8,128)(2,1)}, u32[]{:S(2)}, u32[]{:S(2)}) collective-permute-start(bf16[128,1024]{1,0:T(8,128)(2,1)S(1)} %collective-permute-done.4), channel_id=1, source_target_pairs={{0,1},{1,0},{2,3},{3,2},{4,5},{5,4},{6,7},{7,6},{8,9},{9,8},{10,11... | collective-permute-start | bytes 786440 | tf_op jit(solution)/shard_map/ppermute | solution.py:209

commit v7 on v6

--- a/solution.py
+++ b/solution.py
@@ -189,31 +189,30 @@
 def local(
     layer_input, queries, key_states, value_states, attn_output, out_grad, doc_ids, positions
 ):
-    peers = ("x", "zd", "y")
+    peers = ("xu", "xd", "zd", "y")
     index = lax.axis_index(peers)
     half = lax.axis_index("zu")
     sequence, group = index // GROUPS, index % GROUPS
 
-    quarter = layer_input.shape[2] // 4
-    x_at, core = lax.axis_index("x"), lax.axis_index("core")
-    flat_input = layer_input.reshape(2 * ROWS, 4 * quarter)
-    columns = [
-        lax.dynamic_slice_in_dim(flat_input, (x_at + step) % 4 * quarter, quarter, 1)
-        for step in range(4)
-    ]
-
-    def along_x(step):
-        return lax.ppermute(columns[step], "x", [(i, (i + step) % 4) for i in range(4)])
-
-    def other_core(x):
-        return lax.ppermute(x, "core", [(0, 1), (1, 0)])
-
-    columns[1], columns[3] = along_x(1), along_x(3)
+    wide = layer_input.shape[2] // 2
+    low_bit, core = lax.axis_index("xd"), lax.axis_index("core")
+    flat_input = layer_input.reshape(2 * ROWS, 2 * wide)
+
+    def swapped(array, axis):
+        return lax.ppermute(array, axis, [(0, 1), (1, 0)])
+
+    def columns_of(bit):
+        first = bit * (wide // 2)
+        parts = [
+            lax.dynamic_slice_in_dim(flat_input, first + high * wide, wide // 2, 1)
+            for high in range(2)
+        ]
+        return jnp.stack(parts)
+
+    columns = [columns_of(low_bit), swapped(columns_of(1 - low_bit), "xd")]
 
     row_spec = lambda width: pl.BlockSpec((1, ROWS, width), lambda s: (s, 0, 0))
-    other = lax.ppermute(
-        jnp.concatenate([key_states, value_states], axis=2), "zu", [(0, 1), (1, 0)]
-    )
+    other = swapped(jnp.concatenate([key_states, value_states], axis=2), "zu")
     sent = pl.pallas_call(
         pack_kernel,
         out_shape=jax.ShapeDtypeStruct((PEERS, SEND, HD), BF),
@@ -235,7 +234,6 @@
     )(other, sent)
     arrived = lax.all_to_all(sent, peers, 0, 0, tiled=True)
     arrived, *columns = lax.optimization_barrier((arrived, *columns))
-    columns[2] = along_x(2)
 
     docs = lax.dynamic_index_in_dim(doc_ids, sequence, 0, keepdims=False)
     places = lax.dynamic_index_in_dim(positions, sequence, 0, keepdims=False)
@@ -268,9 +266,8 @@
         name="attend",
     )(arrived, kpos.astype(F32), qpos.astype(F32), qlow.astype(F32))
     home = lax.all_to_all(back, peers, 0, 0, tiled=True)
-    twin = other_core(jnp.stack([columns[0], columns[1], columns[3]]))
-    home, twin, columns[2] = lax.optimization_barrier((home, twin, columns[2]))
-    twin = [twin[0], twin[1], other_core(columns[2]), twin[2]]
+    twin = swapped(jnp.stack(columns), "core")
+    home, twin = lax.optimization_barrier((home, twin))
 
     query_grad, near_grad, far_grad = pl.pallas_call(
         collect_kernel,
@@ -290,23 +287,21 @@
         compiler_params=pltpu.CompilerParams(vmem_limit_bytes=32 << 20),
         name="collect",
     )(home)
-    kv_grad = (near_grad + lax.ppermute(far_grad, "zu", [(0, 1), (1, 0)])).astype(BF)
-
-    kv_grad = jnp.broadcast_to(kv_grad[None], (4, 2, 2 * ROWS, HD))
+    kv_grad = (near_grad + swapped(far_grad, "zu")).astype(BF)
+
+    kv_grad = jnp.broadcast_to(kv_grad[None], (2, 2, 2 * ROWS, HD))
     grads = lax.all_to_all(
-        kv_grad.reshape(8, 2 * ROWS, HD), ("x", "core"), 0, 0, tiled=True
+        kv_grad.reshape(4, 2 * ROWS, HD), ("xd", "core"), 0, 0, tiled=True
     )
-    part = jnp.zeros((quarter, HD), F32)
-    for step in range(4):
-        for piece, at in ((columns[step], core), (twin[step], 1 - core)):
-            grad = lax.dynamic_index_in_dim(
-                grads, (x_at - step) % 4 * 2 + at, 0, keepdims=False
+    part = jnp.zeros((2, wide // 2, HD), F32)
+    for bit, pair in ((low_bit, 0), (1 - low_bit, 1)):
+        for piece, at in ((columns[pair], core), (twin[pair], 1 - core)):
+            grad = lax.dynamic_index_in_dim(grads, bit * 2 + at, 0, keepdims=False)
+            part = part + lax.dot_general(
+                piece, grad, (((1,), (0,)), ((), ())), preferred_element_type=F32
             )
-            part = part + lax.dot_general(
-                piece, grad, (((0,), (0,)), ((), ())), preferred_element_type=F32
-            )
-    part = part.reshape(16, 64, HD).astype(BF)
-    part = lax.all_to_all(part, ("zu", "zd", "y"), 0, 0, tiled=True)
+    part = part.reshape(32, 64, HD).astype(BF)
+    part = lax.all_to_all(part, ("xu", "zu", "zd", "y"), 0, 0, tiled=True)
     part = jnp.sum(part.astype(F32), axis=0).astype(BF)
     part = lax.all_to_all(jnp.broadcast_to(part[None], (4, 64, HD)), "zh", 0, 0, tiled=True)
     part = jnp.sum(part.astype(F32), axis=0)
@@ -315,9 +310,9 @@
 
 
 def solution(mesh):
-    devices = mesh.devices.reshape(4, 2, 2, 4, -1, 2)
-    inner = Mesh(devices, ("x", "zu", "zd", "y", "zh", "core"))
-    ctx, dp = ("x", "zu", "zd", "y"), ("zh", "core")
+    devices = mesh.devices.reshape(2, 2, 2, 2, 4, -1, 2)
+    inner = Mesh(devices, ("xu", "xd", "zu", "zd", "y", "zh", "core"))
+    ctx, dp = ("xu", "xd", "zu", "zd", "y"), ("zh", "core")
     rows = P(dp, ctx, None)
     whole_rows = P(dp, None)
     return jax.shard_map(

time: 144 us -> 148 us (1.028)
  starting transfers between devices: 48.4 us -> 39.8 us
  blocking collectives: 44.9 us -> 52.1 us
  waiting for transfers between devices: 28.9 us -> 35.3 us
  matrix products: 3.04 us -> 1.13 us
    ppermute x7 -> x4, starting transfers between devices: 27.1 us -> 16.9 us  [swapped(): return lax.ppermute(array, axis, [(0, 1), (1, 0)])]
    all_to_all x1, waiting for transfers between devices: 0.01 us -> 8.27 us  [local(): home = lax.all_to_all(back, peers, 0, 0, tiled=True)]
    all_to_all x1, blocking collectives: 16.8 us -> 23.2 us  [local(): part = lax.all_to_all(part, ('xu', 'zu', 'zd', 'y'), 0, 0, tiled=True)]
    all_to_all x1, starting transfers between devices: 6.6 us -> 8.64 us  [local(): home = lax.all_to_all(back, peers, 0, 0, tiled=True)]
    dot_general x8 -> x4, matrix products: 3.04 us -> 1.13 us  [local(): lax.dot_general(piece, grad, (((1,), (0,)), ((), ())), preferred_element_...]
    ppermute x7 -> x4, waiting for transfers between devices: 24.4 us -> 23.4 us  [swapped(): return lax.ppermute(array, axis, [(0, 1), (1, 0)])]
  transfers between devices with their start and end apart: 10 -> 7, of which waited for: 4 -> 5; matrix products, arithmetic and copies ran while one was open for 3% -> 2% of each run, Pallas kernels for 2% -> 2%
where the time goes in v7:
time: 148 us; the launch traced here: 147 us
  blocking collectives  52.1 us (35%)
  starting transfers between devices  39.8 us (27%)
  waiting for transfers between devices  35.3 us (24%)
  Pallas kernels  12.1 us (8%)
  local copies, waits for them, and re-layouts  3.93 us (3%)
  other arithmetic  2.19 us (1%)
    ppermute x4, waiting for transfers between devices, swapped(): return lax.ppermute(array, axis, [(0, 1), (1, 0)])  23.4 us
    all_to_all x1, blocking collectives, local(): lax.all_to_all(jnp.broadcast_to(part[None], (4, 64, HD)), 'zh', 0, 0, til...  23.4 us
    all_to_all x1, blocking collectives, local(): part = lax.all_to_all(part, ('xu', 'zu', 'zd', 'y'), 0, 0, tiled=True)  23.2 us
    ppermute x4, starting transfers between devices, swapped(): return lax.ppermute(array, axis, [(0, 1), (1, 0)])  16.9 us
    all_to_all x1, starting transfers between devices, local(): home = lax.all_to_all(back, peers, 0, 0, tiled=True)  8.64 us
    all_to_all x1, starting transfers between devices, local(): arrived = lax.all_to_all(sent, peers, 0, 0, tiled=True)  8.54 us
    all_to_all x1, waiting for transfers between devices, local(): home = lax.all_to_all(back, peers, 0, 0, tiled=True)  8.27 us
    pallas_call x1, Pallas kernels, local(): pl.pallas_call(attend_kernel, out_shape=jax.ShapeDtypeStruct((PEERS, BACK...  6.61 us
  transfers between devices with their start and end apart: 7, of which 5 were waited for; matrix products, arithmetic and copies ran while one was open for 2% of the time, Pallas kernels for 2%

profile of v7, /device:TPU:1, one launch (start us, length us, event | category | flops | bytes accessed | tf_op | source)
XLA Modules:
  0.0 147.4 jit_solution(10705237901916801959)
XLA Ops:
  0.6 0.8 pad_maximum_fusion.3
  1.4 5.7 %collective-permute-start = (bf16[2,64,256]{2,1,0:T(8,128)(2,1)S(1)}, bf16[2,64,256]{2,1,0:T(8,128)(2,1)S(1)}, u32[]{:S(2)}, u32[]{:S(2)}) collective-permute-start(bf16[2,64,256]{2,1,0:T(8,128)(2,1)S(1)} %pad_maximum_fusion.3), channel_id=1, source_target_pairs={{0,64},{64,0},{1,65},{65,1},{2,66},{66,2},{3,67},{67,3},{4,68},{68... | collective-permute-start | bytes 196616 | tf_op jit(solution)/shard_map/ppermute | solution.py:202
  7.2 2.6 %pack.1.in_ref = bf16[32,152,128]{2,1,0:T(8,128)(2,1)} custom-call(bf16[2,64,1024]{2,1,0:T(8,128)(2,1)} %q_ref.1, bf16[2,64,1024]{2,1,0:T(8,128)(2,1)} %g_ref.1, bf16[2,64,1024]{2,1,0:T(8,128)(2,1)} %o_ref.1, bf16[2,64,128]{2,1,0:T(8,128)(2,1)} %k_ref.1, bf16[2,64,128]{2,1,0:T(8,128)(2,1)} %v_ref.1), custom_call_target="tpu_custom_call" | custom-call | tf_op jit(solution)/shard_map/pack/pallas_call | solution.py:216
  9.7 0.6 copy-done.1
  10.4 1.9 %pack_other.1 = bf16[32,152,128]{2,1,0:T(8,128)(2,1)} custom-call(bf16[2,64,256]{2,1,0:T(8,128)(2,1)} %copy-done.1, bf16[32,152,128]{2,1,0:T(8,128)(2,1)} %pack.1.in_ref), custom_call_target="tpu_custom_call", output_to_operand_aliasing={{}: (1, {})} | custom-call | tf_op jit(solution)/shard_map/pack_other/pallas_call | solution.py:226
  12.3 8.5 %all-to-all-start = ((bf16[32,152,128]{2,1,0:T(8,128)(2,1)}), bf16[32,152,128]{2,1,0:T(8,128)(2,1)S(1)}, u32[]{:S(2)}, u32[]{:S(2)}) async-start(bf16[32,152,128]{2,1,0:T(8,128)(2,1)} %pack_other.1), calls=%async_computation | async-start | bytes 2490368 | tf_op jit(solution)/shard_map/all_to_all | solution.py:235
  20.8 0.1 constant_dynamic-slice_fusion.2
  21.0 0.2 copy.25
  21.1 0.2 copy.26
  21.3 0.9 pad_maximum_fusion.2
  22.2 3.1 %collective-permute-start.1 = (bf16[2,128,1024]{1,2,0:T(8,128)(2,1)}, bf16[2,128,1024]{1,2,0:T(8,128)(2,1)S(1)}, u32[]{:S(2)}, u32[]{:S(2)}) collective-permute-start(bf16[2,128,1024]{1,2,0:T(8,128)(2,1)} %pad_maximum_fusion.2), channel_id=1, source_target_pairs={{0,128},{128,0},{1,129},{129,1},{2,130},{130,2},{3,131},{131,3},{4... | collective-permute-start | bytes 1572872 | tf_op jit(solution)/shard_map/ppermute | solution.py:202
  25.6 0.1 fusion.18
  25.6 0.1 slice.26
  25.7 0.1 reshape.114
  25.8 0.1 concatenate.24
  26.0 0.1 concatenate.23
  26.1 0.1 concatenate.22
  26.2 0.1 convert_reduce_fusion
  26.3 0.1 select_reduce_fusion
  26.4 0.1 concatenate.25
  26.5 0.1 broadcast_in_dim.20
  26.6 0.1 convert_element_type.38.qlow_ref
  26.7 0.1 broadcast_in_dim.18
  26.8 0.1 convert_element_type.35.qpos_ref
  26.9 0.2 copy.24
  27.1 0.2 copy.23
  27.3 18.9 %collective-permute-done.1 = bf16[2,128,1024]{1,2,0:T(8,128)(2,1)S(1)} collective-permute-done((bf16[2,128,1024]{1,2,0:T(8,128)(2,1)}, bf16[2,128,1024]{1,2,0:T(8,128)(2,1)S(1)}, u32[]{:S(2)}, u32[]{:S(2)}) %collective-permute-start.1) | collective-permute-done | bytes 524320 | tf_op jit(solution)/shard_map/ppermute | solution.py:202
  46.2 6.6 %attend.1 = bf16[32,112,128]{2,1,0:T(8,128)(2,1)} custom-call(bf16[32,152,128]{2,1,0:T(8,128)(2,1)S(1)} %all-to-all-done.in_ref, f32[1,1280]{1,0:T(1,128)S(1)} %add_convert_fusion.1.kpos_ref, f32[1,1024]{1,0:T(1,128)S(1)} %convert_element_type.35.qpos_ref, f32[1,1024]{1,0:T(1,128)S(1)} %convert_element_type.38.qlow_ref), custom_call_target="tpu_custom_call" | custom-call | tf_op jit(solution)/shard_map/attend/pallas_call | solution.py:253
  52.8 8.6 %all-to-all-start.1 = ((bf16[32,112,128]{2,1,0:T(8,128)(2,1)}), bf16[32,112,128]{2,1,0:T(8,128)(2,1)S(1)}, u32[]{:S(2)}, u32[]{:S(2)}) async-start(bf16[32,112,128]{2,1,0:T(8,128)(2,1)} %attend.1), calls=%async_computation.1 | async-start | bytes 1835008 | tf_op jit(solution)/shard_map/all_to_all | solution.py:268
  61.5 0.1 pad_maximum_fusion
  61.6 3.1 %collective-permute-start.2 = (bf16[2,2,128,1024]{2,3,1,0:T(8,128)(2,1)S(1)}, bf16[2,2,128,1024]{2,3,1,0:T(8,128)(2,1)S(1)}, u32[]{:S(2)}, u32[]{:S(2)}) collective-permute-start(bf16[2,2,128,1024]{2,3,1,0:T(8,128)(2,1)S(1)} %pad_maximum_fusion), channel_id=1, source_target_pairs={{0,1},{1,0},{2,3},{3,2},{4,5},{5,4},{6,7},{7,6},{8,9},{9,8},{10,11... | collective-permute-start | bytes 3145736 | tf_op jit(solution)/shard_map/ppermute | solution.py:202
  64.7 2.3 %collective-permute-done.2 = bf16[2,2,128,1024]{2,3,1,0:T(8,128)(2,1)S(1)} collective-permute-done((bf16[2,2,128,1024]{2,3,1,0:T(8,128)(2,1)S(1)}, bf16[2,2,128,1024]{2,3,1,0:T(8,128)(2,1)S(1)}, u32[]{:S(2)}, u32[]{:S(2)}) %collective-permute-start.2) | collective-permute-done | bytes 1048608 | tf_op jit(solution)/shard_map/ppermute | solution.py:202
  67.0 8.3 %all-to-all-done.1.in_ref = bf16[32,112,128]{2,1,0:T(8,128)(2,1)S(1)} async-done(((bf16[32,112,128]{2,1,0:T(8,128)(2,1)}), bf16[32,112,128]{2,1,0:T(8,128)(2,1)S(1)}, u32[]{:S(2)}, u32[]{:S(2)}) %all-to-all-start.1) | async-done | bytes 917536 | tf_op jit(solution)/shard_map/all_to_all | solution.py:268
  75.2 1.0 collect.1
  76.3 4.9 %collective-permute-start.3 = (bf16[2,128,128]{2,1,0:T(8,128)(2,1)S(1)}, bf16[2,128,128]{2,1,0:T(8,128)(2,1)S(1)}, u32[]{:S(2)}, u32[]{:S(2)}) collective-permute-start(bf16[2,128,128]{2,1,0:T(8,128)(2,1)S(1)} %get-tuple-element.16), channel_id=1, source_target_pairs={{0,64},{64,0},{1,65},{65,1},{2,66},{66,2},{3,67},{67,3},{4,68},{68... | collective-permute-start | bytes 196616 | tf_op jit(solution)/shard_map/ppermute | solution.py:202
  81.2 2.3 %collective-permute-done.3 = bf16[2,128,128]{2,1,0:T(8,128)(2,1)S(1)} collective-permute-done((bf16[2,128,128]{2,1,0:T(8,128)(2,1)S(1)}, bf16[2,128,128]{2,1,0:T(8,128)(2,1)S(1)}, u32[]{:S(2)}, u32[]{:S(2)}) %collective-permute-start.3) | collective-permute-done | bytes 65568 | tf_op jit(solution)/shard_map/ppermute | solution.py:202
  83.5 0.7 broadcast_in_dim.21
  84.2 5.7 %all-to-all-start.2 = ((bf16[4,128,128]{2,1,0:T(8,128)(2,1)}), bf16[4,128,128]{2,1,0:T(8,128)(2,1)S(1)}, u32[]{:S(2)}, u32[]{:S(2)}) async-start(bf16[4,128,128]{2,1,0:T(8,128)(2,1)} %bitcast.10), calls=%async_computation.2 | async-start | bytes 262144 | tf_op jit(solution)/shard_map/all_to_all | solution.py:293
  89.9 3.6 %all-to-all-done.2 = bf16[4,128,128]{2,1,0:T(8,128)(2,1)S(1)} async-done(((bf16[4,128,128]{2,1,0:T(8,128)(2,1)}), bf16[4,128,128]{2,1,0:T(8,128)(2,1)S(1)}, u32[]{:S(2)}, u32[]{:S(2)}) %all-to-all-start.2) | async-done | bytes 131104 | tf_op jit(solution)/shard_map/all_to_all | solution.py:293
  93.5 0.3 fusion.10
  93.8 0.3 fusion.3
  94.1 0.3 fusion.5
  94.3 0.3 fusion.2
  94.6 23.2 %all_to_all.25 = bf16[32,64,128]{2,1,0:T(8,128)(2,1)S(1)} all-to-all(bf16[32,64,128]{2,1,0:T(8,128)(2,1)S(1)} %bitcast.41), channel_id=1, replica_groups=mesh['xu'=2,'xd'=2,'zu'=2,'zd'=2,'y'=4,'zh'=4,'core'=2] {'xu','zu','zd',..., dimensions={0} | all-to-all | bytes 1048576 | tf_op jit(solution)/shard_map/all_to_all | solution.py:304
  117.9 0.1 reduce_sum.31
  118.0 23.4 %all_to_all.26 = bf16[4,64,128]{2,1,0:T(8,128)(2,1)S(1)} all-to-all(bf16[4,64,128]{2,1,0:T(8,128)(2,1)S(1)} %broadcast_in_dim.22), channel_id=1, replica_groups=mesh['xu'=2,'xd'=2,'zu'=2,'zd'=2,'y'=4,'zh'=4,'core'=2] {'zh'}, dimensions={0} | all-to-all | bytes 131072 | tf_op jit(solution)/shard_map/all_to_all | solution.py:306
  141.3 5.5 %all_gather.3 = f32[64,256]{1,0:T(8,128)S(1)} all-gather(f32[64,128]{1,0:T(8,128)S(1)} %convert_reduce_fusion.1), channel_id=1, replica_groups=mesh['xu'=2,'xd'=2,'zu'=2,'zd'=2,'y'=4,'zh'=4,'core'=2] {'core'}, dimensions={1}, use_global_device_ids=true | all-gather | bytes 98304 | tf_op jit(solution)/shard_map/all_gather | solution.py:308
  146.8 0.6 copy.29
  (19 shorter events, 0.3 us)
Async XLA Ops:
  1.4 8.3 %collective-permute-start = (bf16[2,64,256]{2,1,0:T(8,128)(2,1)S(1)}, bf16[2,64,256]{2,1,0:T(8,128)(2,1)S(1)}, u32[]{:S(2)}, u32[]{:S(2)}) collective-permute-start(bf16[2,64,256]{2,1,0:T(8,128)(2,1)S(1)} %pad_maximum_fusion.3), channel_id=1, source_target_pairs={{0,64},{64,0},{1,65},{65,1},{2,66},{66,2},{3,67},{67,3},{4,68},{68... | collective-permute-start | bytes 196616 | tf_op jit(solution)/shard_map/ppermute | solution.py:202
  9.7 0.6 copy-start.1
  12.3 8.6 %copy-start = (bf16[2,64,4096]{2,1,0:T(8,128)(2,1)S(1)}, bf16[2,64,4096]{2,1,0:T(8,128)(2,1)}, u32[]{:S(2)}) copy-start(bf16[2,64,4096]{2,1,0:T(8,128)(2,1)} %param.8) | copy-start | bytes 3145732
  12.3 33.9 %all-to-all-start = ((bf16[32,152,128]{2,1,0:T(8,128)(2,1)}), bf16[32,152,128]{2,1,0:T(8,128)(2,1)S(1)}, u32[]{:S(2)}, u32[]{:S(2)}) async-start(bf16[32,152,128]{2,1,0:T(8,128)(2,1)} %pack_other.1), calls=%async_computation | async-start | bytes 2490368 | tf_op jit(solution)/shard_map/all_to_all | solution.py:235
  20.9 4.4 %copy-start.2 = (s32[2,4096]{1,0:T(2,128)S(1)}, s32[2,4096]{1,0:T(2,128)}, u32[]{:S(2)}) copy-start(s32[2,4096]{1,0:T(2,128)} %param.15) | copy-start | bytes 98308
  21.0 4.4 %copy-start.3 = (s32[2,4096]{1,0:T(2,128)S(1)}, s32[2,4096]{1,0:T(2,128)}, u32[]{:S(2)}) copy-start(s32[2,4096]{1,0:T(2,128)} %param.14) | copy-start | bytes 98308
  22.2 24.0 %collective-permute-start.1 = (bf16[2,128,1024]{1,2,0:T(8,128)(2,1)}, bf16[2,128,1024]{1,2,0:T(8,128)(2,1)S(1)}, u32[]{:S(2)}, u32[]{:S(2)}) collective-permute-start(bf16[2,128,1024]{1,2,0:T(8,128)(2,1)} %pad_maximum_fusion.2), channel_id=1, source_target_pairs={{0,128},{128,0},{1,129},{129,1},{2,130},{130,2},{3,131},{131,3},{4... | collective-permute-start | bytes 1572872 | tf_op jit(solution)/shard_map/ppermute | solution.py:202
  52.8 22.4 %all-to-all-start.1 = ((bf16[32,112,128]{2,1,0:T(8,128)(2,1)}), bf16[32,112,128]{2,1,0:T(8,128)(2,1)S(1)}, u32[]{:S(2)}, u32[]{:S(2)}) async-start(bf16[32,112,128]{2,1,0:T(8,128)(2,1)} %attend.1), calls=%async_computation.1 | async-start | bytes 1835008 | tf_op jit(solution)/shard_map/all_to_all | solution.py:268
  61.6 5.4 %collective-permute-start.2 = (bf16[2,2,128,1024]{2,3,1,0:T(8,128)(2,1)S(1)}, bf16[2,2,128,1024]{2,3,1,0:T(8,128)(2,1)S(1)}, u32[]{:S(2)}, u32[]{:S(2)}) collective-permute-start(bf16[2,2,128,1024]{2,3,1,0:T(8,128)(2,1)S(1)} %pad_maximum_fusion), channel_id=1, source_target_pairs={{0,1},{1,0},{2,3},{3,2},{4,5},{5,4},{6,7},{7,6},{8,9},{9,8},{10,11... | collective-permute-start | bytes 3145736 | tf_op jit(solution)/shard_map/ppermute | solution.py:202
  76.3 7.2 %collective-permute-start.3 = (bf16[2,128,128]{2,1,0:T(8,128)(2,1)S(1)}, bf16[2,128,128]{2,1,0:T(8,128)(2,1)S(1)}, u32[]{:S(2)}, u32[]{:S(2)}) collective-permute-start(bf16[2,128,128]{2,1,0:T(8,128)(2,1)S(1)} %get-tuple-element.16), channel_id=1, source_target_pairs={{0,64},{64,0},{1,65},{65,1},{2,66},{66,2},{3,67},{67,3},{4,68},{68... | collective-permute-start | bytes 196616 | tf_op jit(solution)/shard_map/ppermute | solution.py:202
  84.2 9.3 %all-to-all-start.2 = ((bf16[4,128,128]{2,1,0:T(8,128)(2,1)}), bf16[4,128,128]{2,1,0:T(8,128)(2,1)S(1)}, u32[]{:S(2)}, u32[]{:S(2)}) async-start(bf16[4,128,128]{2,1,0:T(8,128)(2,1)} %bitcast.10), calls=%async_computation.2 | async-start | bytes 262144 | tf_op jit(solution)/shard_map/all_to_all | solution.py:293

commit v8 on v6

--- a/solution.py
+++ b/solution.py
@@ -234,7 +234,7 @@
         name="pack_other",
     )(other, sent)
     arrived = lax.all_to_all(sent, peers, 0, 0, tiled=True)
-    arrived, *columns = lax.optimization_barrier((arrived, *columns))
+    arrived, columns[2] = lax.optimization_barrier((arrived, columns[2]))
     columns[2] = along_x(2)
 
     docs = lax.dynamic_index_in_dim(doc_ids, sequence, 0, keepdims=False)
@@ -267,10 +267,10 @@
         compiler_params=pltpu.CompilerParams(vmem_limit_bytes=48 << 20),
         name="attend",
     )(arrived, kpos.astype(F32), qpos.astype(F32), qlow.astype(F32))
+    back, columns[1], columns[3] = lax.optimization_barrier((back, columns[1], columns[3]))
     home = lax.all_to_all(back, peers, 0, 0, tiled=True)
     twin = other_core(jnp.stack([columns[0], columns[1], columns[3]]))
-    home, twin, columns[2] = lax.optimization_barrier((home, twin, columns[2]))
-    twin = [twin[0], twin[1], other_core(columns[2]), twin[2]]
+    home, twin = lax.optimization_barrier((home, twin))
 
     query_grad, near_grad, far_grad = pl.pallas_call(
         collect_kernel,
@@ -290,7 +290,10 @@
         compiler_params=pltpu.CompilerParams(vmem_limit_bytes=32 << 20),
         name="collect",
     )(home)
-    kv_grad = (near_grad + lax.ppermute(far_grad, "zu", [(0, 1), (1, 0)])).astype(BF)
+    far_grad = lax.ppermute(far_grad, "zu", [(0, 1), (1, 0)])
+    far_grad, columns[2] = lax.optimization_barrier((far_grad, columns[2]))
+    twin = [twin[0], twin[1], other_core(columns[2]), twin[2]]
+    kv_grad = (near_grad + far_grad).astype(BF)
 
     kv_grad = jnp.broadcast_to(kv_grad[None], (4, 2, 2 * ROWS, HD))
     grads = lax.all_to_all(
@@ -308,9 +311,11 @@
     part = part.reshape(16, 64, HD).astype(BF)
     part = lax.all_to_all(part, ("zu", "zd", "y"), 0, 0, tiled=True)
     part = jnp.sum(part.astype(F32), axis=0).astype(BF)
-    part = lax.all_to_all(jnp.broadcast_to(part[None], (4, 64, HD)), "zh", 0, 0, tiled=True)
-    part = jnp.sum(part.astype(F32), axis=0)
-    weight_grad = lax.all_gather(part, "core", axis=1, tiled=True)
+    part = lax.all_to_all(
+        jnp.broadcast_to(part[None], (8, 64, HD)), ("zh", "core"), 0, 0, tiled=True
+    )
+    part = jnp.sum(part.reshape(4, 2, 64, HD).astype(F32), axis=0)
+    weight_grad = part.transpose(1, 0, 2).reshape(64, 2 * HD)
     return (query_grad, weight_grad)
 
 

time: 144 us -> 135 us (0.938)
  the two profiles are of different devices: /device:TPU:1 before, /device:TPU:32 now
where the time goes in v8:
time: 135 us; the launch traced here: 134 us
  blocking collectives  44.2 us (33%)
  starting transfers between devices  44 us (33%)
  waiting for transfers between devices  22.1 us (16%)
  Pallas kernels  12.1 us (9%)
  matrix products  4.92 us (4%)
  local copies, waits for them, and re-layouts  4.14 us (3%)
    all_to_all x1, blocking collectives, local(): lax.all_to_all(jnp.broadcast_to(part[None], (8, 64, HD)), ('zh', 'core'),...  27.9 us
    all_to_all x1, blocking collectives, local(): part = lax.all_to_all(part, ('zu', 'zd', 'y'), 0, 0, tiled=True)  16.3 us
    ppermute x3, starting transfers between devices, along_x(): lax.ppermute(columns[step], 'x', [(i, (i + step) % 4) for i in range(4)])  11.9 us
    all_to_all x1, starting transfers between devices, local(): arrived = lax.all_to_all(sent, peers, 0, 0, tiled=True)  8.69 us
    all_to_all x1, waiting for transfers between devices, local(): arrived = lax.all_to_all(sent, peers, 0, 0, tiled=True)  8.2 us
    pallas_call x1, Pallas kernels, local(): pl.pallas_call(attend_kernel, out_shape=jax.ShapeDtypeStruct((PEERS, BACK...  6.63 us
    all_to_all x1, waiting for transfers between devices, local(): home = lax.all_to_all(back, peers, 0, 0, tiled=True)  6.51 us
    all_to_all x1, starting transfers between devices, local(): home = lax.all_to_all(back, peers, 0, 0, tiled=True)  5.71 us
  transfers between devices with their start and end apart: 10, of which 4 were waited for; matrix products, arithmetic and copies ran while one was open for 5% of the time, Pallas kernels for 8%

profile of v8, /device:TPU:32, one launch (start us, length us, event | category | flops | bytes accessed | tf_op | source)
XLA Modules:
  0.0 133.8 jit_solution(10005087156500227617)
XLA Ops:
  0.6 0.8 pad_maximum_fusion.1
  1.4 5.2 %collective-permute-start = (bf16[2,64,256]{2,1,0:T(8,128)(2,1)S(1)}, bf16[2,64,256]{2,1,0:T(8,128)(2,1)S(1)}, u32[]{:S(2)}, u32[]{:S(2)}) collective-permute-start(bf16[2,64,256]{2,1,0:T(8,128)(2,1)S(1)} %pad_maximum_fusion.1), channel_id=1, source_target_pairs={{0,64},{64,0},{1,65},{65,1},{2,66},{66,2},{3,67},{67,3},{4,68},{68... | collective-permute-start | bytes 196616 | tf_op jit(solution)/shard_map/ppermute | solution.py:214
  6.6 2.6 %pack.1.in_ref = bf16[32,152,128]{2,1,0:T(8,128)(2,1)} custom-call(bf16[2,64,1024]{2,1,0:T(8,128)(2,1)} %q_ref.1, bf16[2,64,1024]{2,1,0:T(8,128)(2,1)} %g_ref.1, bf16[2,64,1024]{2,1,0:T(8,128)(2,1)} %o_ref.1, bf16[2,64,128]{2,1,0:T(8,128)(2,1)} %k_ref.1, bf16[2,64,128]{2,1,0:T(8,128)(2,1)} %v_ref.1), custom_call_target="tpu_custom_call" | custom-call | tf_op jit(solution)/shard_map/pack/pallas_call | solution.py:217
  9.2 0.6 copy-done.1
  9.8 1.8 %pack_other.1 = bf16[32,152,128]{2,1,0:T(8,128)(2,1)} custom-call(bf16[2,64,256]{2,1,0:T(8,128)(2,1)} %copy-done.1, bf16[32,152,128]{2,1,0:T(8,128)(2,1)} %pack.1.in_ref), custom_call_target="tpu_custom_call", output_to_operand_aliasing={{}: (1, {})} | custom-call | tf_op jit(solution)/shard_map/pack_other/pallas_call | solution.py:227
  11.7 8.7 %all-to-all-start = ((bf16[32,152,128]{2,1,0:T(8,128)(2,1)}), bf16[32,152,128]{2,1,0:T(8,128)(2,1)S(1)}, u32[]{:S(2)}, u32[]{:S(2)}) async-start(bf16[32,152,128]{2,1,0:T(8,128)(2,1)} %pack_other.1), calls=%async_computation | async-start | bytes 2490368 | tf_op jit(solution)/shard_map/all_to_all | solution.py:236
  20.5 0.9 dynamic-slice_bitcast_fusion
  21.4 3.4 %collective-permute-start.1 = (bf16[128,1024]{1,0:T(8,128)(2,1)}, bf16[128,1024]{1,0:T(8,128)(2,1)S(1)}, u32[]{:S(2)}, u32[]{:S(2)}) collective-permute-start(bf16[128,1024]{1,0:T(8,128)(2,1)} %get-tuple-element.28), channel_id=1, source_target_pairs={{0,128},{128,256},{256,384},{384,0},{1,129},{129,257},{257,385},{3... | collective-permute-start | bytes 786440 | tf_op jit(solution)/shard_map/ppermute | solution.py:206
  24.7 3.7 %collective-permute-start.2 = (bf16[128,1024]{1,0:T(8,128)(2,1)}, bf16[128,1024]{1,0:T(8,128)(2,1)S(1)}, u32[]{:S(2)}, u32[]{:S(2)}) collective-permute-start(bf16[128,1024]{1,0:T(8,128)(2,1)} %get-tuple-element.27), channel_id=1, source_target_pairs={{0,384},{128,0},{256,128},{384,256},{1,385},{129,1},{257,129},{385... | collective-permute-start | bytes 786440 | tf_op jit(solution)/shard_map/ppermute | solution.py:206
  28.6 0.1 fusion.33
  28.7 0.1 slice.30
  28.8 0.1 reshape.120
  28.9 0.1 convert_reduce_fusion.1
  29.0 0.1 select_reduce_fusion
  29.1 0.1 concatenate.24
  29.2 0.1 slice.31
  29.3 0.1 concatenate.25
  29.4 0.1 concatenate.22
  29.5 0.1 concatenate.23
  29.6 0.1 broadcast_in_dim.20
  29.7 0.1 convert_element_type.41.qlow_ref
  29.8 0.1 broadcast_in_dim.18
  29.9 0.1 convert_element_type.38.qpos_ref
  30.0 8.2 %all-to-all-done.in_ref = bf16[32,152,128]{2,1,0:T(8,128)(2,1)S(1)} async-done(((bf16[32,152,128]{2,1,0:T(8,128)(2,1)}), bf16[32,152,128]{2,1,0:T(8,128)(2,1)S(1)}, u32[]{:S(2)}, u32[]{:S(2)}) %all-to-all-start) | async-done | bytes 1245216 | tf_op jit(solution)/shard_map/all_to_all | solution.py:236
  38.2 6.6 %attend.1 = bf16[32,112,128]{2,1,0:T(8,128)(2,1)} custom-call(bf16[32,152,128]{2,1,0:T(8,128)(2,1)S(1)} %all-to-all-done.in_ref, f32[1,1280]{1,0:T(1,128)S(1)} %add_convert_fusion.1.kpos_ref, f32[1,1024]{1,0:T(1,128)S(1)} %convert_element_type.38.qpos_ref, f32[1,1024]{1,0:T(1,128)S(1)} %convert_element_type.41.qlow_ref), custom_call_target="tpu_custom_call" | custom-call | tf_op jit(solution)/shard_map/attend/pallas_call | solution.py:255
  44.8 5.7 %all-to-all-start.1 = ((bf16[32,112,128]{2,1,0:T(8,128)(2,1)}), bf16[32,112,128]{2,1,0:T(8,128)(2,1)S(1)}, u32[]{:S(2)}, u32[]{:S(2)}) async-start(bf16[32,112,128]{2,1,0:T(8,128)(2,1)} %attend.1), calls=%async_computation.1 | async-start | bytes 1835008 | tf_op jit(solution)/shard_map/all_to_all | solution.py:271
  50.5 0.1 pad_maximum_fusion
  50.6 1.9 %collective-permute-start.3 = (bf16[3,128,1024]{2,1,0:T(8,128)(2,1)S(1)}, bf16[3,128,1024]{2,1,0:T(8,128)(2,1)}, u32[]{:S(2)}, u32[]{:S(2)}) collective-permute-start(bf16[3,128,1024]{2,1,0:T(8,128)(2,1)S(1)} %pad_maximum_fusion), channel_id=1, source_target_pairs={{0,1},{1,0},{2,3},{3,2},{4,5},{5,4},{6,7},{7,6},{8,9},{9,8},{10,11... | collective-permute-start | bytes 2359304 | tf_op jit(solution)/shard_map/ppermute | solution.py:209
  52.6 4.9 %collective-permute-start.5 = (bf16[128,1024]{1,0:T(8,128)(2,1)S(1)}, bf16[128,1024]{1,0:T(8,128)(2,1)S(1)}, u32[]{:S(2)}, u32[]{:S(2)}) collective-permute-start(bf16[128,1024]{1,0:T(8,128)(2,1)S(1)} %get-tuple-element.22), channel_id=1, source_target_pairs={{0,256},{128,384},{256,0},{384,128},{1,257},{129,385},{257,1},{385... | collective-permute-start | bytes 786440 | tf_op jit(solution)/shard_map/ppermute | solution.py:206
  57.5 6.5 %all-to-all-done.1.in_ref = bf16[32,112,128]{2,1,0:T(8,128)(2,1)S(1)} async-done(((bf16[32,112,128]{2,1,0:T(8,128)(2,1)}), bf16[32,112,128]{2,1,0:T(8,128)(2,1)S(1)}, u32[]{:S(2)}, u32[]{:S(2)}) %all-to-all-start.1) | async-done | bytes 917536 | tf_op jit(solution)/shard_map/all_to_all | solution.py:271
  64.0 1.0 collect.1
  65.0 5.0 %collective-permute-start.4 = (bf16[2,128,128]{2,1,0:T(8,128)(2,1)S(1)}, bf16[2,128,128]{2,1,0:T(8,128)(2,1)S(1)}, u32[]{:S(2)}, u32[]{:S(2)}) collective-permute-start(bf16[2,128,128]{2,1,0:T(8,128)(2,1)S(1)} %get-tuple-element.21), channel_id=1, source_target_pairs={{0,64},{64,0},{1,65},{65,1},{2,66},{66,2},{3,67},{67,3},{4,68},{68... | collective-permute-start | bytes 196616 | tf_op jit(solution)/shard_map/ppermute | solution.py:293
  70.0 2.2 %collective-permute-done.4 = bf16[2,128,128]{2,1,0:T(8,128)(2,1)S(1)} collective-permute-done((bf16[2,128,128]{2,1,0:T(8,128)(2,1)S(1)}, bf16[2,128,128]{2,1,0:T(8,128)(2,1)S(1)}, u32[]{:S(2)}, u32[]{:S(2)}) %collective-permute-start.4) | collective-permute-done | bytes 65568 | tf_op jit(solution)/shard_map/ppermute | solution.py:293
  72.2 0.7 broadcast_in_dim.21
  73.0 3.4 %all-to-all-start.2 = ((bf16[8,128,128]{2,1,0:T(8,128)(2,1)}), bf16[8,128,128]{2,1,0:T(8,128)(2,1)S(1)}, u32[]{:S(2)}, u32[]{:S(2)}) async-start(bf16[8,128,128]{2,1,0:T(8,128)(2,1)} %bitcast.7), calls=%async_computation.2 | async-start | bytes 524288 | tf_op jit(solution)/shard_map/all_to_all | solution.py:299
  76.5 2.2 %collective-permute-start.6 = (bf16[128,1024]{1,0:T(8,128)(2,1)S(1)}, bf16[128,1024]{1,0:T(8,128)(2,1)S(1)}, u32[]{:S(2)}, u32[]{:S(2)}) collective-permute-start(bf16[128,1024]{1,0:T(8,128)(2,1)S(1)} %collective-permute-done.5), channel_id=1, source_target_pairs={{0,1},{1,0},{2,3},{3,2},{4,5},{5,4},{6,7},{7,6},{8,9},{9,8},{10,11... | collective-permute-start | bytes 786440 | tf_op jit(solution)/shard_map/ppermute | solution.py:209
  78.7 5.1 %all-to-all-done.2 = bf16[8,128,128]{2,1,0:T(8,128)(2,1)S(1)} async-done(((bf16[8,128,128]{2,1,0:T(8,128)(2,1)}), bf16[8,128,128]{2,1,0:T(8,128)(2,1)S(1)}, u32[]{:S(2)}, u32[]{:S(2)}) %all-to-all-start.2) | async-done | bytes 262176 | tf_op jit(solution)/shard_map/all_to_all | solution.py:299
  83.9 0.2 fusion.13
  84.1 0.3 fusion.16
  84.4 1.2 fusion.7
  85.6 1.2 fusion.5
  86.8 1.2 convolution_add_fusion.2
  88.0 0.3 fusion
  88.3 0.3 fusion.18
  88.5 0.3 fusion.4
  88.8 16.3 %all_to_all.25 = bf16[16,64,128]{2,1,0:T(8,128)(2,1)S(1)} all-to-all(bf16[16,64,128]{2,1,0:T(8,128)(2,1)S(1)} %bitcast.61), channel_id=1, replica_groups=mesh['x'=4,'zu'=2,'zd'=2,'y'=4,'zh'=4,'core'=2] {'zu','zd','y'}, dimensions={0} | all-to-all | bytes 524288 | tf_op jit(solution)/shard_map/all_to_all | solution.py:312
  105.2 27.9 %all_to_all.26 = bf16[8,64,128]{2,1,0:T(8,128)(2,1)S(1)} all-to-all(bf16[8,64,128]{2,1,0:T(8,128)(2,1)S(1)} %broadcast_in_dim.22), channel_id=1, replica_groups=mesh['x'=4,'zu'=2,'zd'=2,'y'=4,'zh'=4,'core'=2] {'zh','core'}, dimensions={0} | all-to-all | bytes 262144 | tf_op jit(solution)/shard_map/all_to_all | solution.py:314
  133.1 0.6 copy_bitcast_fusion
  (22 shorter events, 0.3 us)
Async XLA Ops:
  1.4 7.8 %collective-permute-start = (bf16[2,64,256]{2,1,0:T(8,128)(2,1)S(1)}, bf16[2,64,256]{2,1,0:T(8,128)(2,1)S(1)}, u32[]{:S(2)}, u32[]{:S(2)}) collective-permute-start(bf16[2,64,256]{2,1,0:T(8,128)(2,1)S(1)} %pad_maximum_fusion.1), channel_id=1, source_target_pairs={{0,64},{64,0},{1,65},{65,1},{2,66},{66,2},{3,67},{67,3},{4,68},{68... | collective-permute-start | bytes 196616 | tf_op jit(solution)/shard_map/ppermute | solution.py:214
  9.2 0.6 copy-start.1
  11.7 8.8 %copy-start = (bf16[2,64,4096]{2,1,0:T(8,128)(2,1)S(1)}, bf16[2,64,4096]{2,1,0:T(8,128)(2,1)}, u32[]{:S(2)}) copy-start(bf16[2,64,4096]{2,1,0:T(8,128)(2,1)} %param.8) | copy-start | bytes 3145732
  11.7 26.5 %all-to-all-start = ((bf16[32,152,128]{2,1,0:T(8,128)(2,1)}), bf16[32,152,128]{2,1,0:T(8,128)(2,1)S(1)}, u32[]{:S(2)}, u32[]{:S(2)}) async-start(bf16[32,152,128]{2,1,0:T(8,128)(2,1)} %pack_other.1), calls=%async_computation | async-start | bytes 2490368 | tf_op jit(solution)/shard_map/all_to_all | solution.py:236
  20.4 8.1 %copy-start.2 = (s32[2,4096]{1,0:T(2,128)S(1)}, s32[2,4096]{1,0:T(2,128)}, u32[]{:S(2)}) copy-start(s32[2,4096]{1,0:T(2,128)} %param.15) | copy-start | bytes 98308
  20.4 8.1 %copy-start.3 = (s32[2,4096]{1,0:T(2,128)S(1)}, s32[2,4096]{1,0:T(2,128)}, u32[]{:S(2)}) copy-start(s32[2,4096]{1,0:T(2,128)} %param.14) | copy-start | bytes 98308
  21.4 23.5 %collective-permute-start.1 = (bf16[128,1024]{1,0:T(8,128)(2,1)}, bf16[128,1024]{1,0:T(8,128)(2,1)S(1)}, u32[]{:S(2)}, u32[]{:S(2)}) collective-permute-start(bf16[128,1024]{1,0:T(8,128)(2,1)} %get-tuple-element.28), channel_id=1, source_target_pairs={{0,128},{128,256},{256,384},{384,0},{1,129},{129,257},{257,385},{3... | collective-permute-start | bytes 786440 | tf_op jit(solution)/shard_map/ppermute | solution.py:206
  24.7 20.1 %collective-permute-start.2 = (bf16[128,1024]{1,0:T(8,128)(2,1)}, bf16[128,1024]{1,0:T(8,128)(2,1)S(1)}, u32[]{:S(2)}, u32[]{:S(2)}) collective-permute-start(bf16[128,1024]{1,0:T(8,128)(2,1)} %get-tuple-element.27), channel_id=1, source_target_pairs={{0,384},{128,0},{256,128},{384,256},{1,385},{129,1},{257,129},{385... | collective-permute-start | bytes 786440 | tf_op jit(solution)/shard_map/ppermute | solution.py:206
  44.8 19.2 %all-to-all-start.1 = ((bf16[32,112,128]{2,1,0:T(8,128)(2,1)}), bf16[32,112,128]{2,1,0:T(8,128)(2,1)S(1)}, u32[]{:S(2)}, u32[]{:S(2)}) async-start(bf16[32,112,128]{2,1,0:T(8,128)(2,1)} %attend.1), calls=%async_computation.1 | async-start | bytes 1835008 | tf_op jit(solution)/shard_map/all_to_all | solution.py:271
  50.6 6.8 %collective-permute-start.3 = (bf16[3,128,1024]{2,1,0:T(8,128)(2,1)S(1)}, bf16[3,128,1024]{2,1,0:T(8,128)(2,1)}, u32[]{:S(2)}, u32[]{:S(2)}) collective-permute-start(bf16[3,128,1024]{2,1,0:T(8,128)(2,1)S(1)} %pad_maximum_fusion), channel_id=1, source_target_pairs={{0,1},{1,0},{2,3},{3,2},{4,5},{5,4},{6,7},{7,6},{8,9},{9,8},{10,11... | collective-permute-start | bytes 2359304 | tf_op jit(solution)/shard_map/ppermute | solution.py:209
  52.6 17.4 %collective-permute-start.5 = (bf16[128,1024]{1,0:T(8,128)(2,1)S(1)}, bf16[128,1024]{1,0:T(8,128)(2,1)S(1)}, u32[]{:S(2)}, u32[]{:S(2)}) collective-permute-start(bf16[128,1024]{1,0:T(8,128)(2,1)S(1)} %get-tuple-element.22), channel_id=1, source_target_pairs={{0,256},{128,384},{256,0},{384,128},{1,257},{129,385},{257,1},{385... | collective-permute-start | bytes 786440 | tf_op jit(solution)/shard_map/ppermute | solution.py:206
  65.0 7.2 %collective-permute-start.4 = (bf16[2,128,128]{2,1,0:T(8,128)(2,1)S(1)}, bf16[2,128,128]{2,1,0:T(8,128)(2,1)S(1)}, u32[]{:S(2)}, u32[]{:S(2)}) collective-permute-start(bf16[2,128,128]{2,1,0:T(8,128)(2,1)S(1)} %get-tuple-element.21), channel_id=1, source_target_pairs={{0,64},{64,0},{1,65},{65,1},{2,66},{66,2},{3,67},{67,3},{4,68},{68... | collective-permute-start | bytes 196616 | tf_op jit(solution)/shard_map/ppermute | solution.py:293
  73.0 10.9 %all-to-all-start.2 = ((bf16[8,128,128]{2,1,0:T(8,128)(2,1)}), bf16[8,128,128]{2,1,0:T(8,128)(2,1)S(1)}, u32[]{:S(2)}, u32[]{:S(2)}) async-start(bf16[8,128,128]{2,1,0:T(8,128)(2,1)} %bitcast.7), calls=%async_computation.2 | async-start | bytes 524288 | tf_op jit(solution)/shard_map/all_to_all | solution.py:299
  76.5 11.8 %collective-permute-start.6 = (bf16[128,1024]{1,0:T(8,128)(2,1)S(1)}, bf16[128,1024]{1,0:T(8,128)(2,1)S(1)}, u32[]{:S(2)}, u32[]{:S(2)}) collective-permute-start(bf16[128,1024]{1,0:T(8,128)(2,1)S(1)} %collective-permute-done.5), channel_id=1, source_target_pairs={{0,1},{1,0},{2,3},{3,2},{4,5},{5,4},{6,7},{7,6},{8,9},{9,8},{10,11... | collective-permute-start | bytes 786440 | tf_op jit(solution)/shard_map/ppermute | solution.py:209

commit v9 on v8

--- a/solution.py
+++ b/solution.py
@@ -223,16 +223,18 @@
         scratch_shapes=[pltpu.VMEM((ROWS * HEADS, HD), F32)],
         name="pack",
     )(queries, out_grad, attn_output, key_states, value_states)
-    hbm = pl.BlockSpec(memory_space=pl.ANY)
+    hbm = pl.BlockSpec(memory_space=pltpu.HBM)
     sent = pl.pallas_call(
         pack_other_kernel,
         out_shape=jax.ShapeDtypeStruct((PEERS, SEND, HD), BF),
-        in_specs=[pl.BlockSpec(memory_space=pltpu.VMEM), hbm],
+        in_specs=[whole((2, ROWS, 2 * HD)), hbm],
         out_specs=hbm,
         scratch_shapes=[pltpu.VMEM((PEERS, 40, HD), BF), pltpu.SemaphoreType.DMA(())],
         input_output_aliases={1: 0},
+        grid=(1,),
+        compiler_params=pltpu.CompilerParams(vmem_limit_bytes=8 << 20),
         name="pack_other",
-    )(other, sent)
+    )(other, pltpu.with_memory_space_constraint(sent, pltpu.HBM))
     arrived = lax.all_to_all(sent, peers, 0, 0, tiled=True)
     arrived, columns[2] = lax.optimization_barrier((arrived, columns[2]))
     columns[2] = along_x(2)
@@ -264,13 +266,16 @@
             pltpu.VMEM((KN, HD), F32),
             pltpu.VMEM((KN, HD), F32),
         ],
-        compiler_params=pltpu.CompilerParams(vmem_limit_bytes=48 << 20),
+        compiler_params=pltpu.CompilerParams(vmem_limit_bytes=24 << 20),
         name="attend",
     )(arrived, kpos.astype(F32), qpos.astype(F32), qlow.astype(F32))
-    back, columns[1], columns[3] = lax.optimization_barrier((back, columns[1], columns[3]))
+    first_twin = other_core(columns[0])
+    back, columns[1], columns[3], first_twin = lax.optimization_barrier(
+        (back, columns[1], columns[3], first_twin)
+    )
     home = lax.all_to_all(back, peers, 0, 0, tiled=True)
-    twin = other_core(jnp.stack([columns[0], columns[1], columns[3]]))
-    home, twin = lax.optimization_barrier((home, twin))
+    twin = [first_twin, other_core(columns[1]), other_core(columns[3])]
+    home, *twin = lax.optimization_barrier((home, *twin))
 
     query_grad, near_grad, far_grad = pl.pallas_call(
         collect_kernel,
@@ -287,7 +292,7 @@
             whole((2, 2 * ROWS, HD)),
         ),
         scratch_shapes=[pltpu.VMEM((GROUPS * 32, HD), F32)],
-        compiler_params=pltpu.CompilerParams(vmem_limit_bytes=32 << 20),
+        compiler_params=pltpu.CompilerParams(vmem_limit_bytes=8 << 20),
         name="collect",
     )(home)
     far_grad = lax.ppermute(far_grad, "zu", [(0, 1), (1, 0)])

time: 135 us -> 131 us (0.970)
  waiting for transfers between devices: 22.1 us -> 17.5 us
  starting transfers between devices: 44 us -> 48.2 us
  matrix products: 4.92 us -> 3.05 us
    ppermute x2 -> x4, starting transfers between devices: 4.12 us -> 8.57 us  [other_core(): return lax.ppermute(x, 'core', [(0, 1), (1, 0)])]
    all_to_all x1, waiting for transfers between devices: 6.51 us -> 2.57 us  [local(): home = lax.all_to_all(back, peers, 0, 0, tiled=True)]
    dot_general x8, matrix products: 4.92 us -> 3.05 us  [local(): lax.dot_general(piece, grad, (((0,), (0,)), ((), ())), preferred_element_...]
  transfers between devices with their start and end apart: 10 -> 12, of which waited for: 4 -> 4; matrix products, arithmetic and copies ran while one was open for 5% -> 2% of each run, Pallas kernels for 8% -> 8%
where the time goes in v9:
time: 131 us; the launch traced here: 130 us
  starting transfers between devices  48.2 us (37%)
  blocking collectives  44.6 us (34%)
  waiting for transfers between devices  17.5 us (13%)
  Pallas kernels  11.3 us (9%)
  local copies, waits for them, and re-layouts  3.42 us (3%)
  matrix products  3.05 us (2%)
    all_to_all x1, blocking collectives, local(): lax.all_to_all(jnp.broadcast_to(part[None], (8, 64, HD)), ('zh', 'core'),...  28.5 us
    all_to_all x1, blocking collectives, local(): part = lax.all_to_all(part, ('zu', 'zd', 'y'), 0, 0, tiled=True)  16.1 us
    ppermute x3, starting transfers between devices, along_x(): lax.ppermute(columns[step], 'x', [(i, (i + step) % 4) for i in range(4)])  11.5 us
    all_to_all x1, starting transfers between devices, local(): arrived = lax.all_to_all(sent, peers, 0, 0, tiled=True)  8.69 us
    ppermute x4, starting transfers between devices, other_core(): return lax.ppermute(x, 'core', [(0, 1), (1, 0)])  8.57 us
    all_to_all x1, waiting for transfers between devices, local(): arrived = lax.all_to_all(sent, peers, 0, 0, tiled=True)  7.54 us
    pallas_call x1, Pallas kernels, local(): pl.pallas_call(attend_kernel, out_shape=jax.ShapeDtypeStruct((PEERS, BACK...  6.61 us
    all_to_all x1, starting transfers between devices, local(): home = lax.all_to_all(back, peers, 0, 0, tiled=True)  5.72 us
  transfers between devices with their start and end apart: 12, of which 4 were waited for; matrix products, arithmetic and copies ran while one was open for 2% of the time, Pallas kernels for 8%

profile of v9, /device:TPU:32, one launch (start us, length us, event | category | flops | bytes accessed | tf_op | source)
XLA Modules:
  0.0 130.3 jit_solution(17481218772292122781)
XLA Ops:
  0.6 0.8 pad_maximum_fusion
  1.4 5.2 %collective-permute-start = (bf16[2,64,256]{2,1,0:T(8,128)(2,1)S(1)}, bf16[2,64,256]{2,1,0:T(8,128)(2,1)S(1)}, u32[]{:S(2)}, u32[]{:S(2)}) collective-permute-start(bf16[2,64,256]{2,1,0:T(8,128)(2,1)S(1)} %pad_maximum_fusion), channel_id=1, source_target_pairs={{0,64},{64,0},{1,65},{65,1},{2,66},{66,2},{3,67},{67,3},{4,68},{68... | collective-permute-start | bytes 196616 | tf_op jit(solution)/shard_map/ppermute | solution.py:214
  6.6 2.6 %pack.1.in_ref = bf16[32,152,128]{2,1,0:T(8,128)(2,1)} custom-call(bf16[2,64,1024]{2,1,0:T(8,128)(2,1)} %q_ref.1, bf16[2,64,1024]{2,1,0:T(8,128)(2,1)} %g_ref.1, bf16[2,64,1024]{2,1,0:T(8,128)(2,1)} %o_ref.1, bf16[2,64,128]{2,1,0:T(8,128)(2,1)} %k_ref.1, bf16[2,64,128]{2,1,0:T(8,128)(2,1)} %v_ref.1), custom_call_target="tpu_custom_call" | custom-call | tf_op jit(solution)/shard_map/pack/pallas_call | solution.py:217
  9.2 1.0 pack_other.1
  10.2 8.7 %all-to-all-start = ((bf16[32,152,128]{2,1,0:T(8,128)(2,1)}), bf16[32,152,128]{2,1,0:T(8,128)(2,1)S(1)}, u32[]{:S(2)}, u32[]{:S(2)}) async-start(bf16[32,152,128]{2,1,0:T(8,128)(2,1)} %pack_other.1), calls=%async_computation | async-start | bytes 2490368 | tf_op jit(solution)/shard_map/all_to_all | solution.py:238
  19.0 0.1 constant_dynamic-slice_fusion
  19.1 4.7 %collective-permute-start.2 = (bf16[128,1024]{1,0:T(8,128)(2,1)S(1)}, bf16[128,1024]{1,0:T(8,128)(2,1)S(1)}, u32[]{:S(2)}, u32[]{:S(2)}) collective-permute-start(bf16[128,1024]{1,0:T(8,128)(2,1)S(1)} %get-tuple-element.33), channel_id=1, source_target_pairs={{0,384},{128,0},{256,128},{384,256},{1,385},{129,1},{257,129},{385... | collective-permute-start | bytes 786440 | tf_op jit(solution)/shard_map/ppermute | solution.py:206
  23.8 1.9 %collective-permute-start.1 = (bf16[128,1024]{1,0:T(8,128)(2,1)S(1)}, bf16[128,1024]{1,0:T(8,128)(2,1)S(1)}, u32[]{:S(2)}, u32[]{:S(2)}) collective-permute-start(bf16[128,1024]{1,0:T(8,128)(2,1)S(1)} %get-tuple-element.34), channel_id=1, source_target_pairs={{0,128},{128,256},{256,384},{384,0},{1,129},{129,257},{257,385},{3... | collective-permute-start | bytes 786440 | tf_op jit(solution)/shard_map/ppermute | solution.py:206
  25.7 1.9 %collective-permute-start.3 = (bf16[128,1024]{1,0:T(8,128)(2,1)S(1)}, bf16[128,1024]{1,0:T(8,128)(2,1)S(1)}, u32[]{:S(2)}, u32[]{:S(2)}) collective-permute-start(bf16[128,1024]{1,0:T(8,128)(2,1)S(1)} %get-tuple-element.32), channel_id=1, source_target_pairs={{0,1},{1,0},{2,3},{3,2},{4,5},{5,4},{6,7},{7,6},{8,9},{9,8},{10,11... | collective-permute-start | bytes 786440 | tf_op jit(solution)/shard_map/ppermute | solution.py:209
  27.8 0.1 fusion.28
  27.9 0.1 slice.18
  28.0 0.1 reshape.120
  28.1 0.1 convert_reduce_fusion.1
  28.3 0.1 select_reduce_fusion
  28.4 0.1 concatenate.24
  28.5 0.1 concatenate.23
  28.6 0.1 concatenate.22
  28.7 0.1 concatenate.25
  28.8 0.1 broadcast_in_dim.20
  28.9 0.1 convert_element_type.41.qlow_ref
  29.0 0.1 broadcast_in_dim.18
  29.1 0.1 convert_element_type.38.qpos_ref
  29.2 7.5 %all-to-all-done.in_ref = bf16[32,152,128]{2,1,0:T(8,128)(2,1)S(1)} async-done(((bf16[32,152,128]{2,1,0:T(8,128)(2,1)}), bf16[32,152,128]{2,1,0:T(8,128)(2,1)S(1)}, u32[]{:S(2)}, u32[]{:S(2)}) %all-to-all-start) | async-done | bytes 1245216 | tf_op jit(solution)/shard_map/all_to_all | solution.py:238
  36.7 6.6 %attend.1 = bf16[32,112,128]{2,1,0:T(8,128)(2,1)} custom-call(bf16[32,152,128]{2,1,0:T(8,128)(2,1)S(1)} %all-to-all-done.in_ref, f32[1,1280]{1,0:T(1,128)S(1)} %add_convert_fusion.1.kpos_ref, f32[1,1024]{1,0:T(1,128)S(1)} %convert_element_type.38.qpos_ref, f32[1,1024]{1,0:T(1,128)S(1)} %convert_element_type.41.qlow_ref), custom_call_target="tpu_custom_call" | custom-call | tf_op jit(solution)/shard_map/attend/pallas_call | solution.py:257
  43.4 5.7 %all-to-all-start.1 = ((bf16[32,112,128]{2,1,0:T(8,128)(2,1)}), bf16[32,112,128]{2,1,0:T(8,128)(2,1)S(1)}, u32[]{:S(2)}, u32[]{:S(2)}) async-start(bf16[32,112,128]{2,1,0:T(8,128)(2,1)} %attend.1), calls=%async_computation.1 | async-start | bytes 1835008 | tf_op jit(solution)/shard_map/all_to_all | solution.py:276
  49.1 1.9 %collective-permute-start.4 = (bf16[128,1024]{1,0:T(8,128)(2,1)S(1)}, bf16[128,1024]{1,0:T(8,128)(2,1)S(1)}, u32[]{:S(2)}, u32[]{:S(2)}) collective-permute-start(bf16[128,1024]{1,0:T(8,128)(2,1)S(1)} %collective-permute-done.1), channel_id=1, source_target_pairs={{0,1},{1,0},{2,3},{3,2},{4,5},{5,4},{6,7},{7,6},{8,9},{9,8},{10,11... | collective-permute-start | bytes 786440 | tf_op jit(solution)/shard_map/ppermute | solution.py:209
  51.0 2.4 %collective-permute-start.5 = (bf16[128,1024]{1,0:T(8,128)(2,1)S(1)}, bf16[128,1024]{1,0:T(8,128)(2,1)S(1)}, u32[]{:S(2)}, u32[]{:S(2)}) collective-permute-start(bf16[128,1024]{1,0:T(8,128)(2,1)S(1)} %collective-permute-done.2), channel_id=1, source_target_pairs={{0,1},{1,0},{2,3},{3,2},{4,5},{5,4},{6,7},{7,6},{8,9},{9,8},{10,11... | collective-permute-start | bytes 786440 | tf_op jit(solution)/shard_map/ppermute | solution.py:209
  53.4 4.9 %collective-permute-start.7 = (bf16[128,1024]{1,0:T(8,128)(2,1)S(1)}, bf16[128,1024]{1,0:T(8,128)(2,1)S(1)}, u32[]{:S(2)}, u32[]{:S(2)}) collective-permute-start(bf16[128,1024]{1,0:T(8,128)(2,1)S(1)} %get-tuple-element.26), channel_id=1, source_target_pairs={{0,256},{128,384},{256,0},{384,128},{1,257},{129,385},{257,1},{385... | collective-permute-start | bytes 786440 | tf_op jit(solution)/shard_map/ppermute | solution.py:206
  58.4 0.7 copy-done.1
  59.1 2.6 %all-to-all-done.1.in_ref = bf16[32,112,128]{2,1,0:T(8,128)(2,1)S(1)} async-done(((bf16[32,112,128]{2,1,0:T(8,128)(2,1)}), bf16[32,112,128]{2,1,0:T(8,128)(2,1)S(1)}, u32[]{:S(2)}, u32[]{:S(2)}) %all-to-all-start.1) | async-done | bytes 917536 | tf_op jit(solution)/shard_map/all_to_all | solution.py:276
  61.7 1.0 collect.1
  62.7 5.2 %collective-permute-start.6 = (bf16[2,128,128]{2,1,0:T(8,128)(2,1)S(1)}, bf16[2,128,128]{2,1,0:T(8,128)(2,1)S(1)}, u32[]{:S(2)}, u32[]{:S(2)}) collective-permute-start(bf16[2,128,128]{2,1,0:T(8,128)(2,1)S(1)} %get-tuple-element.25), channel_id=1, source_target_pairs={{0,64},{64,0},{1,65},{65,1},{2,66},{66,2},{3,67},{67,3},{4,68},{68... | collective-permute-start | bytes 196616 | tf_op jit(solution)/shard_map/ppermute | solution.py:298
  67.9 2.3 %collective-permute-done.6 = bf16[2,128,128]{2,1,0:T(8,128)(2,1)S(1)} collective-permute-done((bf16[2,128,128]{2,1,0:T(8,128)(2,1)S(1)}, bf16[2,128,128]{2,1,0:T(8,128)(2,1)S(1)}, u32[]{:S(2)}, u32[]{:S(2)}) %collective-permute-start.6) | collective-permute-done | bytes 65568 | tf_op jit(solution)/shard_map/ppermute | solution.py:298
  70.2 0.7 broadcast_in_dim.21
  71.0 3.4 %all-to-all-start.2 = ((bf16[8,128,128]{2,1,0:T(8,128)(2,1)}), bf16[8,128,128]{2,1,0:T(8,128)(2,1)S(1)}, u32[]{:S(2)}, u32[]{:S(2)}) async-start(bf16[8,128,128]{2,1,0:T(8,128)(2,1)} %bitcast.4), calls=%async_computation.2 | async-start | bytes 524288 | tf_op jit(solution)/shard_map/all_to_all | solution.py:304
  74.5 2.3 %collective-permute-start.8 = (bf16[128,1024]{1,0:T(8,128)(2,1)S(1)}, bf16[128,1024]{1,0:T(8,128)(2,1)}, u32[]{:S(2)}, u32[]{:S(2)}) collective-permute-start(bf16[128,1024]{1,0:T(8,128)(2,1)S(1)} %collective-permute-done.7), channel_id=1, source_target_pairs={{0,1},{1,0},{2,3},{3,2},{4,5},{5,4},{6,7},{7,6},{8,9},{9,8},{10,11... | collective-permute-start | bytes 786440 | tf_op jit(solution)/shard_map/ppermute | solution.py:209
  76.8 5.0 %all-to-all-done.2 = bf16[8,128,128]{2,1,0:T(8,128)(2,1)S(1)} async-done(((bf16[8,128,128]{2,1,0:T(8,128)(2,1)}), bf16[8,128,128]{2,1,0:T(8,128)(2,1)S(1)}, u32[]{:S(2)}, u32[]{:S(2)}) %all-to-all-start.2) | async-done | bytes 262176 | tf_op jit(solution)/shard_map/all_to_all | solution.py:304
  81.8 0.2 fusion.8
  82.1 0.2 fusion.18
  82.4 0.3 fusion.12
  82.6 0.3 fusion.6
  82.9 0.3 fusion.14
  83.1 0.3 convolution_add_fusion.1
  83.4 1.2 fusion.10
  84.6 0.3 fusion.5
  85.0 16.1 %all_to_all.25 = bf16[16,64,128]{2,1,0:T(8,128)(2,1)S(1)} all-to-all(bf16[16,64,128]{2,1,0:T(8,128)(2,1)S(1)} %bitcast.51), channel_id=1, replica_groups=mesh['x'=4,'zu'=2,'zd'=2,'y'=4,'zh'=4,'core'=2] {'zu','zd','y'}, dimensions={0} | all-to-all | bytes 524288 | tf_op jit(solution)/shard_map/all_to_all | solution.py:317
  101.1 28.5 %all_to_all.26 = bf16[8,64,128]{2,1,0:T(8,128)(2,1)S(1)} all-to-all(bf16[8,64,128]{2,1,0:T(8,128)(2,1)S(1)} %broadcast_in_dim.22), channel_id=1, replica_groups=mesh['x'=4,'zu'=2,'zd'=2,'y'=4,'zh'=4,'core'=2] {'zh','core'}, dimensions={0} | all-to-all | bytes 262144 | tf_op jit(solution)/shard_map/all_to_all | solution.py:319
  129.6 0.6 copy_bitcast_fusion
  (27 shorter events, 0.4 us)
Async XLA Ops:
  1.4 7.7 %collective-permute-start = (bf16[2,64,256]{2,1,0:T(8,128)(2,1)S(1)}, bf16[2,64,256]{2,1,0:T(8,128)(2,1)S(1)}, u32[]{:S(2)}, u32[]{:S(2)}) collective-permute-start(bf16[2,64,256]{2,1,0:T(8,128)(2,1)S(1)} %pad_maximum_fusion), channel_id=1, source_target_pairs={{0,64},{64,0},{1,65},{65,1},{2,66},{66,2},{3,67},{67,3},{4,68},{68... | collective-permute-start | bytes 196616 | tf_op jit(solution)/shard_map/ppermute | solution.py:214
  10.2 8.8 %copy-start = (bf16[2,64,4096]{2,1,0:T(8,128)(2,1)S(1)}, bf16[2,64,4096]{2,1,0:T(8,128)(2,1)}, u32[]{:S(2)}) copy-start(bf16[2,64,4096]{2,1,0:T(8,128)(2,1)} %param.8) | copy-start | bytes 3145732
  10.2 26.5 %all-to-all-start = ((bf16[32,152,128]{2,1,0:T(8,128)(2,1)}), bf16[32,152,128]{2,1,0:T(8,128)(2,1)S(1)}, u32[]{:S(2)}, u32[]{:S(2)}) async-start(bf16[32,152,128]{2,1,0:T(8,128)(2,1)} %pack_other.1), calls=%async_computation | async-start | bytes 2490368 | tf_op jit(solution)/shard_map/all_to_all | solution.py:238
  18.9 8.8 %copy-start.3 = (s32[2,4096]{1,0:T(2,128)S(1)}, s32[2,4096]{1,0:T(2,128)}, u32[]{:S(2)}) copy-start(s32[2,4096]{1,0:T(2,128)} %param.15) | copy-start | bytes 98308
  18.9 8.8 %copy-start.4 = (s32[2,4096]{1,0:T(2,128)S(1)}, s32[2,4096]{1,0:T(2,128)}, u32[]{:S(2)}) copy-start(s32[2,4096]{1,0:T(2,128)} %param.14) | copy-start | bytes 98308
  19.1 24.2 %collective-permute-start.2 = (bf16[128,1024]{1,0:T(8,128)(2,1)S(1)}, bf16[128,1024]{1,0:T(8,128)(2,1)S(1)}, u32[]{:S(2)}, u32[]{:S(2)}) collective-permute-start(bf16[128,1024]{1,0:T(8,128)(2,1)S(1)} %get-tuple-element.33), channel_id=1, source_target_pairs={{0,384},{128,0},{256,128},{384,256},{1,385},{129,1},{257,129},{385... | collective-permute-start | bytes 786440 | tf_op jit(solution)/shard_map/ppermute | solution.py:206
  23.8 19.6 %collective-permute-start.1 = (bf16[128,1024]{1,0:T(8,128)(2,1)S(1)}, bf16[128,1024]{1,0:T(8,128)(2,1)S(1)}, u32[]{:S(2)}, u32[]{:S(2)}) collective-permute-start(bf16[128,1024]{1,0:T(8,128)(2,1)S(1)} %get-tuple-element.34), channel_id=1, source_target_pairs={{0,128},{128,256},{256,384},{384,0},{1,129},{129,257},{257,385},{3... | collective-permute-start | bytes 786440 | tf_op jit(solution)/shard_map/ppermute | solution.py:206
  25.7 17.6 %collective-permute-start.3 = (bf16[128,1024]{1,0:T(8,128)(2,1)S(1)}, bf16[128,1024]{1,0:T(8,128)(2,1)S(1)}, u32[]{:S(2)}, u32[]{:S(2)}) collective-permute-start(bf16[128,1024]{1,0:T(8,128)(2,1)S(1)} %get-tuple-element.32), channel_id=1, source_target_pairs={{0,1},{1,0},{2,3},{3,2},{4,5},{5,4},{6,7},{7,6},{8,9},{9,8},{10,11... | collective-permute-start | bytes 786440 | tf_op jit(solution)/shard_map/ppermute | solution.py:209
  43.4 18.3 %all-to-all-start.1 = ((bf16[32,112,128]{2,1,0:T(8,128)(2,1)}), bf16[32,112,128]{2,1,0:T(8,128)(2,1)S(1)}, u32[]{:S(2)}, u32[]{:S(2)}) async-start(bf16[32,112,128]{2,1,0:T(8,128)(2,1)} %attend.1), calls=%async_computation.1 | async-start | bytes 1835008 | tf_op jit(solution)/shard_map/all_to_all | solution.py:276
  49.1 9.2 %collective-permute-start.4 = (bf16[128,1024]{1,0:T(8,128)(2,1)S(1)}, bf16[128,1024]{1,0:T(8,128)(2,1)S(1)}, u32[]{:S(2)}, u32[]{:S(2)}) collective-permute-start(bf16[128,1024]{1,0:T(8,128)(2,1)S(1)} %collective-permute-done.1), channel_id=1, source_target_pairs={{0,1},{1,0},{2,3},{3,2},{4,5},{5,4},{6,7},{7,6},{8,9},{9,8},{10,11... | collective-permute-start | bytes 786440 | tf_op jit(solution)/shard_map/ppermute | solution.py:209
  51.0 7.3 %collective-permute-start.5 = (bf16[128,1024]{1,0:T(8,128)(2,1)S(1)}, bf16[128,1024]{1,0:T(8,128)(2,1)S(1)}, u32[]{:S(2)}, u32[]{:S(2)}) collective-permute-start(bf16[128,1024]{1,0:T(8,128)(2,1)S(1)} %collective-permute-done.2), channel_id=1, source_target_pairs={{0,1},{1,0},{2,3},{3,2},{4,5},{5,4},{6,7},{7,6},{8,9},{9,8},{10,11... | collective-permute-start | bytes 786440 | tf_op jit(solution)/shard_map/ppermute | solution.py:209
  53.4 14.4 %collective-permute-start.7 = (bf16[128,1024]{1,0:T(8,128)(2,1)S(1)}, bf16[128,1024]{1,0:T(8,128)(2,1)S(1)}, u32[]{:S(2)}, u32[]{:S(2)}) collective-permute-start(bf16[128,1024]{1,0:T(8,128)(2,1)S(1)} %get-tuple-element.26), channel_id=1, source_target_pairs={{0,256},{128,384},{256,0},{384,128},{1,257},{129,385},{257,1},{385... | collective-permute-start | bytes 786440 | tf_op jit(solution)/shard_map/ppermute | solution.py:206
  58.4 0.7 copy-start.1
  62.7 7.5 %collective-permute-start.6 = (bf16[2,128,128]{2,1,0:T(8,128)(2,1)S(1)}, bf16[2,128,128]{2,1,0:T(8,128)(2,1)S(1)}, u32[]{:S(2)}, u32[]{:S(2)}) collective-permute-start(bf16[2,128,128]{2,1,0:T(8,128)(2,1)S(1)} %get-tuple-element.25), channel_id=1, source_target_pairs={{0,64},{64,0},{1,65},{65,1},{2,66},{66,2},{3,67},{67,3},{4,68},{68... | collective-permute-start | bytes 196616 | tf_op jit(solution)/shard_map/ppermute | solution.py:298
  71.0 10.9 %all-to-all-start.2 = ((bf16[8,128,128]{2,1,0:T(8,128)(2,1)}), bf16[8,128,128]{2,1,0:T(8,128)(2,1)S(1)}, u32[]{:S(2)}, u32[]{:S(2)}) async-start(bf16[8,128,128]{2,1,0:T(8,128)(2,1)} %bitcast.4), calls=%async_computation.2 | async-start | bytes 524288 | tf_op jit(solution)/shard_map/all_to_all | solution.py:304
  74.5 8.2 %copy-start.2 = (bf16[128,1024]{1,0:T(8,128)(2,1)S(1)}, bf16[128,1024]{1,0:T(8,128)(2,1)}, u32[]{:S(2)}) copy-start(bf16[128,1024]{1,0:T(8,128)(2,1)} %copy-done.1) | copy-start | bytes 786436
  74.5 8.9 %collective-permute-start.8 = (bf16[128,1024]{1,0:T(8,128)(2,1)S(1)}, bf16[128,1024]{1,0:T(8,128)(2,1)}, u32[]{:S(2)}, u32[]{:S(2)}) collective-permute-start(bf16[128,1024]{1,0:T(8,128)(2,1)S(1)} %collective-permute-done.7), channel_id=1, source_target_pairs={{0,1},{1,0},{2,3},{3,2},{4,5},{5,4},{6,7},{7,6},{8,9},{9,8},{10,11... | collective-permute-start | bytes 786440 | tf_op jit(solution)/shard_map/ppermute | solution.py:209

commit v10 on v9

--- a/solution.py
+++ b/solution.py
@@ -182,6 +182,12 @@
             q_ref[s, :, h * HD : (h + 1) * HD] = split[pl.ds(h, ROWS, stride=HEADS), :].astype(BF)
 
 
+def spread_kernel(near_ref, far_ref, out_ref):
+    total = (near_ref[...] + far_ref[...].astype(F32)).astype(BF)
+    for copy in range(4):
+        out_ref[2 * copy : 2 * copy + 2] = total
+
+
 def whole(shape):
     return pl.BlockSpec(shape, lambda *_: (0,) * len(shape))
 
@@ -208,7 +214,6 @@
     def other_core(x):
         return lax.ppermute(x, "core", [(0, 1), (1, 0)])
 
-    columns[1], columns[3] = along_x(1), along_x(3)
 
     row_spec = lambda width: pl.BlockSpec((1, ROWS, width), lambda s: (s, 0, 0))
     other = lax.ppermute(
@@ -253,6 +258,11 @@
     low = jnp.max(jnp.where(starts[:, None] <= own[None, :], starts[:, None], 0), axis=0)
     qpos = jnp.repeat(own, HEADS)[None, :]
     qlow = jnp.repeat(low, HEADS)[None, :]
+    kpos, qpos, qlow = kpos.astype(F32), qpos.astype(F32), qlow.astype(F32)
+    kpos, qlow, columns[0], columns[1], columns[3] = lax.optimization_barrier(
+        (kpos, qlow, columns[0], columns[1], columns[3])
+    )
+    columns[1], columns[3] = along_x(1), along_x(3)
 
     back = pl.pallas_call(
         attend_kernel,
@@ -266,9 +276,9 @@
             pltpu.VMEM((KN, HD), F32),
             pltpu.VMEM((KN, HD), F32),
         ],
-        compiler_params=pltpu.CompilerParams(vmem_limit_bytes=24 << 20),
+        compiler_params=pltpu.CompilerParams(vmem_limit_bytes=16 << 20),
         name="attend",
-    )(arrived, kpos.astype(F32), qpos.astype(F32), qlow.astype(F32))
+    )(arrived, kpos, qpos, qlow)
     first_twin = other_core(columns[0])
     back, columns[1], columns[3], first_twin = lax.optimization_barrier(
         (back, columns[1], columns[3], first_twin)
@@ -298,12 +308,16 @@
     far_grad = lax.ppermute(far_grad, "zu", [(0, 1), (1, 0)])
     far_grad, columns[2] = lax.optimization_barrier((far_grad, columns[2]))
     twin = [twin[0], twin[1], other_core(columns[2]), twin[2]]
-    kv_grad = (near_grad + far_grad).astype(BF)
-
-    kv_grad = jnp.broadcast_to(kv_grad[None], (4, 2, 2 * ROWS, HD))
-    grads = lax.all_to_all(
-        kv_grad.reshape(8, 2 * ROWS, HD), ("x", "core"), 0, 0, tiled=True
-    )
+    kv_grad = pl.pallas_call(
+        spread_kernel,
+        out_shape=jax.ShapeDtypeStruct((8, 2 * ROWS, HD), BF),
+        grid=(1,),
+        in_specs=[whole((2, 2 * ROWS, HD)), whole((2, 2 * ROWS, HD))],
+        out_specs=whole((8, 2 * ROWS, HD)),
+        compiler_params=pltpu.CompilerParams(vmem_limit_bytes=4 << 20),
+        name="spread",
+    )(near_grad, far_grad)
+    grads = lax.all_to_all(kv_grad, ("x", "core"), 0, 0, tiled=True)
     part = jnp.zeros((quarter, HD), F32)
     for step in range(4):
         for piece, at in ((columns[step], core), (twin[step], 1 - core)):

time: 131 us -> 131 us (level)
  no operation moved by 1% of the time
where the time goes in v10:
time: 131 us; the launch traced here: 130 us
  starting transfers between devices  48.6 us (37%)
  blocking collectives  44.7 us (34%)
  waiting for transfers between devices  16.9 us (13%)
  Pallas kernels  12 us (9%)
  matrix products  3.07 us (2%)
  local copies, waits for them, and re-layouts  2.68 us (2%)
    all_to_all x1, blocking collectives, local(): lax.all_to_all(jnp.broadcast_to(part[None], (8, 64, HD)), ('zh', 'core'),...  28.6 us
    all_to_all x1, blocking collectives, local(): part = lax.all_to_all(part, ('zu', 'zd', 'y'), 0, 0, tiled=True)  16.1 us
    ppermute x3, starting transfers between devices, along_x(): lax.ppermute(columns[step], 'x', [(i, (i + step) % 4) for i in range(4)])  11.9 us
    all_to_all x1, starting transfers between devices, local(): arrived = lax.all_to_all(sent, peers, 0, 0, tiled=True)  8.69 us
    ppermute x4, starting transfers between devices, other_core(): return lax.ppermute(x, 'core', [(0, 1), (1, 0)])  8.57 us
    all_to_all x1, waiting for transfers between devices, local(): arrived = lax.all_to_all(sent, peers, 0, 0, tiled=True)  7.06 us
    pallas_call x1, Pallas kernels, local(): pl.pallas_call(attend_kernel, out_shape=jax.ShapeDtypeStruct((PEERS, BACK...  6.61 us
    all_to_all x1, starting transfers between devices, local(): home = lax.all_to_all(back, peers, 0, 0, tiled=True)  5.73 us
  transfers between devices with their start and end apart: 12, of which 4 were waited for; matrix products, arithmetic and copies ran while one was open for 2% of the time, Pallas kernels for 8%

profile of v10, /device:TPU:32, one launch (start us, length us, event | category | flops | bytes accessed | tf_op | source)
XLA Modules:
  0.0 130.3 jit_solution(10901155116451996966)
XLA Ops:
  0.6 0.8 pad_maximum_fusion
  1.4 5.2 %collective-permute-start = (bf16[2,64,256]{2,1,0:T(8,128)(2,1)S(1)}, bf16[2,64,256]{2,1,0:T(8,128)(2,1)S(1)}, u32[]{:S(2)}, u32[]{:S(2)}) collective-permute-start(bf16[2,64,256]{2,1,0:T(8,128)(2,1)S(1)} %pad_maximum_fusion), channel_id=1, source_target_pairs={{0,64},{64,0},{1,65},{65,1},{2,66},{66,2},{3,67},{67,3},{4,68},{68... | collective-permute-start | bytes 196616 | tf_op jit(solution)/shard_map/ppermute | solution.py:219
  6.6 2.6 %pack.1.in_ref = bf16[32,152,128]{2,1,0:T(8,128)(2,1)} custom-call(bf16[2,64,1024]{2,1,0:T(8,128)(2,1)} %q_ref.1, bf16[2,64,1024]{2,1,0:T(8,128)(2,1)} %g_ref.1, bf16[2,64,1024]{2,1,0:T(8,128)(2,1)} %o_ref.1, bf16[2,64,128]{2,1,0:T(8,128)(2,1)} %k_ref.1, bf16[2,64,128]{2,1,0:T(8,128)(2,1)} %v_ref.1), custom_call_target="tpu_custom_call" | custom-call | tf_op jit(solution)/shard_map/pack/pallas_call | solution.py:222
  9.2 1.0 pack_other.1
  10.3 8.7 %all-to-all-start = ((bf16[32,152,128]{2,1,0:T(8,128)(2,1)}), bf16[32,152,128]{2,1,0:T(8,128)(2,1)S(1)}, u32[]{:S(2)}, u32[]{:S(2)}) async-start(bf16[32,152,128]{2,1,0:T(8,128)(2,1)} %pack_other.1), calls=%async_computation | async-start | bytes 2490368 | tf_op jit(solution)/shard_map/all_to_all | solution.py:243
  19.2 0.1 fusion.28
  19.3 0.1 slice.18
  19.4 0.1 le.16
  19.5 0.1 concatenate.24
  19.7 0.1 concatenate.23
  19.7 0.1 concatenate.22
  19.8 0.2 convert_reduce_fusion.1
  20.0 0.1 select_reduce_fusion
  20.1 0.1 concatenate.25
  20.2 0.1 broadcast_in_dim.17
  20.3 0.1 convert_element_type.51.qlow_ref
  20.4 0.1 constant_dynamic-slice_fusion
  20.5 3.4 %collective-permute-start.1 = (bf16[128,1024]{1,0:T(8,128)(2,1)S(1)}, bf16[128,1024]{1,0:T(8,128)(2,1)S(1)}, u32[]{:S(2)}, u32[]{:S(2)}) collective-permute-start(bf16[128,1024]{1,0:T(8,128)(2,1)S(1)} %get-tuple-element.25), channel_id=1, source_target_pairs={{0,128},{128,256},{256,384},{384,0},{1,129},{129,257},{257,385},{3... | collective-permute-start | bytes 786440 | tf_op jit(solution)/shard_map/ppermute | solution.py:212
  23.9 3.7 %collective-permute-start.2 = (bf16[128,1024]{1,0:T(8,128)(2,1)S(1)}, bf16[128,1024]{1,0:T(8,128)(2,1)S(1)}, u32[]{:S(2)}, u32[]{:S(2)}) collective-permute-start(bf16[128,1024]{1,0:T(8,128)(2,1)S(1)} %get-tuple-element.26), channel_id=1, source_target_pairs={{0,384},{128,0},{256,128},{384,256},{1,385},{129,1},{257,129},{385... | collective-permute-start | bytes 786440 | tf_op jit(solution)/shard_map/ppermute | solution.py:212
  27.6 1.9 %collective-permute-start.3 = (bf16[128,1024]{1,0:T(8,128)(2,1)S(1)}, bf16[128,1024]{1,0:T(8,128)(2,1)S(1)}, u32[]{:S(2)}, u32[]{:S(2)}) collective-permute-start(bf16[128,1024]{1,0:T(8,128)(2,1)S(1)} %get-tuple-element.27), channel_id=1, source_target_pairs={{0,1},{1,0},{2,3},{3,2},{4,5},{5,4},{6,7},{7,6},{8,9},{9,8},{10,11... | collective-permute-start | bytes 786440 | tf_op jit(solution)/shard_map/ppermute | solution.py:215
  29.5 0.1 broadcast_in_dim.18
  29.6 0.1 convert_element_type.53.qpos_ref
  29.7 7.1 %all-to-all-done.in_ref = bf16[32,152,128]{2,1,0:T(8,128)(2,1)S(1)} async-done(((bf16[32,152,128]{2,1,0:T(8,128)(2,1)}), bf16[32,152,128]{2,1,0:T(8,128)(2,1)S(1)}, u32[]{:S(2)}, u32[]{:S(2)}) %all-to-all-start) | async-done | bytes 1245216 | tf_op jit(solution)/shard_map/all_to_all | solution.py:243
  36.8 6.6 %attend.1 = bf16[32,112,128]{2,1,0:T(8,128)(2,1)} custom-call(bf16[32,152,128]{2,1,0:T(8,128)(2,1)S(1)} %all-to-all-done.in_ref, f32[1,1280]{1,0:T(1,128)S(1)} %add_convert_fusion.kpos_ref, f32[1,1024]{1,0:T(1,128)S(1)} %convert_element_type.53.qpos_ref, f32[1,1024]{1,0:T(1,128)S(1)} %convert_element_type.51.qlow_ref), custom_call_target="tpu_custom_call" | custom-call | tf_op jit(solution)/shard_map/attend/pallas_call | solution.py:267
  43.4 5.7 %all-to-all-start.1 = ((bf16[32,112,128]{2,1,0:T(8,128)(2,1)}), bf16[32,112,128]{2,1,0:T(8,128)(2,1)S(1)}, u32[]{:S(2)}, u32[]{:S(2)}) async-start(bf16[32,112,128]{2,1,0:T(8,128)(2,1)} %attend.1), calls=%async_computation.1 | async-start | bytes 1835008 | tf_op jit(solution)/shard_map/all_to_all | solution.py:286
  49.1 1.9 %collective-permute-start.4 = (bf16[128,1024]{1,0:T(8,128)(2,1)S(1)}, bf16[128,1024]{1,0:T(8,128)(2,1)S(1)}, u32[]{:S(2)}, u32[]{:S(2)}) collective-permute-start(bf16[128,1024]{1,0:T(8,128)(2,1)S(1)} %collective-permute-done.1), channel_id=1, source_target_pairs={{0,1},{1,0},{2,3},{3,2},{4,5},{5,4},{6,7},{7,6},{8,9},{9,8},{10,11... | collective-permute-start | bytes 786440 | tf_op jit(solution)/shard_map/ppermute | solution.py:215
  51.1 2.4 %collective-permute-start.5 = (bf16[128,1024]{1,0:T(8,128)(2,1)S(1)}, bf16[128,1024]{1,0:T(8,128)(2,1)S(1)}, u32[]{:S(2)}, u32[]{:S(2)}) collective-permute-start(bf16[128,1024]{1,0:T(8,128)(2,1)S(1)} %collective-permute-done.2), channel_id=1, source_target_pairs={{0,1},{1,0},{2,3},{3,2},{4,5},{5,4},{6,7},{7,6},{8,9},{9,8},{10,11... | collective-permute-start | bytes 786440 | tf_op jit(solution)/shard_map/ppermute | solution.py:215
  53.5 4.9 %collective-permute-start.7 = (bf16[128,1024]{1,0:T(8,128)(2,1)S(1)}, bf16[128,1024]{1,0:T(8,128)(2,1)S(1)}, u32[]{:S(2)}, u32[]{:S(2)}) collective-permute-start(bf16[128,1024]{1,0:T(8,128)(2,1)S(1)} %get-tuple-element.36), channel_id=1, source_target_pairs={{0,256},{128,384},{256,0},{384,128},{1,257},{129,385},{257,1},{385... | collective-permute-start | bytes 786440 | tf_op jit(solution)/shard_map/ppermute | solution.py:212
  58.4 0.7 copy-done.1
  59.1 2.5 %all-to-all-done.1.in_ref = bf16[32,112,128]{2,1,0:T(8,128)(2,1)S(1)} async-done(((bf16[32,112,128]{2,1,0:T(8,128)(2,1)}), bf16[32,112,128]{2,1,0:T(8,128)(2,1)S(1)}, u32[]{:S(2)}, u32[]{:S(2)}) %all-to-all-start.1) | async-done | bytes 917536 | tf_op jit(solution)/shard_map/all_to_all | solution.py:286
  61.6 1.0 collect.1
  62.6 5.1 %collective-permute-start.6 = (bf16[2,128,128]{2,1,0:T(8,128)(2,1)S(1)}, bf16[2,128,128]{2,1,0:T(8,128)(2,1)S(1)}, u32[]{:S(2)}, u32[]{:S(2)}) collective-permute-start(bf16[2,128,128]{2,1,0:T(8,128)(2,1)S(1)} %get-tuple-element.35), channel_id=1, source_target_pairs={{0,64},{64,0},{1,65},{65,1},{2,66},{66,2},{3,67},{67,3},{4,68},{68... | collective-permute-start | bytes 196616 | tf_op jit(solution)/shard_map/ppermute | solution.py:308
  67.8 2.3 %collective-permute-done.6.far_ref = bf16[2,128,128]{2,1,0:T(8,128)(2,1)S(1)} collective-permute-done((bf16[2,128,128]{2,1,0:T(8,128)(2,1)S(1)}, bf16[2,128,128]{2,1,0:T(8,128)(2,1)S(1)}, u32[]{:S(2)}, u32[]{:S(2)}) %collective-permute-start.6) | collective-permute-done | bytes 65568 | tf_op jit(solution)/shard_map/ppermute | solution.py:308
  70.1 0.7 spread.1
  70.8 3.4 %all-to-all-start.2 = ((bf16[8,128,128]{2,1,0:T(8,128)(2,1)}), bf16[8,128,128]{2,1,0:T(8,128)(2,1)S(1)}, u32[]{:S(2)}, u32[]{:S(2)}) async-start(bf16[8,128,128]{2,1,0:T(8,128)(2,1)} %spread.1), calls=%async_computation.2 | async-start | bytes 524288 | tf_op jit(solution)/shard_map/all_to_all | solution.py:320
  74.4 2.3 %collective-permute-start.8 = (bf16[128,1024]{1,0:T(8,128)(2,1)S(1)}, bf16[128,1024]{1,0:T(8,128)(2,1)}, u32[]{:S(2)}, u32[]{:S(2)}) collective-permute-start(bf16[128,1024]{1,0:T(8,128)(2,1)S(1)} %collective-permute-done.7), channel_id=1, source_target_pairs={{0,1},{1,0},{2,3},{3,2},{4,5},{5,4},{6,7},{7,6},{8,9},{9,8},{10,11... | collective-permute-start | bytes 786440 | tf_op jit(solution)/shard_map/ppermute | solution.py:215
  76.7 5.0 %all-to-all-done.2 = bf16[8,128,128]{2,1,0:T(8,128)(2,1)S(1)} async-done(((bf16[8,128,128]{2,1,0:T(8,128)(2,1)}), bf16[8,128,128]{2,1,0:T(8,128)(2,1)S(1)}, u32[]{:S(2)}, u32[]{:S(2)}) %all-to-all-start.2) | async-done | bytes 262176 | tf_op jit(solution)/shard_map/all_to_all | solution.py:320
  81.7 0.2 fusion.8
  82.0 0.3 fusion.18
  82.2 0.3 fusion.12
  82.5 0.3 fusion.6
  82.8 0.3 fusion.14
  83.0 0.3 convolution_add_fusion.1
  83.3 1.2 fusion.10
  84.5 0.3 fusion.5
  84.8 16.1 %all_to_all.25 = bf16[16,64,128]{2,1,0:T(8,128)(2,1)S(1)} all-to-all(bf16[16,64,128]{2,1,0:T(8,128)(2,1)S(1)} %bitcast.50), channel_id=1, replica_groups=mesh['x'=4,'zu'=2,'zd'=2,'y'=4,'zh'=4,'core'=2] {'zu','zd','y'}, dimensions={0} | all-to-all | bytes 524288 | tf_op jit(solution)/shard_map/all_to_all | solution.py:331
  101.0 28.6 %all_to_all.26 = bf16[8,64,128]{2,1,0:T(8,128)(2,1)S(1)} all-to-all(bf16[8,64,128]{2,1,0:T(8,128)(2,1)S(1)} %broadcast_in_dim.30), channel_id=1, replica_groups=mesh['x'=4,'zu'=2,'zd'=2,'y'=4,'zh'=4,'core'=2] {'zh','core'}, dimensions={0} | all-to-all | bytes 262144 | tf_op jit(solution)/shard_map/all_to_all | solution.py:333
  129.6 0.6 copy_bitcast_fusion
  (26 shorter events, 0.3 us)
Async XLA Ops:
  1.4 7.7 %collective-permute-start = (bf16[2,64,256]{2,1,0:T(8,128)(2,1)S(1)}, bf16[2,64,256]{2,1,0:T(8,128)(2,1)S(1)}, u32[]{:S(2)}, u32[]{:S(2)}) collective-permute-start(bf16[2,64,256]{2,1,0:T(8,128)(2,1)S(1)} %pad_maximum_fusion), channel_id=1, source_target_pairs={{0,64},{64,0},{1,65},{65,1},{2,66},{66,2},{3,67},{67,3},{4,68},{68... | collective-permute-start | bytes 196616 | tf_op jit(solution)/shard_map/ppermute | solution.py:219
  10.2 8.8 %copy-start.3 = (s32[2,4096]{1,0:T(2,128)S(1)}, s32[2,4096]{1,0:T(2,128)}, u32[]{:S(2)}) copy-start(s32[2,4096]{1,0:T(2,128)} %param.15) | copy-start | bytes 98308
  10.2 8.8 %copy-start.4 = (s32[2,4096]{1,0:T(2,128)S(1)}, s32[2,4096]{1,0:T(2,128)}, u32[]{:S(2)}) copy-start(s32[2,4096]{1,0:T(2,128)} %param.14) | copy-start | bytes 98308
  10.2 10.1 %copy-start = (bf16[2,64,4096]{2,1,0:T(8,128)(2,1)S(1)}, bf16[2,64,4096]{2,1,0:T(8,128)(2,1)}, u32[]{:S(2)}) copy-start(bf16[2,64,4096]{2,1,0:T(8,128)(2,1)} %param.8) | copy-start | bytes 3145732
  10.3 26.5 %all-to-all-start = ((bf16[32,152,128]{2,1,0:T(8,128)(2,1)}), bf16[32,152,128]{2,1,0:T(8,128)(2,1)S(1)}, u32[]{:S(2)}, u32[]{:S(2)}) async-start(bf16[32,152,128]{2,1,0:T(8,128)(2,1)} %pack_other.1), calls=%async_computation | async-start | bytes 2490368 | tf_op jit(solution)/shard_map/all_to_all | solution.py:243
  20.5 22.9 %collective-permute-start.1 = (bf16[128,1024]{1,0:T(8,128)(2,1)S(1)}, bf16[128,1024]{1,0:T(8,128)(2,1)S(1)}, u32[]{:S(2)}, u32[]{:S(2)}) collective-permute-start(bf16[128,1024]{1,0:T(8,128)(2,1)S(1)} %get-tuple-element.25), channel_id=1, source_target_pairs={{0,128},{128,256},{256,384},{384,0},{1,129},{129,257},{257,385},{3... | collective-permute-start | bytes 786440 | tf_op jit(solution)/shard_map/ppermute | solution.py:212
  23.9 19.5 %collective-permute-start.2 = (bf16[128,1024]{1,0:T(8,128)(2,1)S(1)}, bf16[128,1024]{1,0:T(8,128)(2,1)S(1)}, u32[]{:S(2)}, u32[]{:S(2)}) collective-permute-start(bf16[128,1024]{1,0:T(8,128)(2,1)S(1)} %get-tuple-element.26), channel_id=1, source_target_pairs={{0,384},{128,0},{256,128},{384,256},{1,385},{129,1},{257,129},{385... | collective-permute-start | bytes 786440 | tf_op jit(solution)/shard_map/ppermute | solution.py:212
  27.6 15.8 %collective-permute-start.3 = (bf16[128,1024]{1,0:T(8,128)(2,1)S(1)}, bf16[128,1024]{1,0:T(8,128)(2,1)S(1)}, u32[]{:S(2)}, u32[]{:S(2)}) collective-permute-start(bf16[128,1024]{1,0:T(8,128)(2,1)S(1)} %get-tuple-element.27), channel_id=1, source_target_pairs={{0,1},{1,0},{2,3},{3,2},{4,5},{5,4},{6,7},{7,6},{8,9},{9,8},{10,11... | collective-permute-start | bytes 786440 | tf_op jit(solution)/shard_map/ppermute | solution.py:215
  43.4 18.2 %all-to-all-start.1 = ((bf16[32,112,128]{2,1,0:T(8,128)(2,1)}), bf16[32,112,128]{2,1,0:T(8,128)(2,1)S(1)}, u32[]{:S(2)}, u32[]{:S(2)}) async-start(bf16[32,112,128]{2,1,0:T(8,128)(2,1)} %attend.1), calls=%async_computation.1 | async-start | bytes 1835008 | tf_op jit(solution)/shard_map/all_to_all | solution.py:286
  49.1 9.2 %collective-permute-start.4 = (bf16[128,1024]{1,0:T(8,128)(2,1)S(1)}, bf16[128,1024]{1,0:T(8,128)(2,1)S(1)}, u32[]{:S(2)}, u32[]{:S(2)}) collective-permute-start(bf16[128,1024]{1,0:T(8,128)(2,1)S(1)} %collective-permute-done.1), channel_id=1, source_target_pairs={{0,1},{1,0},{2,3},{3,2},{4,5},{5,4},{6,7},{7,6},{8,9},{9,8},{10,11... | collective-permute-start | bytes 786440 | tf_op jit(solution)/shard_map/ppermute | solution.py:215
  51.1 7.3 %collective-permute-start.5 = (bf16[128,1024]{1,0:T(8,128)(2,1)S(1)}, bf16[128,1024]{1,0:T(8,128)(2,1)S(1)}, u32[]{:S(2)}, u32[]{:S(2)}) collective-permute-start(bf16[128,1024]{1,0:T(8,128)(2,1)S(1)} %collective-permute-done.2), channel_id=1, source_target_pairs={{0,1},{1,0},{2,3},{3,2},{4,5},{5,4},{6,7},{7,6},{8,9},{9,8},{10,11... | collective-permute-start | bytes 786440 | tf_op jit(solution)/shard_map/ppermute | solution.py:215
  53.5 14.3 %collective-permute-start.7 = (bf16[128,1024]{1,0:T(8,128)(2,1)S(1)}, bf16[128,1024]{1,0:T(8,128)(2,1)S(1)}, u32[]{:S(2)}, u32[]{:S(2)}) collective-permute-start(bf16[128,1024]{1,0:T(8,128)(2,1)S(1)} %get-tuple-element.36), channel_id=1, source_target_pairs={{0,256},{128,384},{256,0},{384,128},{1,257},{129,385},{257,1},{385... | collective-permute-start | bytes 786440 | tf_op jit(solution)/shard_map/ppermute | solution.py:212
  58.4 0.7 copy-start.1
  62.6 7.5 %collective-permute-start.6 = (bf16[2,128,128]{2,1,0:T(8,128)(2,1)S(1)}, bf16[2,128,128]{2,1,0:T(8,128)(2,1)S(1)}, u32[]{:S(2)}, u32[]{:S(2)}) collective-permute-start(bf16[2,128,128]{2,1,0:T(8,128)(2,1)S(1)} %get-tuple-element.35), channel_id=1, source_target_pairs={{0,64},{64,0},{1,65},{65,1},{2,66},{66,2},{3,67},{67,3},{4,68},{68... | collective-permute-start | bytes 196616 | tf_op jit(solution)/shard_map/ppermute | solution.py:308
  70.8 10.9 %all-to-all-start.2 = ((bf16[8,128,128]{2,1,0:T(8,128)(2,1)}), bf16[8,128,128]{2,1,0:T(8,128)(2,1)S(1)}, u32[]{:S(2)}, u32[]{:S(2)}) async-start(bf16[8,128,128]{2,1,0:T(8,128)(2,1)} %spread.1), calls=%async_computation.2 | async-start | bytes 524288 | tf_op jit(solution)/shard_map/all_to_all | solution.py:320
  74.3 8.2 %copy-start.2 = (bf16[128,1024]{1,0:T(8,128)(2,1)S(1)}, bf16[128,1024]{1,0:T(8,128)(2,1)}, u32[]{:S(2)}) copy-start(bf16[128,1024]{1,0:T(8,128)(2,1)} %copy-done.1) | copy-start | bytes 786436
  74.4 8.9 %collective-permute-start.8 = (bf16[128,1024]{1,0:T(8,128)(2,1)S(1)}, bf16[128,1024]{1,0:T(8,128)(2,1)}, u32[]{:S(2)}, u32[]{:S(2)}) collective-permute-start(bf16[128,1024]{1,0:T(8,128)(2,1)S(1)} %collective-permute-done.7), channel_id=1, source_target_pairs={{0,1},{1,0},{2,3},{3,2},{4,5},{5,4},{6,7},{7,6},{8,9},{9,8},{10,11... | collective-permute-start | bytes 786440 | tf_op jit(solution)/shard_map/ppermute | solution.py:215

commit v11 on v10

--- a/solution.py
+++ b/solution.py
@@ -117,9 +117,9 @@
     values[:, HD : 2 * HD] = one_hot(iota((KN, HD), 1) < 24)
     delta = picked(104, 0)
     kpos = jnp.broadcast_to(kpos_ref[...], (HD, KN)).T
-    kpos = jnp.concatenate([kpos, kpos], axis=1)
     key_columns = keys[...].astype(F32).T.astype(BF)
-    count = 256
+    count = 512
+    kpos = jnp.concatenate([kpos] * (count // HD), axis=1)
     srcs = count // (OWN * HEADS)
     for c in range(QN // count):
         first = c * srcs
@@ -188,6 +188,14 @@
         out_ref[2 * copy : 2 * copy + 2] = total
 
 
+def finish_kernel(in_ref, out_ref):
+    for core in range(2):
+        total = in_ref[core].astype(F32)
+        for replica in range(1, in_ref.shape[0] // 2):
+            total = total + in_ref[2 * replica + core].astype(F32)
+        out_ref[:, core * HD : (core + 1) * HD] = total
+
+
 def whole(shape):
     return pl.BlockSpec(shape, lambda *_: (0,) * len(shape))
 
@@ -276,7 +284,7 @@
             pltpu.VMEM((KN, HD), F32),
             pltpu.VMEM((KN, HD), F32),
         ],
-        compiler_params=pltpu.CompilerParams(vmem_limit_bytes=16 << 20),
+        compiler_params=pltpu.CompilerParams(vmem_limit_bytes=24 << 20),
         name="attend",
     )(arrived, kpos, qpos, qlow)
     first_twin = other_core(columns[0])
@@ -307,7 +315,6 @@
     )(home)
     far_grad = lax.ppermute(far_grad, "zu", [(0, 1), (1, 0)])
     far_grad, columns[2] = lax.optimization_barrier((far_grad, columns[2]))
-    twin = [twin[0], twin[1], other_core(columns[2]), twin[2]]
     kv_grad = pl.pallas_call(
         spread_kernel,
         out_shape=jax.ShapeDtypeStruct((8, 2 * ROWS, HD), BF),
@@ -317,6 +324,7 @@
         compiler_params=pltpu.CompilerParams(vmem_limit_bytes=4 << 20),
         name="spread",
     )(near_grad, far_grad)
+    twin = [twin[0], twin[1], other_core(columns[2]), twin[2]]
     grads = lax.all_to_all(kv_grad, ("x", "core"), 0, 0, tiled=True)
     part = jnp.zeros((quarter, HD), F32)
     for step in range(4):
@@ -333,8 +341,14 @@
     part = lax.all_to_all(
         jnp.broadcast_to(part[None], (8, 64, HD)), ("zh", "core"), 0, 0, tiled=True
     )
-    part = jnp.sum(part.reshape(4, 2, 64, HD).astype(F32), axis=0)
-    weight_grad = part.transpose(1, 0, 2).reshape(64, 2 * HD)
+    weight_grad = pl.pallas_call(
+        finish_kernel,
+        out_shape=jax.ShapeDtypeStruct((64, 2 * HD), F32),
+        in_specs=[pl.BlockSpec(memory_space=pltpu.VMEM)],
+        out_specs=pl.BlockSpec(memory_space=pltpu.VMEM),
+        compiler_params=pltpu.CompilerParams(vmem_limit_bytes=4 << 20),
+        name="finish",
+    )(part)
     return (query_grad, weight_grad)
 
 

time: 131 us -> 130 us (level)
  waiting for transfers between devices: 16.9 us -> 18.7 us
  local copies, waits for them, and re-layouts: 2.68 us -> 1.33 us
    all_to_all x1, waiting for transfers between devices: 2.49 us -> 4.15 us  [local(): home = lax.all_to_all(back, peers, 0, 0, tiled=True)]
  transfers between devices with their start and end apart: 12 -> 12, of which waited for: 4 -> 4; matrix products, arithmetic and copies ran while one was open for 2% -> 2% of each run, Pallas kernels for 8% -> 7%
where the time goes in v11:
time: 130 us; the launch traced here: 129 us
  starting transfers between devices  48.3 us (37%)
  blocking collectives  44.6 us (34%)
  waiting for transfers between devices  18.7 us (14%)
  Pallas kernels  11.9 us (9%)
  matrix products  2.13 us (2%)
  local copies, waits for them, and re-layouts  1.33 us (1%)
    all_to_all x1, blocking collectives, local(): lax.all_to_all(jnp.broadcast_to(part[None], (8, 64, HD)), ('zh', 'core'),...  28.5 us
    all_to_all x1, blocking collectives, local(): part = lax.all_to_all(part, ('zu', 'zd', 'y'), 0, 0, tiled=True)  16.1 us
    ppermute x3, starting transfers between devices, along_x(): lax.ppermute(columns[step], 'x', [(i, (i + step) % 4) for i in range(4)])  11.9 us
    all_to_all x1, starting transfers between devices, local(): arrived = lax.all_to_all(sent, peers, 0, 0, tiled=True)  8.69 us
    ppermute x4, starting transfers between devices, other_core(): return lax.ppermute(x, 'core', [(0, 1), (1, 0)])  8.45 us
    all_to_all x1, waiting for transfers between devices, local(): arrived = lax.all_to_all(sent, peers, 0, 0, tiled=True)  7.06 us
    pallas_call x1, Pallas kernels, local(): pl.pallas_call(attend_kernel, out_shape=jax.ShapeDtypeStruct((PEERS, BACK...  5.84 us
    all_to_all x1, starting transfers between devices, local(): home = lax.all_to_all(back, peers, 0, 0, tiled=True)  5.73 us
  transfers between devices with their start and end apart: 12, of which 4 were waited for; matrix products, arithmetic and copies ran while one was open for 2% of the time, Pallas kernels for 7%

profile of v11, /device:TPU:32, one launch (start us, length us, event | category | flops | bytes accessed | tf_op | source)
XLA Modules:
  0.0 129.2 jit_solution(10796141252047558423)
XLA Ops:
  0.6 0.8 pad_maximum_fusion
  1.4 5.2 %collective-permute-start = (bf16[2,64,256]{2,1,0:T(8,128)(2,1)S(1)}, bf16[2,64,256]{2,1,0:T(8,128)(2,1)S(1)}, u32[]{:S(2)}, u32[]{:S(2)}) collective-permute-start(bf16[2,64,256]{2,1,0:T(8,128)(2,1)S(1)} %pad_maximum_fusion), channel_id=1, source_target_pairs={{0,64},{64,0},{1,65},{65,1},{2,66},{66,2},{3,67},{67,3},{4,68},{68... | collective-permute-start | bytes 196616 | tf_op jit(solution)/shard_map/ppermute | solution.py:227
  6.6 2.6 %pack.1.in_ref = bf16[32,152,128]{2,1,0:T(8,128)(2,1)} custom-call(bf16[2,64,1024]{2,1,0:T(8,128)(2,1)} %q_ref.1, bf16[2,64,1024]{2,1,0:T(8,128)(2,1)} %g_ref.1, bf16[2,64,1024]{2,1,0:T(8,128)(2,1)} %o_ref.1, bf16[2,64,128]{2,1,0:T(8,128)(2,1)} %k_ref.1, bf16[2,64,128]{2,1,0:T(8,128)(2,1)} %v_ref.1), custom_call_target="tpu_custom_call" | custom-call | tf_op jit(solution)/shard_map/pack/pallas_call | solution.py:230
  9.2 1.0 pack_other.1
  10.3 8.7 %all-to-all-start = ((bf16[32,152,128]{2,1,0:T(8,128)(2,1)}), bf16[32,152,128]{2,1,0:T(8,128)(2,1)S(1)}, u32[]{:S(2)}, u32[]{:S(2)}) async-start(bf16[32,152,128]{2,1,0:T(8,128)(2,1)} %pack_other.1), calls=%async_computation | async-start | bytes 2490368 | tf_op jit(solution)/shard_map/all_to_all | solution.py:251
  19.2 0.1 fusion.28
  19.3 0.1 slice.18
  19.4 0.1 le.16
  19.5 0.1 concatenate.24
  19.6 0.1 slice.19
  19.7 0.1 concatenate.23
  19.7 0.1 concatenate.22
  19.8 0.2 convert_reduce_fusion
  20.0 0.1 select_reduce_fusion
  20.1 0.1 concatenate.25
  20.2 0.1 broadcast_in_dim.17
  20.2 0.1 convert_element_type.45.qlow_ref
  20.4 0.1 constant_dynamic-slice_fusion
  20.5 3.4 %collective-permute-start.1 = (bf16[128,1024]{1,0:T(8,128)(2,1)S(1)}, bf16[128,1024]{1,0:T(8,128)(2,1)S(1)}, u32[]{:S(2)}, u32[]{:S(2)}) collective-permute-start(bf16[128,1024]{1,0:T(8,128)(2,1)S(1)} %get-tuple-element.25), channel_id=1, source_target_pairs={{0,128},{128,256},{256,384},{384,0},{1,129},{129,257},{257,385},{3... | collective-permute-start | bytes 786440 | tf_op jit(solution)/shard_map/ppermute | solution.py:220
  23.9 3.7 %collective-permute-start.2 = (bf16[128,1024]{1,0:T(8,128)(2,1)S(1)}, bf16[128,1024]{1,0:T(8,128)(2,1)S(1)}, u32[]{:S(2)}, u32[]{:S(2)}) collective-permute-start(bf16[128,1024]{1,0:T(8,128)(2,1)S(1)} %get-tuple-element.26), channel_id=1, source_target_pairs={{0,384},{128,0},{256,128},{384,256},{1,385},{129,1},{257,129},{385... | collective-permute-start | bytes 786440 | tf_op jit(solution)/shard_map/ppermute | solution.py:220
  27.6 1.9 %collective-permute-start.3 = (bf16[128,1024]{1,0:T(8,128)(2,1)S(1)}, bf16[128,1024]{1,0:T(8,128)(2,1)S(1)}, u32[]{:S(2)}, u32[]{:S(2)}) collective-permute-start(bf16[128,1024]{1,0:T(8,128)(2,1)S(1)} %get-tuple-element.27), channel_id=1, source_target_pairs={{0,1},{1,0},{2,3},{3,2},{4,5},{5,4},{6,7},{7,6},{8,9},{9,8},{10,11... | collective-permute-start | bytes 786440 | tf_op jit(solution)/shard_map/ppermute | solution.py:223
  29.5 0.1 broadcast_in_dim.18
  29.6 0.1 convert_element_type.47.qpos_ref
  29.7 7.1 %all-to-all-done.in_ref = bf16[32,152,128]{2,1,0:T(8,128)(2,1)S(1)} async-done(((bf16[32,152,128]{2,1,0:T(8,128)(2,1)}), bf16[32,152,128]{2,1,0:T(8,128)(2,1)S(1)}, u32[]{:S(2)}, u32[]{:S(2)}) %all-to-all-start) | async-done | bytes 1245216 | tf_op jit(solution)/shard_map/all_to_all | solution.py:251
  36.8 5.8 %attend.1 = bf16[32,112,128]{2,1,0:T(8,128)(2,1)} custom-call(bf16[32,152,128]{2,1,0:T(8,128)(2,1)S(1)} %all-to-all-done.in_ref, f32[1,1280]{1,0:T(1,128)S(1)} %add_convert_fusion.kpos_ref, f32[1,1024]{1,0:T(1,128)S(1)} %convert_element_type.47.qpos_ref, f32[1,1024]{1,0:T(1,128)S(1)} %convert_element_type.45.qlow_ref), custom_call_target="tpu_custom_call" | custom-call | tf_op jit(solution)/shard_map/attend/pallas_call | solution.py:275
  42.6 5.7 %all-to-all-start.1 = ((bf16[32,112,128]{2,1,0:T(8,128)(2,1)}), bf16[32,112,128]{2,1,0:T(8,128)(2,1)S(1)}, u32[]{:S(2)}, u32[]{:S(2)}) async-start(bf16[32,112,128]{2,1,0:T(8,128)(2,1)} %attend.1), calls=%async_computation.1 | async-start | bytes 1835008 | tf_op jit(solution)/shard_map/all_to_all | solution.py:294
  48.4 1.9 %collective-permute-start.4 = (bf16[128,1024]{1,0:T(8,128)(2,1)S(1)}, bf16[128,1024]{1,0:T(8,128)(2,1)S(1)}, u32[]{:S(2)}, u32[]{:S(2)}) collective-permute-start(bf16[128,1024]{1,0:T(8,128)(2,1)S(1)} %collective-permute-done.1), channel_id=1, source_target_pairs={{0,1},{1,0},{2,3},{3,2},{4,5},{5,4},{6,7},{7,6},{8,9},{9,8},{10,11... | collective-permute-start | bytes 786440 | tf_op jit(solution)/shard_map/ppermute | solution.py:223
  50.3 2.4 %collective-permute-start.5 = (bf16[128,1024]{1,0:T(8,128)(2,1)S(1)}, bf16[128,1024]{1,0:T(8,128)(2,1)S(1)}, u32[]{:S(2)}, u32[]{:S(2)}) collective-permute-start(bf16[128,1024]{1,0:T(8,128)(2,1)S(1)} %collective-permute-done.2), channel_id=1, source_target_pairs={{0,1},{1,0},{2,3},{3,2},{4,5},{5,4},{6,7},{7,6},{8,9},{9,8},{10,11... | collective-permute-start | bytes 786440 | tf_op jit(solution)/shard_map/ppermute | solution.py:223
  52.7 4.9 %collective-permute-start.7 = (bf16[128,1024]{1,0:T(8,128)(2,1)S(1)}, bf16[128,1024]{1,0:T(8,128)(2,1)S(1)}, u32[]{:S(2)}, u32[]{:S(2)}) collective-permute-start(bf16[128,1024]{1,0:T(8,128)(2,1)S(1)} %get-tuple-element.36), channel_id=1, source_target_pairs={{0,256},{128,384},{256,0},{384,128},{1,257},{129,385},{257,1},{385... | collective-permute-start | bytes 786440 | tf_op jit(solution)/shard_map/ppermute | solution.py:220
  57.6 4.2 %all-to-all-done.1.in_ref = bf16[32,112,128]{2,1,0:T(8,128)(2,1)S(1)} async-done(((bf16[32,112,128]{2,1,0:T(8,128)(2,1)}), bf16[32,112,128]{2,1,0:T(8,128)(2,1)S(1)}, u32[]{:S(2)}, u32[]{:S(2)}) %all-to-all-start.1) | async-done | bytes 917536 | tf_op jit(solution)/shard_map/all_to_all | solution.py:294
  61.8 1.0 collect.1
  62.8 4.9 %collective-permute-start.6 = (bf16[2,128,128]{2,1,0:T(8,128)(2,1)S(1)}, bf16[2,128,128]{2,1,0:T(8,128)(2,1)S(1)}, u32[]{:S(2)}, u32[]{:S(2)}) collective-permute-start(bf16[2,128,128]{2,1,0:T(8,128)(2,1)S(1)} %get-tuple-element.35), channel_id=1, source_target_pairs={{0,64},{64,0},{1,65},{65,1},{2,66},{66,2},{3,67},{67,3},{4,68},{68... | collective-permute-start | bytes 196616 | tf_op jit(solution)/shard_map/ppermute | solution.py:316
  67.8 2.3 %collective-permute-done.6.far_ref = bf16[2,128,128]{2,1,0:T(8,128)(2,1)S(1)} collective-permute-done((bf16[2,128,128]{2,1,0:T(8,128)(2,1)S(1)}, bf16[2,128,128]{2,1,0:T(8,128)(2,1)S(1)}, u32[]{:S(2)}, u32[]{:S(2)}) %collective-permute-start.6) | collective-permute-done | bytes 65568 | tf_op jit(solution)/shard_map/ppermute | solution.py:316
  70.1 0.7 spread.1
  70.8 3.4 %all-to-all-start.2 = ((bf16[8,128,128]{2,1,0:T(8,128)(2,1)}), bf16[8,128,128]{2,1,0:T(8,128)(2,1)S(1)}, u32[]{:S(2)}, u32[]{:S(2)}) async-start(bf16[8,128,128]{2,1,0:T(8,128)(2,1)} %spread.1), calls=%async_computation.2 | async-start | bytes 524288 | tf_op jit(solution)/shard_map/all_to_all | solution.py:328
  74.3 2.2 %collective-permute-start.8 = (bf16[128,1024]{1,0:T(8,128)(2,1)S(1)}, bf16[128,1024]{1,0:T(8,128)(2,1)S(1)}, u32[]{:S(2)}, u32[]{:S(2)}) collective-permute-start(bf16[128,1024]{1,0:T(8,128)(2,1)S(1)} %collective-permute-done.7), channel_id=1, source_target_pairs={{0,1},{1,0},{2,3},{3,2},{4,5},{5,4},{6,7},{7,6},{8,9},{9,8},{10,11... | collective-permute-start | bytes 786440 | tf_op jit(solution)/shard_map/ppermute | solution.py:223
  76.6 5.1 %all-to-all-done.2 = bf16[8,128,128]{2,1,0:T(8,128)(2,1)S(1)} async-done(((bf16[8,128,128]{2,1,0:T(8,128)(2,1)}), bf16[8,128,128]{2,1,0:T(8,128)(2,1)S(1)}, u32[]{:S(2)}, u32[]{:S(2)}) %all-to-all-start.2) | async-done | bytes 262176 | tf_op jit(solution)/shard_map/all_to_all | solution.py:328
  81.7 0.2 fusion.8
  82.0 0.3 fusion.18
  82.2 0.3 fusion.12
  82.5 0.3 fusion.6
  82.7 0.3 fusion.14
  83.0 0.3 convolution_add_fusion.1
  83.3 0.3 fusion.10
  83.5 0.3 fusion.5
  83.9 16.1 %all_to_all.25 = bf16[16,64,128]{2,1,0:T(8,128)(2,1)S(1)} all-to-all(bf16[16,64,128]{2,1,0:T(8,128)(2,1)S(1)} %bitcast.42), channel_id=1, replica_groups=mesh['x'=4,'zu'=2,'zd'=2,'y'=4,'zh'=4,'core'=2] {'zu','zd','y'}, dimensions={0} | all-to-all | bytes 524288 | tf_op jit(solution)/shard_map/all_to_all | solution.py:339
  100.1 28.5 %all_to_all.26.in_ref = bf16[8,64,128]{2,1,0:T(8,128)(2,1)S(1)} all-to-all(bf16[8,64,128]{2,1,0:T(8,128)(2,1)S(1)} %broadcast_in_dim.30), channel_id=1, replica_groups=mesh['x'=4,'zu'=2,'zd'=2,'y'=4,'zh'=4,'core'=2] {'zh','core'}, dimensions={0} | all-to-all | bytes 262144 | tf_op jit(solution)/shard_map/all_to_all | solution.py:341
  128.6 0.6 finish.1
  (21 shorter events, 0.3 us)
Async XLA Ops:
  1.4 7.8 %collective-permute-start = (bf16[2,64,256]{2,1,0:T(8,128)(2,1)S(1)}, bf16[2,64,256]{2,1,0:T(8,128)(2,1)S(1)}, u32[]{:S(2)}, u32[]{:S(2)}) collective-permute-start(bf16[2,64,256]{2,1,0:T(8,128)(2,1)S(1)} %pad_maximum_fusion), channel_id=1, source_target_pairs={{0,64},{64,0},{1,65},{65,1},{2,66},{66,2},{3,67},{67,3},{4,68},{68... | collective-permute-start | bytes 196616 | tf_op jit(solution)/shard_map/ppermute | solution.py:227
  10.2 8.8 %copy-start.1 = (s32[2,4096]{1,0:T(2,128)S(1)}, s32[2,4096]{1,0:T(2,128)}, u32[]{:S(2)}) copy-start(s32[2,4096]{1,0:T(2,128)} %param.15) | copy-start | bytes 98308
  10.2 8.8 %copy-start.2 = (s32[2,4096]{1,0:T(2,128)S(1)}, s32[2,4096]{1,0:T(2,128)}, u32[]{:S(2)}) copy-start(s32[2,4096]{1,0:T(2,128)} %param.14) | copy-start | bytes 98308
  10.2 10.1 %copy-start = (bf16[2,64,4096]{2,1,0:T(8,128)(2,1)S(1)}, bf16[2,64,4096]{2,1,0:T(8,128)(2,1)}, u32[]{:S(2)}) copy-start(bf16[2,64,4096]{2,1,0:T(8,128)(2,1)} %param.8) | copy-start | bytes 3145732
  10.3 26.5 %all-to-all-start = ((bf16[32,152,128]{2,1,0:T(8,128)(2,1)}), bf16[32,152,128]{2,1,0:T(8,128)(2,1)S(1)}, u32[]{:S(2)}, u32[]{:S(2)}) async-start(bf16[32,152,128]{2,1,0:T(8,128)(2,1)} %pack_other.1), calls=%async_computation | async-start | bytes 2490368 | tf_op jit(solution)/shard_map/all_to_all | solution.py:251
  20.5 22.1 %collective-permute-start.1 = (bf16[128,1024]{1,0:T(8,128)(2,1)S(1)}, bf16[128,1024]{1,0:T(8,128)(2,1)S(1)}, u32[]{:S(2)}, u32[]{:S(2)}) collective-permute-start(bf16[128,1024]{1,0:T(8,128)(2,1)S(1)} %get-tuple-element.25), channel_id=1, source_target_pairs={{0,128},{128,256},{256,384},{384,0},{1,129},{129,257},{257,385},{3... | collective-permute-start | bytes 786440 | tf_op jit(solution)/shard_map/ppermute | solution.py:220
  23.9 18.7 %collective-permute-start.2 = (bf16[128,1024]{1,0:T(8,128)(2,1)S(1)}, bf16[128,1024]{1,0:T(8,128)(2,1)S(1)}, u32[]{:S(2)}, u32[]{:S(2)}) collective-permute-start(bf16[128,1024]{1,0:T(8,128)(2,1)S(1)} %get-tuple-element.26), channel_id=1, source_target_pairs={{0,384},{128,0},{256,128},{384,256},{1,385},{129,1},{257,129},{385... | collective-permute-start | bytes 786440 | tf_op jit(solution)/shard_map/ppermute | solution.py:220
  27.6 15.0 %collective-permute-start.3 = (bf16[128,1024]{1,0:T(8,128)(2,1)S(1)}, bf16[128,1024]{1,0:T(8,128)(2,1)S(1)}, u32[]{:S(2)}, u32[]{:S(2)}) collective-permute-start(bf16[128,1024]{1,0:T(8,128)(2,1)S(1)} %get-tuple-element.27), channel_id=1, source_target_pairs={{0,1},{1,0},{2,3},{3,2},{4,5},{5,4},{6,7},{7,6},{8,9},{9,8},{10,11... | collective-permute-start | bytes 786440 | tf_op jit(solution)/shard_map/ppermute | solution.py:223
  42.6 19.2 %all-to-all-start.1 = ((bf16[32,112,128]{2,1,0:T(8,128)(2,1)}), bf16[32,112,128]{2,1,0:T(8,128)(2,1)S(1)}, u32[]{:S(2)}, u32[]{:S(2)}) async-start(bf16[32,112,128]{2,1,0:T(8,128)(2,1)} %attend.1), calls=%async_computation.1 | async-start | bytes 1835008 | tf_op jit(solution)/shard_map/all_to_all | solution.py:294
  48.4 9.2 %collective-permute-start.4 = (bf16[128,1024]{1,0:T(8,128)(2,1)S(1)}, bf16[128,1024]{1,0:T(8,128)(2,1)S(1)}, u32[]{:S(2)}, u32[]{:S(2)}) collective-permute-start(bf16[128,1024]{1,0:T(8,128)(2,1)S(1)} %collective-permute-done.1), channel_id=1, source_target_pairs={{0,1},{1,0},{2,3},{3,2},{4,5},{5,4},{6,7},{7,6},{8,9},{9,8},{10,11... | collective-permute-start | bytes 786440 | tf_op jit(solution)/shard_map/ppermute | solution.py:223
  50.3 7.3 %collective-permute-start.5 = (bf16[128,1024]{1,0:T(8,128)(2,1)S(1)}, bf16[128,1024]{1,0:T(8,128)(2,1)S(1)}, u32[]{:S(2)}, u32[]{:S(2)}) collective-permute-start(bf16[128,1024]{1,0:T(8,128)(2,1)S(1)} %collective-permute-done.2), channel_id=1, source_target_pairs={{0,1},{1,0},{2,3},{3,2},{4,5},{5,4},{6,7},{7,6},{8,9},{9,8},{10,11... | collective-permute-start | bytes 786440 | tf_op jit(solution)/shard_map/ppermute | solution.py:223
  52.7 15.1 %collective-permute-start.7 = (bf16[128,1024]{1,0:T(8,128)(2,1)S(1)}, bf16[128,1024]{1,0:T(8,128)(2,1)S(1)}, u32[]{:S(2)}, u32[]{:S(2)}) collective-permute-start(bf16[128,1024]{1,0:T(8,128)(2,1)S(1)} %get-tuple-element.36), channel_id=1, source_target_pairs={{0,256},{128,384},{256,0},{384,128},{1,257},{129,385},{257,1},{385... | collective-permute-start | bytes 786440 | tf_op jit(solution)/shard_map/ppermute | solution.py:220
  62.8 7.3 %collective-permute-start.6 = (bf16[2,128,128]{2,1,0:T(8,128)(2,1)S(1)}, bf16[2,128,128]{2,1,0:T(8,128)(2,1)S(1)}, u32[]{:S(2)}, u32[]{:S(2)}) collective-permute-start(bf16[2,128,128]{2,1,0:T(8,128)(2,1)S(1)} %get-tuple-element.35), channel_id=1, source_target_pairs={{0,64},{64,0},{1,65},{65,1},{2,66},{66,2},{3,67},{67,3},{4,68},{68... | collective-permute-start | bytes 196616 | tf_op jit(solution)/shard_map/ppermute | solution.py:316
  70.8 10.9 %all-to-all-start.2 = ((bf16[8,128,128]{2,1,0:T(8,128)(2,1)}), bf16[8,128,128]{2,1,0:T(8,128)(2,1)S(1)}, u32[]{:S(2)}, u32[]{:S(2)}) async-start(bf16[8,128,128]{2,1,0:T(8,128)(2,1)} %spread.1), calls=%async_computation.2 | async-start | bytes 524288 | tf_op jit(solution)/shard_map/all_to_all | solution.py:328
  74.3 8.9 %collective-permute-start.8 = (bf16[128,1024]{1,0:T(8,128)(2,1)S(1)}, bf16[128,1024]{1,0:T(8,128)(2,1)S(1)}, u32[]{:S(2)}, u32[]{:S(2)}) collective-permute-start(bf16[128,1024]{1,0:T(8,128)(2,1)S(1)} %collective-permute-done.7), channel_id=1, source_target_pairs={{0,1},{1,0},{2,3},{3,2},{4,5},{5,4},{6,7},{7,6},{8,9},{9,8},{10,11... | collective-permute-start | bytes 786440 | tf_op jit(solution)/shard_map/ppermute | solution.py:223

commit v12 on v11

--- a/solution.py
+++ b/solution.py
@@ -314,7 +314,6 @@
         name="collect",
     )(home)
     far_grad = lax.ppermute(far_grad, "zu", [(0, 1), (1, 0)])
-    far_grad, columns[2] = lax.optimization_barrier((far_grad, columns[2]))
     kv_grad = pl.pallas_call(
         spread_kernel,
         out_shape=jax.ShapeDtypeStruct((8, 2 * ROWS, HD), BF),

time: 130 us -> 131 us (level)
  waiting for transfers between devices: 18.7 us -> 21.4 us
  blocking collectives: 44.6 us -> 43 us
    all_to_all x1, waiting for transfers between devices: 4.15 us -> 7.72 us  [local(): home = lax.all_to_all(back, peers, 0, 0, tiled=True)]
    ppermute x1, waiting for transfers between devices: 2.32 us -> 0.01 us  [local(): far_grad = lax.ppermute(far_grad, 'zu', [(0, 1), (1, 0)])]
    ppermute x3, waiting for transfers between devices: 0.01 us -> 1.94 us  [along_x(): lax.ppermute(columns[step], 'x', [(i, (i + step) % 4) for i in range(4)])]
    all_to_all x1, blocking collectives: 16.1 us -> 14.4 us  [local(): part = lax.all_to_all(part, ('zu', 'zd', 'y'), 0, 0, tiled=True)]
    all_to_all x1, waiting for transfers between devices: 5.15 us -> 3.5 us  [local(): grads = lax.all_to_all(kv_grad, ('x', 'core'), 0, 0, tiled=True)]
  transfers between devices with their start and end apart: 12 -> 12, of which waited for: 4 -> 5; matrix products, arithmetic and copies ran while one was open for 2% -> 3% of each run, Pallas kernels for 7% -> 7%
where the time goes in v12:
time: 131 us; the launch traced here: 130 us
  starting transfers between devices  47 us (36%)
  blocking collectives  43 us (33%)
  waiting for transfers between devices  21.4 us (16%)
  Pallas kernels  11.9 us (9%)
  matrix products  3.03 us (2%)
  local copies, waits for them, and re-layouts  1.76 us (1%)
    all_to_all x1, blocking collectives, local(): lax.all_to_all(jnp.broadcast_to(part[None], (8, 64, HD)), ('zh', 'core'),...  28.6 us
    all_to_all x1, blocking collectives, local(): part = lax.all_to_all(part, ('zu', 'zd', 'y'), 0, 0, tiled=True)  14.4 us
    ppermute x3, starting transfers between devices, along_x(): lax.ppermute(columns[step], 'x', [(i, (i + step) % 4) for i in range(4)])  10.7 us
    all_to_all x1, starting transfers between devices, local(): arrived = lax.all_to_all(sent, peers, 0, 0, tiled=True)  8.69 us
    ppermute x4, starting transfers between devices, other_core(): return lax.ppermute(x, 'core', [(0, 1), (1, 0)])  8.16 us
    all_to_all x1, waiting for transfers between devices, local(): home = lax.all_to_all(back, peers, 0, 0, tiled=True)  7.72 us
    all_to_all x1, waiting for transfers between devices, local(): arrived = lax.all_to_all(sent, peers, 0, 0, tiled=True)  7.06 us
    pallas_call x1, Pallas kernels, local(): pl.pallas_call(attend_kernel, out_shape=jax.ShapeDtypeStruct((PEERS, BACK...  5.84 us
  transfers between devices with their start and end apart: 12, of which 5 were waited for; matrix products, arithmetic and copies ran while one was open for 3% of the time, Pallas kernels for 7%

profile of v12, /device:TPU:32, one launch (start us, length us, event | category | flops | bytes accessed | tf_op | source)
XLA Modules:
  0.0 130.3 jit_solution(17750357982605004426)
XLA Ops:
  0.6 0.8 pad_maximum_fusion
  1.4 5.2 %collective-permute-start = (bf16[2,64,256]{2,1,0:T(8,128)(2,1)S(1)}, bf16[2,64,256]{2,1,0:T(8,128)(2,1)S(1)}, u32[]{:S(2)}, u32[]{:S(2)}) collective-permute-start(bf16[2,64,256]{2,1,0:T(8,128)(2,1)S(1)} %pad_maximum_fusion), channel_id=1, source_target_pairs={{0,64},{64,0},{1,65},{65,1},{2,66},{66,2},{3,67},{67,3},{4,68},{68... | collective-permute-start | bytes 196616 | tf_op jit(solution)/shard_map/ppermute | solution.py:227
  6.6 2.6 %pack.1.in_ref = bf16[32,152,128]{2,1,0:T(8,128)(2,1)} custom-call(bf16[2,64,1024]{2,1,0:T(8,128)(2,1)} %q_ref.1, bf16[2,64,1024]{2,1,0:T(8,128)(2,1)} %g_ref.1, bf16[2,64,1024]{2,1,0:T(8,128)(2,1)} %o_ref.1, bf16[2,64,128]{2,1,0:T(8,128)(2,1)} %k_ref.1, bf16[2,64,128]{2,1,0:T(8,128)(2,1)} %v_ref.1), custom_call_target="tpu_custom_call" | custom-call | tf_op jit(solution)/shard_map/pack/pallas_call | solution.py:230
  9.2 1.1 pack_other.1
  10.3 8.7 %all-to-all-start = ((bf16[32,152,128]{2,1,0:T(8,128)(2,1)}), bf16[32,152,128]{2,1,0:T(8,128)(2,1)S(1)}, u32[]{:S(2)}, u32[]{:S(2)}) async-start(bf16[32,152,128]{2,1,0:T(8,128)(2,1)} %pack_other.1), calls=%async_computation | async-start | bytes 2490368 | tf_op jit(solution)/shard_map/all_to_all | solution.py:251
  19.2 0.1 fusion.26
  19.3 0.1 slice.18
  19.4 0.1 concatenate.24
  19.5 0.1 le.16
  19.7 0.1 concatenate.25
  19.8 0.1 concatenate.22
  19.9 0.1 concatenate.23
  20.0 0.2 convert_reduce_fusion
  20.1 0.1 select_reduce_fusion
  20.2 0.1 broadcast_in_dim.17
  20.3 0.1 convert_element_type.45.qlow_ref
  20.5 0.1 constant_dynamic-slice_fusion
  20.6 3.4 %collective-permute-start.1 = (bf16[128,1024]{1,0:T(8,128)(2,1)S(1)}, bf16[128,1024]{1,0:T(8,128)(2,1)S(1)}, u32[]{:S(2)}, u32[]{:S(2)}) collective-permute-start(bf16[128,1024]{1,0:T(8,128)(2,1)S(1)} %get-tuple-element.23), channel_id=1, source_target_pairs={{0,128},{128,256},{256,384},{384,0},{1,129},{129,257},{257,385},{3... | collective-permute-start | bytes 786440 | tf_op jit(solution)/shard_map/ppermute | solution.py:220
  24.0 3.7 %collective-permute-start.2 = (bf16[128,1024]{1,0:T(8,128)(2,1)S(1)}, bf16[128,1024]{1,0:T(8,128)(2,1)S(1)}, u32[]{:S(2)}, u32[]{:S(2)}) collective-permute-start(bf16[128,1024]{1,0:T(8,128)(2,1)S(1)} %get-tuple-element.24), channel_id=1, source_target_pairs={{0,384},{128,0},{256,128},{384,256},{1,385},{129,1},{257,129},{385... | collective-permute-start | bytes 786440 | tf_op jit(solution)/shard_map/ppermute | solution.py:220
  27.6 1.9 %collective-permute-start.3 = (bf16[128,1024]{1,0:T(8,128)(2,1)S(1)}, bf16[128,1024]{1,0:T(8,128)(2,1)S(1)}, u32[]{:S(2)}, u32[]{:S(2)}) collective-permute-start(bf16[128,1024]{1,0:T(8,128)(2,1)S(1)} %get-tuple-element.25), channel_id=1, source_target_pairs={{0,1},{1,0},{2,3},{3,2},{4,5},{5,4},{6,7},{7,6},{8,9},{9,8},{10,11... | collective-permute-start | bytes 786440 | tf_op jit(solution)/shard_map/ppermute | solution.py:223
  29.7 0.1 convert_element_type.47.qpos_ref
  29.8 7.1 %all-to-all-done.in_ref = bf16[32,152,128]{2,1,0:T(8,128)(2,1)S(1)} async-done(((bf16[32,152,128]{2,1,0:T(8,128)(2,1)}), bf16[32,152,128]{2,1,0:T(8,128)(2,1)S(1)}, u32[]{:S(2)}, u32[]{:S(2)}) %all-to-all-start) | async-done | bytes 1245216 | tf_op jit(solution)/shard_map/all_to_all | solution.py:251
  36.8 5.8 %attend.1 = bf16[32,112,128]{2,1,0:T(8,128)(2,1)} custom-call(bf16[32,152,128]{2,1,0:T(8,128)(2,1)S(1)} %all-to-all-done.in_ref, f32[1,1280]{1,0:T(1,128)S(1)} %add_convert_fusion.kpos_ref, f32[1,1024]{1,0:T(1,128)S(1)} %convert_element_type.47.qpos_ref, f32[1,1024]{1,0:T(1,128)S(1)} %convert_element_type.45.qlow_ref), custom_call_target="tpu_custom_call" | custom-call | tf_op jit(solution)/shard_map/attend/pallas_call | solution.py:275
  42.7 5.7 %all-to-all-start.1 = ((bf16[32,112,128]{2,1,0:T(8,128)(2,1)}), bf16[32,112,128]{2,1,0:T(8,128)(2,1)S(1)}, u32[]{:S(2)}, u32[]{:S(2)}) async-start(bf16[32,112,128]{2,1,0:T(8,128)(2,1)} %attend.1), calls=%async_computation.1 | async-start | bytes 1835008 | tf_op jit(solution)/shard_map/all_to_all | solution.py:294
  48.4 1.9 %collective-permute-start.4 = (bf16[128,1024]{1,0:T(8,128)(2,1)S(1)}, bf16[128,1024]{1,0:T(8,128)(2,1)S(1)}, u32[]{:S(2)}, u32[]{:S(2)}) collective-permute-start(bf16[128,1024]{1,0:T(8,128)(2,1)S(1)} %collective-permute-done.1), channel_id=1, source_target_pairs={{0,1},{1,0},{2,3},{3,2},{4,5},{5,4},{6,7},{7,6},{8,9},{9,8},{10,11... | collective-permute-start | bytes 786440 | tf_op jit(solution)/shard_map/ppermute | solution.py:223
  50.4 2.4 %collective-permute-start.5 = (bf16[128,1024]{1,0:T(8,128)(2,1)S(1)}, bf16[128,1024]{1,0:T(8,128)(2,1)S(1)}, u32[]{:S(2)}, u32[]{:S(2)}) collective-permute-start(bf16[128,1024]{1,0:T(8,128)(2,1)S(1)} %collective-permute-done.2), channel_id=1, source_target_pairs={{0,1},{1,0},{2,3},{3,2},{4,5},{5,4},{6,7},{7,6},{8,9},{9,8},{10,11... | collective-permute-start | bytes 786440 | tf_op jit(solution)/shard_map/ppermute | solution.py:223
  52.8 1.1 collective-permute-done.5
  53.9 7.7 %all-to-all-done.1.in_ref = bf16[32,112,128]{2,1,0:T(8,128)(2,1)S(1)} async-done(((bf16[32,112,128]{2,1,0:T(8,128)(2,1)}), bf16[32,112,128]{2,1,0:T(8,128)(2,1)S(1)}, u32[]{:S(2)}, u32[]{:S(2)}) %all-to-all-start.1) | async-done | bytes 917536 | tf_op jit(solution)/shard_map/all_to_all | solution.py:294
  61.6 1.0 collect.1
  62.7 5.2 %collective-permute-start.6 = (bf16[2,128,128]{2,1,0:T(8,128)(2,1)S(1)}, bf16[2,128,128]{2,1,0:T(8,128)(2,1)S(1)}, u32[]{:S(2)}, u32[]{:S(2)}) collective-permute-start(bf16[2,128,128]{2,1,0:T(8,128)(2,1)S(1)} %get-tuple-element.33), channel_id=1, source_target_pairs={{0,64},{64,0},{1,65},{65,1},{2,66},{66,2},{3,67},{67,3},{4,68},{68... | collective-permute-start | bytes 196616 | tf_op jit(solution)/shard_map/ppermute | solution.py:316
  67.8 3.7 %collective-permute-start.7 = (bf16[128,1024]{1,0:T(8,128)(2,1)S(1)}, bf16[128,1024]{1,0:T(8,128)(2,1)}, u32[]{:S(2)}, u32[]{:S(2)}) collective-permute-start(bf16[128,1024]{1,0:T(8,128)(2,1)S(1)} %get-tuple-element.36), channel_id=1, source_target_pairs={{0,256},{128,384},{256,0},{384,128},{1,257},{129,385},{257,1},{385... | collective-permute-start | bytes 786440 | tf_op jit(solution)/shard_map/ppermute | solution.py:220
  71.5 0.7 spread.1
  72.3 3.4 %all-to-all-start.2 = ((bf16[8,128,128]{2,1,0:T(8,128)(2,1)}), bf16[8,128,128]{2,1,0:T(8,128)(2,1)S(1)}, u32[]{:S(2)}, u32[]{:S(2)}) async-start(bf16[8,128,128]{2,1,0:T(8,128)(2,1)} %spread.1), calls=%async_computation.2 | async-start | bytes 524288 | tf_op jit(solution)/shard_map/all_to_all | solution.py:327
  75.8 1.9 %collective-permute-done.7 = bf16[128,1024]{1,0:T(8,128)(2,1)} collective-permute-done((bf16[128,1024]{1,0:T(8,128)(2,1)S(1)}, bf16[128,1024]{1,0:T(8,128)(2,1)}, u32[]{:S(2)}, u32[]{:S(2)}) %collective-permute-start.7) | collective-permute-done | bytes 262176 | tf_op jit(solution)/shard_map/ppermute | solution.py:220
  77.7 1.9 %collective-permute-start.8 = (bf16[128,1024]{1,0:T(8,128)(2,1)}, bf16[128,1024]{1,0:T(8,128)(2,1)S(1)}, u32[]{:S(2)}, u32[]{:S(2)}) collective-permute-start(bf16[128,1024]{1,0:T(8,128)(2,1)} %collective-permute-done.7), channel_id=1, source_target_pairs={{0,1},{1,0},{2,3},{3,2},{4,5},{5,4},{6,7},{7,6},{8,9},{9,8},{10,11... | collective-permute-start | bytes 786440 | tf_op jit(solution)/shard_map/ppermute | solution.py:223
  79.6 3.5 %all-to-all-done.2 = bf16[8,128,128]{2,1,0:T(8,128)(2,1)S(1)} async-done(((bf16[8,128,128]{2,1,0:T(8,128)(2,1)}), bf16[8,128,128]{2,1,0:T(8,128)(2,1)S(1)}, u32[]{:S(2)}, u32[]{:S(2)}) %all-to-all-start.2) | async-done | bytes 262176 | tf_op jit(solution)/shard_map/all_to_all | solution.py:327
  83.1 1.2 fusion.10
  84.3 0.3 fusion.15
  84.6 0.3 convolution_add_fusion.2
  84.9 0.3 fusion.12
  85.1 0.4 copy-done.2
  85.5 0.3 fusion.1
  85.8 0.3 fusion.7
  86.1 0.3 fusion.5
  86.4 0.3 fusion.4
  86.6 14.4 %all_to_all.25 = bf16[16,64,128]{2,1,0:T(8,128)(2,1)S(1)} all-to-all(bf16[16,64,128]{2,1,0:T(8,128)(2,1)S(1)} %bitcast.42), channel_id=1, replica_groups=mesh['x'=4,'zu'=2,'zd'=2,'y'=4,'zh'=4,'core'=2] {'zu','zd','y'}, dimensions={0} | all-to-all | bytes 524288 | tf_op jit(solution)/shard_map/all_to_all | solution.py:338
  101.1 28.6 %all_to_all.26.in_ref = bf16[8,64,128]{2,1,0:T(8,128)(2,1)S(1)} all-to-all(bf16[8,64,128]{2,1,0:T(8,128)(2,1)S(1)} %broadcast_in_dim.30), channel_id=1, replica_groups=mesh['x'=4,'zu'=2,'zd'=2,'y'=4,'zh'=4,'core'=2] {'zh','core'}, dimensions={0} | all-to-all | bytes 262144 | tf_op jit(solution)/shard_map/all_to_all | solution.py:340
  129.7 0.6 finish.1
  (25 shorter events, 0.4 us)
Async XLA Ops:
  1.4 7.8 %collective-permute-start = (bf16[2,64,256]{2,1,0:T(8,128)(2,1)S(1)}, bf16[2,64,256]{2,1,0:T(8,128)(2,1)S(1)}, u32[]{:S(2)}, u32[]{:S(2)}) collective-permute-start(bf16[2,64,256]{2,1,0:T(8,128)(2,1)S(1)} %pad_maximum_fusion), channel_id=1, source_target_pairs={{0,64},{64,0},{1,65},{65,1},{2,66},{66,2},{3,67},{67,3},{4,68},{68... | collective-permute-start | bytes 196616 | tf_op jit(solution)/shard_map/ppermute | solution.py:227
  10.3 8.8 %copy-start.3 = (s32[2,4096]{1,0:T(2,128)S(1)}, s32[2,4096]{1,0:T(2,128)}, u32[]{:S(2)}) copy-start(s32[2,4096]{1,0:T(2,128)} %param.15) | copy-start | bytes 98308
  10.3 8.8 %copy-start.4 = (s32[2,4096]{1,0:T(2,128)S(1)}, s32[2,4096]{1,0:T(2,128)}, u32[]{:S(2)}) copy-start(s32[2,4096]{1,0:T(2,128)} %param.14) | copy-start | bytes 98308
  10.3 10.1 %copy-start = (bf16[2,64,4096]{2,1,0:T(8,128)(2,1)S(1)}, bf16[2,64,4096]{2,1,0:T(8,128)(2,1)}, u32[]{:S(2)}) copy-start(bf16[2,64,4096]{2,1,0:T(8,128)(2,1)} %param.8) | copy-start | bytes 3145732
  10.3 26.5 %all-to-all-start = ((bf16[32,152,128]{2,1,0:T(8,128)(2,1)}), bf16[32,152,128]{2,1,0:T(8,128)(2,1)S(1)}, u32[]{:S(2)}, u32[]{:S(2)}) async-start(bf16[32,152,128]{2,1,0:T(8,128)(2,1)} %pack_other.1), calls=%async_computation | async-start | bytes 2490368 | tf_op jit(solution)/shard_map/all_to_all | solution.py:251
  20.6 22.1 %collective-permute-start.1 = (bf16[128,1024]{1,0:T(8,128)(2,1)S(1)}, bf16[128,1024]{1,0:T(8,128)(2,1)S(1)}, u32[]{:S(2)}, u32[]{:S(2)}) collective-permute-start(bf16[128,1024]{1,0:T(8,128)(2,1)S(1)} %get-tuple-element.23), channel_id=1, source_target_pairs={{0,128},{128,256},{256,384},{384,0},{1,129},{129,257},{257,385},{3... | collective-permute-start | bytes 786440 | tf_op jit(solution)/shard_map/ppermute | solution.py:220
  24.0 18.7 %collective-permute-start.2 = (bf16[128,1024]{1,0:T(8,128)(2,1)S(1)}, bf16[128,1024]{1,0:T(8,128)(2,1)S(1)}, u32[]{:S(2)}, u32[]{:S(2)}) collective-permute-start(bf16[128,1024]{1,0:T(8,128)(2,1)S(1)} %get-tuple-element.24), channel_id=1, source_target_pairs={{0,384},{128,0},{256,128},{384,256},{1,385},{129,1},{257,129},{385... | collective-permute-start | bytes 786440 | tf_op jit(solution)/shard_map/ppermute | solution.py:220
  27.6 15.0 %collective-permute-start.3 = (bf16[128,1024]{1,0:T(8,128)(2,1)S(1)}, bf16[128,1024]{1,0:T(8,128)(2,1)S(1)}, u32[]{:S(2)}, u32[]{:S(2)}) collective-permute-start(bf16[128,1024]{1,0:T(8,128)(2,1)S(1)} %get-tuple-element.25), channel_id=1, source_target_pairs={{0,1},{1,0},{2,3},{3,2},{4,5},{5,4},{6,7},{7,6},{8,9},{9,8},{10,11... | collective-permute-start | bytes 786440 | tf_op jit(solution)/shard_map/ppermute | solution.py:223
  42.7 20.0 %copy-start.1 = (bf16[128,1024]{1,0:T(8,128)(2,1)}, bf16[128,1024]{1,0:T(8,128)(2,1)S(1)}, u32[]{:S(2)}) copy-start(bf16[128,1024]{1,0:T(8,128)(2,1)S(1)} %collective-permute-done.1) | copy-start | bytes 786436
  42.7 18.9 %all-to-all-start.1 = ((bf16[32,112,128]{2,1,0:T(8,128)(2,1)}), bf16[32,112,128]{2,1,0:T(8,128)(2,1)S(1)}, u32[]{:S(2)}, u32[]{:S(2)}) async-start(bf16[32,112,128]{2,1,0:T(8,128)(2,1)} %attend.1), calls=%async_computation.1 | async-start | bytes 1835008 | tf_op jit(solution)/shard_map/all_to_all | solution.py:294
  48.4 4.3 %collective-permute-start.4 = (bf16[128,1024]{1,0:T(8,128)(2,1)S(1)}, bf16[128,1024]{1,0:T(8,128)(2,1)S(1)}, u32[]{:S(2)}, u32[]{:S(2)}) collective-permute-start(bf16[128,1024]{1,0:T(8,128)(2,1)S(1)} %collective-permute-done.1), channel_id=1, source_target_pairs={{0,1},{1,0},{2,3},{3,2},{4,5},{5,4},{6,7},{7,6},{8,9},{9,8},{10,11... | collective-permute-start | bytes 786440 | tf_op jit(solution)/shard_map/ppermute | solution.py:223
  50.4 3.6 %collective-permute-start.5 = (bf16[128,1024]{1,0:T(8,128)(2,1)S(1)}, bf16[128,1024]{1,0:T(8,128)(2,1)S(1)}, u32[]{:S(2)}, u32[]{:S(2)}) collective-permute-start(bf16[128,1024]{1,0:T(8,128)(2,1)S(1)} %collective-permute-done.2), channel_id=1, source_target_pairs={{0,1},{1,0},{2,3},{3,2},{4,5},{5,4},{6,7},{7,6},{8,9},{9,8},{10,11... | collective-permute-start | bytes 786440 | tf_op jit(solution)/shard_map/ppermute | solution.py:223
  62.7 8.8 %collective-permute-start.6 = (bf16[2,128,128]{2,1,0:T(8,128)(2,1)S(1)}, bf16[2,128,128]{2,1,0:T(8,128)(2,1)S(1)}, u32[]{:S(2)}, u32[]{:S(2)}) collective-permute-start(bf16[2,128,128]{2,1,0:T(8,128)(2,1)S(1)} %get-tuple-element.33), channel_id=1, source_target_pairs={{0,64},{64,0},{1,65},{65,1},{2,66},{66,2},{3,67},{67,3},{4,68},{68... | collective-permute-start | bytes 196616 | tf_op jit(solution)/shard_map/ppermute | solution.py:316
  67.8 9.9 %collective-permute-start.7 = (bf16[128,1024]{1,0:T(8,128)(2,1)S(1)}, bf16[128,1024]{1,0:T(8,128)(2,1)}, u32[]{:S(2)}, u32[]{:S(2)}) collective-permute-start(bf16[128,1024]{1,0:T(8,128)(2,1)S(1)} %get-tuple-element.36), channel_id=1, source_target_pairs={{0,256},{128,384},{256,0},{384,128},{1,257},{129,385},{257,1},{385... | collective-permute-start | bytes 786440 | tf_op jit(solution)/shard_map/ppermute | solution.py:220
  72.3 10.9 %all-to-all-start.2 = ((bf16[8,128,128]{2,1,0:T(8,128)(2,1)}), bf16[8,128,128]{2,1,0:T(8,128)(2,1)S(1)}, u32[]{:S(2)}, u32[]{:S(2)}) async-start(bf16[8,128,128]{2,1,0:T(8,128)(2,1)} %spread.1), calls=%async_computation.2 | async-start | bytes 524288 | tf_op jit(solution)/shard_map/all_to_all | solution.py:327
  77.7 8.6 %collective-permute-start.8 = (bf16[128,1024]{1,0:T(8,128)(2,1)}, bf16[128,1024]{1,0:T(8,128)(2,1)S(1)}, u32[]{:S(2)}, u32[]{:S(2)}) collective-permute-start(bf16[128,1024]{1,0:T(8,128)(2,1)} %collective-permute-done.7), channel_id=1, source_target_pairs={{0,1},{1,0},{2,3},{3,2},{4,5},{5,4},{6,7},{7,6},{8,9},{9,8},{10,11... | collective-permute-start | bytes 786440 | tf_op jit(solution)/shard_map/ppermute | solution.py:223
  84.6 1.0 copy-start.2

commit v13 on v11

--- a/solution.py
+++ b/solution.py
@@ -117,7 +117,7 @@
     values[:, HD : 2 * HD] = one_hot(iota((KN, HD), 1) < 24)
     delta = picked(104, 0)
     kpos = jnp.broadcast_to(kpos_ref[...], (HD, KN)).T
-    key_columns = keys[...].astype(F32).T.astype(BF)
+    key_columns = keys[...].T
     count = 512
     kpos = jnp.concatenate([kpos] * (count // HD), axis=1)
     srcs = count // (OWN * HEADS)

time: 130 us -> 130 us (level)
  no operation moved by 1% of the time
where the time goes in v13:
time: 130 us; the launch traced here: 129 us
  starting transfers between devices  48.3 us (37%)
  blocking collectives  44.7 us (34%)
  waiting for transfers between devices  18.8 us (14%)
  Pallas kernels  11.8 us (9%)
  matrix products  2.13 us (2%)
  local copies, waits for them, and re-layouts  1.33 us (1%)
    all_to_all x1, blocking collectives, local(): lax.all_to_all(jnp.broadcast_to(part[None], (8, 64, HD)), ('zh', 'core'),...  28.5 us
    all_to_all x1, blocking collectives, local(): part = lax.all_to_all(part, ('zu', 'zd', 'y'), 0, 0, tiled=True)  16.1 us
    ppermute x3, starting transfers between devices, along_x(): lax.ppermute(columns[step], 'x', [(i, (i + step) % 4) for i in range(4)])  11.9 us
    all_to_all x1, starting transfers between devices, local(): arrived = lax.all_to_all(sent, peers, 0, 0, tiled=True)  8.69 us
    ppermute x4, starting transfers between devices, other_core(): return lax.ppermute(x, 'core', [(0, 1), (1, 0)])  8.45 us
    all_to_all x1, waiting for transfers between devices, local(): arrived = lax.all_to_all(sent, peers, 0, 0, tiled=True)  7.06 us
    pallas_call x1, Pallas kernels, local(): pl.pallas_call(attend_kernel, out_shape=jax.ShapeDtypeStruct((PEERS, BACK...  5.8 us
    all_to_all x1, starting transfers between devices, local(): home = lax.all_to_all(back, peers, 0, 0, tiled=True)  5.73 us
  transfers between devices with their start and end apart: 12, of which 4 were waited for; matrix products, arithmetic and copies ran while one was open for 2% of the time, Pallas kernels for 7%

profile of v13, /device:TPU:32, one launch (start us, length us, event | category | flops | bytes accessed | tf_op | source)
XLA Modules:
  0.0 129.2 jit_solution(15067765688122897625)
XLA Ops:
  0.6 0.8 pad_maximum_fusion
  1.4 5.2 %collective-permute-start = (bf16[2,64,256]{2,1,0:T(8,128)(2,1)S(1)}, bf16[2,64,256]{2,1,0:T(8,128)(2,1)S(1)}, u32[]{:S(2)}, u32[]{:S(2)}) collective-permute-start(bf16[2,64,256]{2,1,0:T(8,128)(2,1)S(1)} %pad_maximum_fusion), channel_id=1, source_target_pairs={{0,64},{64,0},{1,65},{65,1},{2,66},{66,2},{3,67},{67,3},{4,68},{68... | collective-permute-start | bytes 196616 | tf_op jit(solution)/shard_map/ppermute | solution.py:227
  6.6 2.6 %pack.1.in_ref = bf16[32,152,128]{2,1,0:T(8,128)(2,1)} custom-call(bf16[2,64,1024]{2,1,0:T(8,128)(2,1)} %q_ref.1, bf16[2,64,1024]{2,1,0:T(8,128)(2,1)} %g_ref.1, bf16[2,64,1024]{2,1,0:T(8,128)(2,1)} %o_ref.1, bf16[2,64,128]{2,1,0:T(8,128)(2,1)} %k_ref.1, bf16[2,64,128]{2,1,0:T(8,128)(2,1)} %v_ref.1), custom_call_target="tpu_custom_call" | custom-call | tf_op jit(solution)/shard_map/pack/pallas_call | solution.py:230
  9.2 1.0 pack_other.1
  10.3 8.7 %all-to-all-start = ((bf16[32,152,128]{2,1,0:T(8,128)(2,1)}), bf16[32,152,128]{2,1,0:T(8,128)(2,1)S(1)}, u32[]{:S(2)}, u32[]{:S(2)}) async-start(bf16[32,152,128]{2,1,0:T(8,128)(2,1)} %pack_other.1), calls=%async_computation | async-start | bytes 2490368 | tf_op jit(solution)/shard_map/all_to_all | solution.py:251
  19.2 0.1 fusion.28
  19.3 0.1 slice.18
  19.4 0.1 le.16
  19.5 0.1 concatenate.24
  19.6 0.1 slice.19
  19.7 0.1 concatenate.23
  19.7 0.1 concatenate.22
  19.8 0.2 convert_reduce_fusion
  20.0 0.1 select_reduce_fusion
  20.1 0.1 concatenate.25
  20.2 0.1 broadcast_in_dim.17
  20.2 0.1 convert_element_type.45.qlow_ref
  20.4 0.1 constant_dynamic-slice_fusion
  20.5 3.4 %collective-permute-start.1 = (bf16[128,1024]{1,0:T(8,128)(2,1)S(1)}, bf16[128,1024]{1,0:T(8,128)(2,1)S(1)}, u32[]{:S(2)}, u32[]{:S(2)}) collective-permute-start(bf16[128,1024]{1,0:T(8,128)(2,1)S(1)} %get-tuple-element.25), channel_id=1, source_target_pairs={{0,128},{128,256},{256,384},{384,0},{1,129},{129,257},{257,385},{3... | collective-permute-start | bytes 786440 | tf_op jit(solution)/shard_map/ppermute | solution.py:220
  23.9 3.7 %collective-permute-start.2 = (bf16[128,1024]{1,0:T(8,128)(2,1)S(1)}, bf16[128,1024]{1,0:T(8,128)(2,1)S(1)}, u32[]{:S(2)}, u32[]{:S(2)}) collective-permute-start(bf16[128,1024]{1,0:T(8,128)(2,1)S(1)} %get-tuple-element.26), channel_id=1, source_target_pairs={{0,384},{128,0},{256,128},{384,256},{1,385},{129,1},{257,129},{385... | collective-permute-start | bytes 786440 | tf_op jit(solution)/shard_map/ppermute | solution.py:220
  27.6 1.9 %collective-permute-start.3 = (bf16[128,1024]{1,0:T(8,128)(2,1)S(1)}, bf16[128,1024]{1,0:T(8,128)(2,1)S(1)}, u32[]{:S(2)}, u32[]{:S(2)}) collective-permute-start(bf16[128,1024]{1,0:T(8,128)(2,1)S(1)} %get-tuple-element.27), channel_id=1, source_target_pairs={{0,1},{1,0},{2,3},{3,2},{4,5},{5,4},{6,7},{7,6},{8,9},{9,8},{10,11... | collective-permute-start | bytes 786440 | tf_op jit(solution)/shard_map/ppermute | solution.py:223
  29.5 0.1 broadcast_in_dim.18
  29.6 0.1 convert_element_type.47.qpos_ref
  29.7 7.1 %all-to-all-done.in_ref = bf16[32,152,128]{2,1,0:T(8,128)(2,1)S(1)} async-done(((bf16[32,152,128]{2,1,0:T(8,128)(2,1)}), bf16[32,152,128]{2,1,0:T(8,128)(2,1)S(1)}, u32[]{:S(2)}, u32[]{:S(2)}) %all-to-all-start) | async-done | bytes 1245216 | tf_op jit(solution)/shard_map/all_to_all | solution.py:251
  36.8 5.8 %attend.1 = bf16[32,112,128]{2,1,0:T(8,128)(2,1)} custom-call(bf16[32,152,128]{2,1,0:T(8,128)(2,1)S(1)} %all-to-all-done.in_ref, f32[1,1280]{1,0:T(1,128)S(1)} %add_convert_fusion.kpos_ref, f32[1,1024]{1,0:T(1,128)S(1)} %convert_element_type.47.qpos_ref, f32[1,1024]{1,0:T(1,128)S(1)} %convert_element_type.45.qlow_ref), custom_call_target="tpu_custom_call" | custom-call | tf_op jit(solution)/shard_map/attend/pallas_call | solution.py:275
  42.6 5.7 %all-to-all-start.1 = ((bf16[32,112,128]{2,1,0:T(8,128)(2,1)}), bf16[32,112,128]{2,1,0:T(8,128)(2,1)S(1)}, u32[]{:S(2)}, u32[]{:S(2)}) async-start(bf16[32,112,128]{2,1,0:T(8,128)(2,1)} %attend.1), calls=%async_computation.1 | async-start | bytes 1835008 | tf_op jit(solution)/shard_map/all_to_all | solution.py:294
  48.3 1.9 %collective-permute-start.4 = (bf16[128,1024]{1,0:T(8,128)(2,1)S(1)}, bf16[128,1024]{1,0:T(8,128)(2,1)S(1)}, u32[]{:S(2)}, u32[]{:S(2)}) collective-permute-start(bf16[128,1024]{1,0:T(8,128)(2,1)S(1)} %collective-permute-done.1), channel_id=1, source_target_pairs={{0,1},{1,0},{2,3},{3,2},{4,5},{5,4},{6,7},{7,6},{8,9},{9,8},{10,11... | collective-permute-start | bytes 786440 | tf_op jit(solution)/shard_map/ppermute | solution.py:223
  50.2 2.4 %collective-permute-start.5 = (bf16[128,1024]{1,0:T(8,128)(2,1)S(1)}, bf16[128,1024]{1,0:T(8,128)(2,1)S(1)}, u32[]{:S(2)}, u32[]{:S(2)}) collective-permute-start(bf16[128,1024]{1,0:T(8,128)(2,1)S(1)} %collective-permute-done.2), channel_id=1, source_target_pairs={{0,1},{1,0},{2,3},{3,2},{4,5},{5,4},{6,7},{7,6},{8,9},{9,8},{10,11... | collective-permute-start | bytes 786440 | tf_op jit(solution)/shard_map/ppermute | solution.py:223
  52.7 4.9 %collective-permute-start.7 = (bf16[128,1024]{1,0:T(8,128)(2,1)S(1)}, bf16[128,1024]{1,0:T(8,128)(2,1)S(1)}, u32[]{:S(2)}, u32[]{:S(2)}) collective-permute-start(bf16[128,1024]{1,0:T(8,128)(2,1)S(1)} %get-tuple-element.36), channel_id=1, source_target_pairs={{0,256},{128,384},{256,0},{384,128},{1,257},{129,385},{257,1},{385... | collective-permute-start | bytes 786440 | tf_op jit(solution)/shard_map/ppermute | solution.py:220
  57.6 4.2 %all-to-all-done.1.in_ref = bf16[32,112,128]{2,1,0:T(8,128)(2,1)S(1)} async-done(((bf16[32,112,128]{2,1,0:T(8,128)(2,1)}), bf16[32,112,128]{2,1,0:T(8,128)(2,1)S(1)}, u32[]{:S(2)}, u32[]{:S(2)}) %all-to-all-start.1) | async-done | bytes 917536 | tf_op jit(solution)/shard_map/all_to_all | solution.py:294
  61.8 1.0 collect.1
  62.9 4.9 %collective-permute-start.6 = (bf16[2,128,128]{2,1,0:T(8,128)(2,1)S(1)}, bf16[2,128,128]{2,1,0:T(8,128)(2,1)S(1)}, u32[]{:S(2)}, u32[]{:S(2)}) collective-permute-start(bf16[2,128,128]{2,1,0:T(8,128)(2,1)S(1)} %get-tuple-element.35), channel_id=1, source_target_pairs={{0,64},{64,0},{1,65},{65,1},{2,66},{66,2},{3,67},{67,3},{4,68},{68... | collective-permute-start | bytes 196616 | tf_op jit(solution)/shard_map/ppermute | solution.py:316
  67.8 2.3 %collective-permute-done.6.far_ref = bf16[2,128,128]{2,1,0:T(8,128)(2,1)S(1)} collective-permute-done((bf16[2,128,128]{2,1,0:T(8,128)(2,1)S(1)}, bf16[2,128,128]{2,1,0:T(8,128)(2,1)S(1)}, u32[]{:S(2)}, u32[]{:S(2)}) %collective-permute-start.6) | collective-permute-done | bytes 65568 | tf_op jit(solution)/shard_map/ppermute | solution.py:316
  70.1 0.7 spread.1
  70.8 3.4 %all-to-all-start.2 = ((bf16[8,128,128]{2,1,0:T(8,128)(2,1)}), bf16[8,128,128]{2,1,0:T(8,128)(2,1)S(1)}, u32[]{:S(2)}, u32[]{:S(2)}) async-start(bf16[8,128,128]{2,1,0:T(8,128)(2,1)} %spread.1), calls=%async_computation.2 | async-start | bytes 524288 | tf_op jit(solution)/shard_map/all_to_all | solution.py:328
  74.3 2.2 %collective-permute-start.8 = (bf16[128,1024]{1,0:T(8,128)(2,1)S(1)}, bf16[128,1024]{1,0:T(8,128)(2,1)S(1)}, u32[]{:S(2)}, u32[]{:S(2)}) collective-permute-start(bf16[128,1024]{1,0:T(8,128)(2,1)S(1)} %collective-permute-done.7), channel_id=1, source_target_pairs={{0,1},{1,0},{2,3},{3,2},{4,5},{5,4},{6,7},{7,6},{8,9},{9,8},{10,11... | collective-permute-start | bytes 786440 | tf_op jit(solution)/shard_map/ppermute | solution.py:223
  76.6 5.1 %all-to-all-done.2 = bf16[8,128,128]{2,1,0:T(8,128)(2,1)S(1)} async-done(((bf16[8,128,128]{2,1,0:T(8,128)(2,1)}), bf16[8,128,128]{2,1,0:T(8,128)(2,1)S(1)}, u32[]{:S(2)}, u32[]{:S(2)}) %all-to-all-start.2) | async-done | bytes 262176 | tf_op jit(solution)/shard_map/all_to_all | solution.py:328
  81.7 0.2 fusion.8
  82.0 0.3 fusion.18
  82.2 0.3 fusion.12
  82.5 0.3 fusion.6
  82.7 0.3 fusion.14
  83.0 0.3 convolution_add_fusion.1
  83.3 0.3 fusion.10
  83.5 0.3 fusion.5
  83.9 16.1 %all_to_all.25 = bf16[16,64,128]{2,1,0:T(8,128)(2,1)S(1)} all-to-all(bf16[16,64,128]{2,1,0:T(8,128)(2,1)S(1)} %bitcast.42), channel_id=1, replica_groups=mesh['x'=4,'zu'=2,'zd'=2,'y'=4,'zh'=4,'core'=2] {'zu','zd','y'}, dimensions={0} | all-to-all | bytes 524288 | tf_op jit(solution)/shard_map/all_to_all | solution.py:339
  100.1 28.5 %all_to_all.26.in_ref = bf16[8,64,128]{2,1,0:T(8,128)(2,1)S(1)} all-to-all(bf16[8,64,128]{2,1,0:T(8,128)(2,1)S(1)} %broadcast_in_dim.30), channel_id=1, replica_groups=mesh['x'=4,'zu'=2,'zd'=2,'y'=4,'zh'=4,'core'=2] {'zh','core'}, dimensions={0} | all-to-all | bytes 262144 | tf_op jit(solution)/shard_map/all_to_all | solution.py:341
  128.6 0.6 finish.1
  (21 shorter events, 0.3 us)
Async XLA Ops:
  1.4 7.8 %collective-permute-start = (bf16[2,64,256]{2,1,0:T(8,128)(2,1)S(1)}, bf16[2,64,256]{2,1,0:T(8,128)(2,1)S(1)}, u32[]{:S(2)}, u32[]{:S(2)}) collective-permute-start(bf16[2,64,256]{2,1,0:T(8,128)(2,1)S(1)} %pad_maximum_fusion), channel_id=1, source_target_pairs={{0,64},{64,0},{1,65},{65,1},{2,66},{66,2},{3,67},{67,3},{4,68},{68... | collective-permute-start | bytes 196616 | tf_op jit(solution)/shard_map/ppermute | solution.py:227
  10.2 8.8 %copy-start.1 = (s32[2,4096]{1,0:T(2,128)S(1)}, s32[2,4096]{1,0:T(2,128)}, u32[]{:S(2)}) copy-start(s32[2,4096]{1,0:T(2,128)} %param.15) | copy-start | bytes 98308
  10.2 8.8 %copy-start.2 = (s32[2,4096]{1,0:T(2,128)S(1)}, s32[2,4096]{1,0:T(2,128)}, u32[]{:S(2)}) copy-start(s32[2,4096]{1,0:T(2,128)} %param.14) | copy-start | bytes 98308
  10.2 10.1 %copy-start = (bf16[2,64,4096]{2,1,0:T(8,128)(2,1)S(1)}, bf16[2,64,4096]{2,1,0:T(8,128)(2,1)}, u32[]{:S(2)}) copy-start(bf16[2,64,4096]{2,1,0:T(8,128)(2,1)} %param.8) | copy-start | bytes 3145732
  10.3 26.5 %all-to-all-start = ((bf16[32,152,128]{2,1,0:T(8,128)(2,1)}), bf16[32,152,128]{2,1,0:T(8,128)(2,1)S(1)}, u32[]{:S(2)}, u32[]{:S(2)}) async-start(bf16[32,152,128]{2,1,0:T(8,128)(2,1)} %pack_other.1), calls=%async_computation | async-start | bytes 2490368 | tf_op jit(solution)/shard_map/all_to_all | solution.py:251
  20.5 22.1 %collective-permute-start.1 = (bf16[128,1024]{1,0:T(8,128)(2,1)S(1)}, bf16[128,1024]{1,0:T(8,128)(2,1)S(1)}, u32[]{:S(2)}, u32[]{:S(2)}) collective-permute-start(bf16[128,1024]{1,0:T(8,128)(2,1)S(1)} %get-tuple-element.25), channel_id=1, source_target_pairs={{0,128},{128,256},{256,384},{384,0},{1,129},{129,257},{257,385},{3... | collective-permute-start | bytes 786440 | tf_op jit(solution)/shard_map/ppermute | solution.py:220
  23.9 18.7 %collective-permute-start.2 = (bf16[128,1024]{1,0:T(8,128)(2,1)S(1)}, bf16[128,1024]{1,0:T(8,128)(2,1)S(1)}, u32[]{:S(2)}, u32[]{:S(2)}) collective-permute-start(bf16[128,1024]{1,0:T(8,128)(2,1)S(1)} %get-tuple-element.26), channel_id=1, source_target_pairs={{0,384},{128,0},{256,128},{384,256},{1,385},{129,1},{257,129},{385... | collective-permute-start | bytes 786440 | tf_op jit(solution)/shard_map/ppermute | solution.py:220
  27.6 15.0 %collective-permute-start.3 = (bf16[128,1024]{1,0:T(8,128)(2,1)S(1)}, bf16[128,1024]{1,0:T(8,128)(2,1)S(1)}, u32[]{:S(2)}, u32[]{:S(2)}) collective-permute-start(bf16[128,1024]{1,0:T(8,128)(2,1)S(1)} %get-tuple-element.27), channel_id=1, source_target_pairs={{0,1},{1,0},{2,3},{3,2},{4,5},{5,4},{6,7},{7,6},{8,9},{9,8},{10,11... | collective-permute-start | bytes 786440 | tf_op jit(solution)/shard_map/ppermute | solution.py:223
  42.6 19.2 %all-to-all-start.1 = ((bf16[32,112,128]{2,1,0:T(8,128)(2,1)}), bf16[32,112,128]{2,1,0:T(8,128)(2,1)S(1)}, u32[]{:S(2)}, u32[]{:S(2)}) async-start(bf16[32,112,128]{2,1,0:T(8,128)(2,1)} %attend.1), calls=%async_computation.1 | async-start | bytes 1835008 | tf_op jit(solution)/shard_map/all_to_all | solution.py:294
  48.3 9.2 %collective-permute-start.4 = (bf16[128,1024]{1,0:T(8,128)(2,1)S(1)}, bf16[128,1024]{1,0:T(8,128)(2,1)S(1)}, u32[]{:S(2)}, u32[]{:S(2)}) collective-permute-start(bf16[128,1024]{1,0:T(8,128)(2,1)S(1)} %collective-permute-done.1), channel_id=1, source_target_pairs={{0,1},{1,0},{2,3},{3,2},{4,5},{5,4},{6,7},{7,6},{8,9},{9,8},{10,11... | collective-permute-start | bytes 786440 | tf_op jit(solution)/shard_map/ppermute | solution.py:223
  50.2 7.3 %collective-permute-start.5 = (bf16[128,1024]{1,0:T(8,128)(2,1)S(1)}, bf16[128,1024]{1,0:T(8,128)(2,1)S(1)}, u32[]{:S(2)}, u32[]{:S(2)}) collective-permute-start(bf16[128,1024]{1,0:T(8,128)(2,1)S(1)} %collective-permute-done.2), channel_id=1, source_target_pairs={{0,1},{1,0},{2,3},{3,2},{4,5},{5,4},{6,7},{7,6},{8,9},{9,8},{10,11... | collective-permute-start | bytes 786440 | tf_op jit(solution)/shard_map/ppermute | solution.py:223
  52.7 15.1 %collective-permute-start.7 = (bf16[128,1024]{1,0:T(8,128)(2,1)S(1)}, bf16[128,1024]{1,0:T(8,128)(2,1)S(1)}, u32[]{:S(2)}, u32[]{:S(2)}) collective-permute-start(bf16[128,1024]{1,0:T(8,128)(2,1)S(1)} %get-tuple-element.36), channel_id=1, source_target_pairs={{0,256},{128,384},{256,0},{384,128},{1,257},{129,385},{257,1},{385... | collective-permute-start | bytes 786440 | tf_op jit(solution)/shard_map/ppermute | solution.py:220
  62.9 7.2 %collective-permute-start.6 = (bf16[2,128,128]{2,1,0:T(8,128)(2,1)S(1)}, bf16[2,128,128]{2,1,0:T(8,128)(2,1)S(1)}, u32[]{:S(2)}, u32[]{:S(2)}) collective-permute-start(bf16[2,128,128]{2,1,0:T(8,128)(2,1)S(1)} %get-tuple-element.35), channel_id=1, source_target_pairs={{0,64},{64,0},{1,65},{65,1},{2,66},{66,2},{3,67},{67,3},{4,68},{68... | collective-permute-start | bytes 196616 | tf_op jit(solution)/shard_map/ppermute | solution.py:316
  70.8 10.9 %all-to-all-start.2 = ((bf16[8,128,128]{2,1,0:T(8,128)(2,1)}), bf16[8,128,128]{2,1,0:T(8,128)(2,1)S(1)}, u32[]{:S(2)}, u32[]{:S(2)}) async-start(bf16[8,128,128]{2,1,0:T(8,128)(2,1)} %spread.1), calls=%async_computation.2 | async-start | bytes 524288 | tf_op jit(solution)/shard_map/all_to_all | solution.py:328
  74.3 8.9 %collective-permute-start.8 = (bf16[128,1024]{1,0:T(8,128)(2,1)S(1)}, bf16[128,1024]{1,0:T(8,128)(2,1)S(1)}, u32[]{:S(2)}, u32[]{:S(2)}) collective-permute-start(bf16[128,1024]{1,0:T(8,128)(2,1)S(1)} %collective-permute-done.7), channel_id=1, source_target_pairs={{0,1},{1,0},{2,3},{3,2},{4,5},{5,4},{6,7},{7,6},{8,9},{9,8},{10,11... | collective-permute-start | bytes 786440 | tf_op jit(solution)/shard_map/ppermute | solution.py:223
